TPU v7x, 32 devices: a whole 2x2x4 slice. The times are simulated.
32 devices in a mesh: gx: 8 (over z, x), gy: 4 (over y, core).
Axes of the slice: x: 2, y: 2, z: 4, core: 2. Of those that a mesh axis runs over, the one named last changes fastest.
Arguments:
- voxels: bfloat16 [64, 32, 8, 96], P('gx', 'gy'), may hold values from -6 to 6
- occupancy: int32 [64, 32, 8], P('gx', 'gy'), may hold values 0 or 1
- conv_weight: bfloat16 [27, 96, 96], replicated, may hold values from -0.125 to 0.125
- conv_bias: float32 [96], replicated, may hold values from -3 to 3
- down_weight: bfloat16 [27, 96, 96], replicated, may hold values from -0.125 to 0.125
- down_cotangent: bfloat16 [32, 16, 4, 96], P('gx', 'gy'), may hold values from -6 to 6
Outputs:
- down: bfloat16 [32, 16, 4, 96], P('gx', 'gy')
- grad_voxels: bfloat16 [64, 32, 8, 96], P('gx', 'gy')
- grad_conv: float32 [27, 96, 96], replicated
- grad_bias: float32 [96], replicated
- grad_down: float32 [27, 96, 96], replicated
Inputs may be any that keep to these rules, and one draw needn't show every extreme that they name: `occupancy`: 0 or 1 for every voxel.
All inputs are finite; a program needn't handle non-finite values. No bound on the sum of `occupancy` on one device may be relied on, other than what follows from the above.
Results may differ from a plain program's by a relative error of at most 0.006.
Values may be sent and summed in bfloat16 or wider, within the bound.
No kernel may reach another device: no remote copies, remote signals or barrier semaphores. Data moves between devices by JAX's collectives and lax.ppermute only.
A program may use at most 64 MiB of HBM per device.

v0:
```python
import math

import jax
import jax.numpy as jnp
from jax import lax
from jax.sharding import PartitionSpec as P

TAP_OFFSETS = [
    (step_x, step_y, step_z)
    for step_x in (-1, 0, 1)
    for step_y in (-1, 0, 1)
    for step_z in (-1, 0, 1)
]
PARITY_TERMS = {0: [(0, 0)], 1: [(1, 0), (-1, 1)]}


def with_halo(value, sides, width):
    for axis, dim in sides:
        peers, length = (lax.axis_size(axis), value.shape[dim])
        up = [(i, (i + 1) % peers) for i in range(peers - 1)]
        down = [(j, i) for i, j in up]
        last = lax.slice_in_dim(value, length - width, length, axis=dim)
        leading = lax.slice_in_dim(value, 0, width, axis=dim)
        before = lax.ppermute(last, axis, up)
        after = lax.ppermute(leading, axis, down)
        value = jnp.concatenate([before, value, after], axis=dim)
    return value


def from_behind(block, axis, distance):
    devices = range(lax.axis_size(axis))
    route = [(i - distance, i) for i in devices if i - distance in devices]
    return lax.ppermute(block, axis, route)


def conv_same(padded, weight, size_x, size_y, size_z):
    channels = padded.shape[-1]
    running = jnp.zeros((size_x * size_y * size_z, weight.shape[2]), jnp.float32)
    for tap_index, (step_x, step_y, step_z) in enumerate(TAP_OFFSETS):
        window = padded[
            1 + step_x : 1 + step_x + size_x,
            1 + step_y : 1 + step_y + size_y,
            1 + step_z : 1 + step_z + size_z,
        ]
        running = running + jnp.dot(
            window.reshape(-1, channels), weight[tap_index], preferred_element_type=jnp.float32
        )
    return running.reshape(size_x, size_y, size_z, -1)


def weight_taps(padded, grad_out, size_x, size_y, size_z):
    channels = padded.shape[-1]
    flat_grad = grad_out.reshape(-1, grad_out.shape[-1])
    pieces = []
    for step_x, step_y, step_z in TAP_OFFSETS:
        window = padded[
            1 + step_x : 1 + step_x + size_x,
            1 + step_y : 1 + step_y + size_y,
            1 + step_z : 1 + step_z + size_z,
        ]
        pieces.append(
            jnp.dot(window.reshape(-1, channels).T, flat_grad, preferred_element_type=jnp.float32)
        )
    return jnp.stack(pieces)


def stride_window(padded, step_x, step_y, step_z, size_x, size_y, size_z):
    channels = padded.shape[-1]
    return lax.slice(
        padded,
        (1 + step_x, 1 + step_y, 1 + step_z, 0),
        (
            2 + step_x + 2 * (size_x - 1),
            2 + step_y + 2 * (size_y - 1),
            2 + step_z + 2 * (size_z - 1),
            channels,
        ),
        (2, 2, 2, 1),
    )


def stride_conv(padded, weight, size_x, size_y, size_z):
    channels = padded.shape[-1]
    running = jnp.zeros((size_x * size_y * size_z, weight.shape[2]), jnp.float32)
    for tap_index, (step_x, step_y, step_z) in enumerate(TAP_OFFSETS):
        window = stride_window(padded, step_x, step_y, step_z, size_x, size_y, size_z)
        running = running + jnp.dot(
            window.reshape(-1, channels), weight[tap_index], preferred_element_type=jnp.float32
        )
    return running.reshape(size_x, size_y, size_z, -1)


def stride_weight(padded, grad_out, size_x, size_y, size_z):
    channels = padded.shape[-1]
    flat_grad = grad_out.reshape(-1, grad_out.shape[-1])
    pieces = []
    for step_x, step_y, step_z in TAP_OFFSETS:
        window = stride_window(padded, step_x, step_y, step_z, size_x, size_y, size_z)
        pieces.append(
            jnp.dot(window.reshape(-1, channels).T, flat_grad, preferred_element_type=jnp.float32)
        )
    return jnp.stack(pieces)


def fine_from_coarse(padded, weight, size_x, size_y, size_z):
    channels = padded.shape[-1]
    flipped = jnp.swapaxes(weight, 1, 2)
    blocks = []
    for parity_x in (0, 1):
        for parity_y in (0, 1):
            for parity_z in (0, 1):
                running = jnp.zeros((size_x * size_y * size_z, weight.shape[1]), jnp.float32)
                for step_x, shift_x in PARITY_TERMS[parity_x]:
                    for step_y, shift_y in PARITY_TERMS[parity_y]:
                        for step_z, shift_z in PARITY_TERMS[parity_z]:
                            tap_index = (step_x + 1) * 9 + (step_y + 1) * 3 + (step_z + 1)
                            window = padded[
                                shift_x : shift_x + size_x,
                                shift_y : shift_y + size_y,
                                shift_z : shift_z + size_z,
                            ]
                            running = running + jnp.dot(
                                window.reshape(-1, channels),
                                flipped[tap_index],
                                preferred_element_type=jnp.float32,
                            )
                blocks.append(running.reshape(size_x, size_y, size_z, -1))
    stacked = jnp.stack(blocks).reshape(2, 2, 2, size_x, size_y, size_z, -1)
    return jnp.transpose(stacked, (3, 0, 4, 1, 5, 2, 6)).reshape(
        2 * size_x, 2 * size_y, 2 * size_z, -1
    )


def on_device(voxels, occupancy, conv_weight, conv_bias, down_weight, down_cotangent):
    tile_x, tile_y, size_z, channels = voxels.shape
    half_x, half_y, half_z = (tile_x // 2, tile_y // 2, size_z // 2)
    occupied = occupancy.astype(jnp.float32)[..., None]
    masked = (voxels.astype(jnp.float32) * occupied).astype(jnp.bfloat16)
    padded_in = with_halo(masked, (("gx", 0), ("gy", 1)), 1)
    padded_in = jnp.pad(padded_in, ((0, 0), (0, 0), (1, 1), (0, 0)))
    preact = conv_same(padded_in, conv_weight, tile_x, tile_y, size_z) + conv_bias
    summed = (masked.astype(jnp.float32) + jax.nn.silu(preact) * occupied).astype(jnp.bfloat16)
    coarse_live = (
        occupancy.reshape(half_x, 2, half_y, 2, half_z, 2)
        .max(axis=(1, 3, 5))
        .astype(jnp.float32)[..., None]
    )
    edge_row = from_behind(summed[tile_x - 1 :], "gx", 1)
    with_row = jnp.concatenate([edge_row, summed], 0)
    edge_col = from_behind(with_row[:, tile_y - 1 :], "gy", 1)
    stride_in = jnp.pad(jnp.concatenate([edge_col, with_row], 1), ((0, 0), (0, 0), (1, 0), (0, 0)))
    down = (stride_conv(stride_in, down_weight, half_x, half_y, half_z) * coarse_live).astype(
        jnp.bfloat16
    )
    grad_coarse = (down_cotangent.astype(jnp.float32) * coarse_live).astype(jnp.bfloat16)
    grad_stride = stride_weight(stride_in, grad_coarse, half_x, half_y, half_z)
    coarse_pad = jnp.pad(grad_coarse, ((1, 1), (1, 1), (0, 1), (0, 0)))
    spread = fine_from_coarse(coarse_pad, down_weight, half_x + 1, half_y + 1, half_z)[1:, 1:]
    arrived = from_behind(spread[:1], "gx", -1)
    spread = jnp.concatenate([spread[1:tile_x], spread[tile_x:] + arrived], 0)
    arrived = from_behind(spread[:, :1], "gy", -1)
    grad_sum = jnp.concatenate([spread[:, 1:tile_y], spread[:, tile_y:] + arrived], 1)
    sigmoid_val = jax.nn.sigmoid(preact)
    grad_pre = (grad_sum * occupied * sigmoid_val * (1.0 + preact * (1.0 - sigmoid_val))).astype(
        jnp.bfloat16
    )
    grad_bias = jnp.sum(grad_pre.astype(jnp.float32), axis=(0, 1, 2))
    grad_conv = weight_taps(padded_in, grad_pre, tile_x, tile_y, size_z)
    grad_padded = with_halo(grad_pre, (("gx", 0), ("gy", 1)), 1)
    grad_padded = jnp.pad(grad_padded, ((0, 0), (0, 0), (1, 1), (0, 0)))
    back_weight = jnp.swapaxes(conv_weight[::-1], 1, 2)
    grad_in = grad_sum + conv_same(grad_padded, back_weight, tile_x, tile_y, size_z)
    grad_voxels = (grad_in * occupied).astype(jnp.bfloat16)
    grad_conv, grad_bias, grad_stride = lax.psum((grad_conv, grad_bias, grad_stride), ("gx", "gy"))
    all_cells = tile_x * lax.axis_size("gx") * tile_y * lax.axis_size("gy") * size_z
    factor = 1.0 / math.sqrt(all_cells)
    return (down, grad_voxels, grad_conv * factor, grad_bias * factor, grad_stride * factor)


def solution(mesh):
    placed = (
        P("gx", "gy", None, None),
        P("gx", "gy", None),
        P(),
        P(),
        P(),
        P("gx", "gy", None, None),
    )
    return jax.shard_map(
        on_device,
        mesh=mesh,
        in_specs=placed,
        out_specs=(P("gx", "gy", None, None), P("gx", "gy", None, None), P(), P(), P()),
        check_vma=False,
    )
```

profile of v0, /device:TPU:0, one launch (start us, length us, event | category | flops | bytes accessed | tf_op | source)
XLA Modules:
  0.0 425.7 jit_solution(18280210113143955065)
XLA Ops:
  8.0 1.0 multiply_convert_fusion.2
  9.1 1.3 collective-permute-start.1
  10.4 5.5 %collective-permute-start = (bf16[1,8,8,96]{3,2,1,0:T(8,128)(2,1)S(1)}, bf16[1,8,8,96]{3,2,1,0:T(8,128)(2,1)S(1)}, u32[]{:S(2)}, u32[]{:S(2)}) collective-permute-start(bf16[1,8,8,96]{3,2,1,0:T(8,128)(2,1)S(1)} %get-tuple-element.89), channel_id=1, source_target_pairs={{0,4},{4,8},{8,12},{12,16},{16,20},{20,24},{24,28},{1,5},{5,9},{9,... | collective-permute-start | bytes 36872 | tf_op jit(solution)/shard_map/ppermute | solution.py:24
  16.7 1.4 copy.107
  26.2 1.3 collective-permute-start.6
  27.7 1.3 collective-permute-start.3
  29.0 3.0 collective-permute-start.2
  34.3 1.3 collective-permute-start.7
  42.9 5.4 %collective-permute-start.4 = (bf16[1,8,8,96]{3,2,1,0:T(8,128)(2,1)S(1)}, bf16[1,8,8,96]{3,2,1,0:T(8,128)(2,1)S(1)}, u32[]{:S(2)}, u32[]{:S(2)}) collective-permute-start(bf16[1,8,8,96]{3,2,1,0:T(8,128)(2,1)S(1)} %slice.989), channel_id=1, source_target_pairs={{0,4},{4,8},{8,12},{12,16},{16,20},{20,24},{24,28},{1,5},{5,9},{9,... | collective-permute-start | bytes 36872 | tf_op jit(solution)/shard_map/ppermute | solution.py:33
  48.3 1.3 collective-permute-start.9
  49.6 5.5 %collective-permute-start.8 = (bf16[1,8,8,96]{3,2,1,0:T(8,128)(2,1)S(1)}, bf16[1,8,8,96]{3,2,1,0:T(8,128)(2,1)S(1)}, u32[]{:S(2)}, u32[]{:S(2)}) collective-permute-start(bf16[1,8,8,96]{3,2,1,0:T(8,128)(2,1)S(1)} %get-tuple-element.85), channel_id=1, source_target_pairs={{0,4},{4,8},{8,12},{12,16},{16,20},{20,24},{24,28},{1,5},{5,9},{9,... | collective-permute-start | bytes 36872 | tf_op jit(solution)/shard_map/ppermute | solution.py:24
  77.4 44.4 %psum.22 = f32[96]{0:T(128)S(1)} all-reduce(f32[96]{0:T(128)S(1)} %get-tuple-element.22), channel_id=1, replica_groups=mesh['gx'=8,'gy'=4] {'gx','gy'}, use_global_device_ids=true, to_apply=%region_3.4 | all-reduce | flops 96 | bytes 768 | tf_op jit(solution)/shard_map/psum | solution.py:174
  122.5 1.3 collective-permute-start.5
  124.5 1.3 collective-permute-start.11
  125.8 6.1 %collective-permute-start.10 = (bf16[10,1,8,96]{3,2,1,0:T(8,128)(2,1)}, bf16[10,1,8,96]{3,2,1,0:T(8,128)(2,1)}, u32[]{:S(2)}, u32[]{:S(2)}) collective-permute-start(bf16[10,1,8,96]{3,2,1,0:T(8,128)(2,1)} %get-tuple-element.77), channel_id=1, source_target_pairs={{0,1},{1,2},{2,3},{4,5},{5,6},{6,7},{8,9},{9,10},{10,11},{12,13},{... | collective-permute-start | bytes 46088 | tf_op jit(solution)/shard_map/ppermute | solution.py:24
  132.1 4.7 %slice.811 = bf16[4,4,4,96]{3,2,1,0:T(4,128)(2,1)} slice(bf16[9,9,9,96]{3,2,1,0:T(8,128)(2,1)S(1)} %fusion.69), slice={[0:7:2], [0:7:2], [0:7:2], [0:96:1]} | slice | bytes 24576 | tf_op jit(solution)/shard_map/slice | solution.py:69
  136.7 4.6 %slice.813 = bf16[4,4,4,96]{3,2,1,0:T(4,128)(2,1)} slice(bf16[9,9,9,96]{3,2,1,0:T(8,128)(2,1)S(1)} %fusion.69), slice={[0:7:2], [0:7:2], [1:8:2], [0:96:1]} | slice | bytes 24576 | tf_op jit(solution)/shard_map/slice | solution.py:69
  141.4 4.6 %slice.815 = bf16[4,4,4,96]{3,2,1,0:T(4,128)(2,1)} slice(bf16[9,9,9,96]{3,2,1,0:T(8,128)(2,1)S(1)} %fusion.69), slice={[0:7:2], [0:7:2], [2:9:2], [0:96:1]} | slice | bytes 24576 | tf_op jit(solution)/shard_map/slice | solution.py:69
  146.0 4.7 %slice.817 = bf16[4,4,4,96]{3,2,1,0:T(4,128)(2,1)} slice(bf16[9,9,9,96]{3,2,1,0:T(8,128)(2,1)S(1)} %fusion.69), slice={[0:7:2], [1:8:2], [0:7:2], [0:96:1]} | slice | bytes 24576 | tf_op jit(solution)/shard_map/slice | solution.py:69
  150.8 4.8 %slice.819 = bf16[4,4,4,96]{3,2,1,0:T(4,128)(2,1)} slice(bf16[9,9,9,96]{3,2,1,0:T(8,128)(2,1)S(1)} %fusion.69), slice={[0:7:2], [1:8:2], [1:8:2], [0:96:1]} | slice | bytes 24576 | tf_op jit(solution)/shard_map/slice | solution.py:69
  155.5 4.8 %slice.821 = bf16[4,4,4,96]{3,2,1,0:T(4,128)(2,1)} slice(bf16[9,9,9,96]{3,2,1,0:T(8,128)(2,1)S(1)} %fusion.69), slice={[0:7:2], [1:8:2], [2:9:2], [0:96:1]} | slice | bytes 24576 | tf_op jit(solution)/shard_map/slice | solution.py:69
  160.3 4.7 %slice.823 = bf16[4,4,4,96]{3,2,1,0:T(4,128)(2,1)} slice(bf16[9,9,9,96]{3,2,1,0:T(8,128)(2,1)S(1)} %fusion.69), slice={[0:7:2], [2:9:2], [0:7:2], [0:96:1]} | slice | bytes 24576 | tf_op jit(solution)/shard_map/slice | solution.py:69
  165.0 4.8 %slice.825 = bf16[4,4,4,96]{3,2,1,0:T(4,128)(2,1)} slice(bf16[9,9,9,96]{3,2,1,0:T(8,128)(2,1)S(1)} %fusion.69), slice={[0:7:2], [2:9:2], [1:8:2], [0:96:1]} | slice | bytes 24576 | tf_op jit(solution)/shard_map/slice | solution.py:69
  169.8 4.8 %slice.827 = bf16[4,4,4,96]{3,2,1,0:T(4,128)(2,1)} slice(bf16[9,9,9,96]{3,2,1,0:T(8,128)(2,1)S(1)} %fusion.69), slice={[0:7:2], [2:9:2], [2:9:2], [0:96:1]} | slice | bytes 24576 | tf_op jit(solution)/shard_map/slice | solution.py:69
  174.6 4.7 %slice.829 = bf16[4,4,4,96]{3,2,1,0:T(4,128)(2,1)} slice(bf16[9,9,9,96]{3,2,1,0:T(8,128)(2,1)S(1)} %fusion.69), slice={[1:8:2], [0:7:2], [0:7:2], [0:96:1]} | slice | bytes 24576 | tf_op jit(solution)/shard_map/slice | solution.py:69
  179.3 4.8 %slice.831 = bf16[4,4,4,96]{3,2,1,0:T(4,128)(2,1)} slice(bf16[9,9,9,96]{3,2,1,0:T(8,128)(2,1)S(1)} %fusion.69), slice={[1:8:2], [0:7:2], [1:8:2], [0:96:1]} | slice | bytes 24576 | tf_op jit(solution)/shard_map/slice | solution.py:69
  184.0 4.8 %slice.833 = bf16[4,4,4,96]{3,2,1,0:T(4,128)(2,1)} slice(bf16[9,9,9,96]{3,2,1,0:T(8,128)(2,1)S(1)} %fusion.69), slice={[1:8:2], [0:7:2], [2:9:2], [0:96:1]} | slice | bytes 24576 | tf_op jit(solution)/shard_map/slice | solution.py:69
  188.8 4.8 %slice.835 = bf16[4,4,4,96]{3,2,1,0:T(4,128)(2,1)} slice(bf16[9,9,9,96]{3,2,1,0:T(8,128)(2,1)S(1)} %fusion.69), slice={[1:8:2], [1:8:2], [0:7:2], [0:96:1]} | slice | bytes 24576 | tf_op jit(solution)/shard_map/slice | solution.py:69
  193.6 4.7 %slice.837 = bf16[4,4,4,96]{3,2,1,0:T(4,128)(2,1)} slice(bf16[9,9,9,96]{3,2,1,0:T(8,128)(2,1)S(1)} %fusion.69), slice={[1:8:2], [1:8:2], [1:8:2], [0:96:1]} | slice | bytes 24576 | tf_op jit(solution)/shard_map/slice | solution.py:69
  198.3 4.7 %slice.839 = bf16[4,4,4,96]{3,2,1,0:T(4,128)(2,1)} slice(bf16[9,9,9,96]{3,2,1,0:T(8,128)(2,1)S(1)} %fusion.69), slice={[1:8:2], [1:8:2], [2:9:2], [0:96:1]} | slice | bytes 24576 | tf_op jit(solution)/shard_map/slice | solution.py:69
  203.0 4.8 %slice.841 = bf16[4,4,4,96]{3,2,1,0:T(4,128)(2,1)} slice(bf16[9,9,9,96]{3,2,1,0:T(8,128)(2,1)S(1)} %fusion.69), slice={[1:8:2], [2:9:2], [0:7:2], [0:96:1]} | slice | bytes 24576 | tf_op jit(solution)/shard_map/slice | solution.py:69
  207.8 4.7 %slice.843 = bf16[4,4,4,96]{3,2,1,0:T(4,128)(2,1)} slice(bf16[9,9,9,96]{3,2,1,0:T(8,128)(2,1)S(1)} %fusion.69), slice={[1:8:2], [2:9:2], [1:8:2], [0:96:1]} | slice | bytes 24576 | tf_op jit(solution)/shard_map/slice | solution.py:69
  212.6 4.7 %slice.845 = bf16[4,4,4,96]{3,2,1,0:T(4,128)(2,1)} slice(bf16[9,9,9,96]{3,2,1,0:T(8,128)(2,1)S(1)} %fusion.69), slice={[1:8:2], [2:9:2], [2:9:2], [0:96:1]} | slice | bytes 24576 | tf_op jit(solution)/shard_map/slice | solution.py:69
  217.3 4.8 %slice.847 = bf16[4,4,4,96]{3,2,1,0:T(4,128)(2,1)} slice(bf16[9,9,9,96]{3,2,1,0:T(8,128)(2,1)S(1)} %fusion.69), slice={[2:9:2], [0:7:2], [0:7:2], [0:96:1]} | slice | bytes 24576 | tf_op jit(solution)/shard_map/slice | solution.py:69
  222.0 4.7 %slice.849 = bf16[4,4,4,96]{3,2,1,0:T(4,128)(2,1)} slice(bf16[9,9,9,96]{3,2,1,0:T(8,128)(2,1)S(1)} %fusion.69), slice={[2:9:2], [0:7:2], [1:8:2], [0:96:1]} | slice | bytes 24576 | tf_op jit(solution)/shard_map/slice | solution.py:69
  226.8 4.7 %slice.851 = bf16[4,4,4,96]{3,2,1,0:T(4,128)(2,1)} slice(bf16[9,9,9,96]{3,2,1,0:T(8,128)(2,1)S(1)} %fusion.69), slice={[2:9:2], [0:7:2], [2:9:2], [0:96:1]} | slice | bytes 24576 | tf_op jit(solution)/shard_map/slice | solution.py:69
  231.5 4.7 %slice.853 = bf16[4,4,4,96]{3,2,1,0:T(4,128)(2,1)} slice(bf16[9,9,9,96]{3,2,1,0:T(8,128)(2,1)S(1)} %fusion.69), slice={[2:9:2], [1:8:2], [0:7:2], [0:96:1]} | slice | bytes 24576 | tf_op jit(solution)/shard_map/slice | solution.py:69
  236.3 4.7 %slice.855 = bf16[4,4,4,96]{3,2,1,0:T(4,128)(2,1)} slice(bf16[9,9,9,96]{3,2,1,0:T(8,128)(2,1)S(1)} %fusion.69), slice={[2:9:2], [1:8:2], [1:8:2], [0:96:1]} | slice | bytes 24576 | tf_op jit(solution)/shard_map/slice | solution.py:69
  241.0 4.7 %slice.857 = bf16[4,4,4,96]{3,2,1,0:T(4,128)(2,1)} slice(bf16[9,9,9,96]{3,2,1,0:T(8,128)(2,1)S(1)} %fusion.69), slice={[2:9:2], [1:8:2], [2:9:2], [0:96:1]} | slice | bytes 24576 | tf_op jit(solution)/shard_map/slice | solution.py:69
  245.7 4.8 %slice.859 = bf16[4,4,4,96]{3,2,1,0:T(4,128)(2,1)} slice(bf16[9,9,9,96]{3,2,1,0:T(8,128)(2,1)S(1)} %fusion.69), slice={[2:9:2], [2:9:2], [0:7:2], [0:96:1]} | slice | bytes 24576 | tf_op jit(solution)/shard_map/slice | solution.py:69
  250.5 4.8 %slice.861 = bf16[4,4,4,96]{3,2,1,0:T(4,128)(2,1)} slice(bf16[9,9,9,96]{3,2,1,0:T(8,128)(2,1)S(1)} %fusion.69), slice={[2:9:2], [2:9:2], [1:8:2], [0:96:1]} | slice | bytes 24576 | tf_op jit(solution)/shard_map/slice | solution.py:69
  255.2 4.8 %slice.863 = bf16[4,4,4,96]{3,2,1,0:T(4,128)(2,1)} slice(bf16[9,9,9,96]{3,2,1,0:T(8,128)(2,1)S(1)} %fusion.69), slice={[2:9:2], [2:9:2], [2:9:2], [0:96:1]} | slice | bytes 24576 | tf_op jit(solution)/shard_map/slice | solution.py:69
  260.0 1.0 fusion.40
  267.6 1.0 fusion.35
  279.7 1.0 select_maximum_fusion
  288.0 127.1 %all-reduce.7.cloned.1.call-done = (f32[27,96,96]{2,1,0:T(8,128)}, f32[27,96,96]{2,1,0:T(8,128)}) async-done(((f32[27,96,96]{2,1,0:T(8,128)}, f32[27,96,96]{2,1,0:T(8,128)}), (f32[27,96,96]{2,1,0:T(8,128)}, f32[27,96,96]{2,1,0:T(8,128)})) %all-reduce.7.cloned.1.call-update) | async-done | bytes 1990672 | tf_op jit(solution)/shard_map/psum | solution.py:174
  415.1 2.6 broadcast_multiply_fusion.1
  417.7 1.2 broadcast_multiply_fusion
  (339 shorter events, 67.2 us)
Async XLA Ops:
  7.2 11.5 %copy-start.41 = (bf16[4,4,4,96]{3,2,1,0:T(4,128)(2,1)S(1)}, bf16[4,4,4,96]{3,2,1,0:T(4,128)(2,1)}, u32[]{:S(2)}) copy-start(bf16[4,4,4,96]{3,2,1,0:T(4,128)(2,1)} %param.11) | copy-start | bytes 36868
  7.2 407.9 %all-reduce.7.cloned.1.call-start = ((), (), s32[]{:S(2)}) async-start(), calls=%async_computation | async-start | bytes 5308416 | tf_op jit(solution)/shard_map/psum | solution.py:174
  8.0 19.6 %copy-start.4 = (f32[8,8,8]{2,1,0:T(8,128)}, f32[8,8,8]{2,1,0:T(8,128)S(1)}, u32[]{:S(2)}) copy-start(f32[8,8,8]{2,1,0:T(8,128)S(1)} %convert_element_type.53) | copy-start | bytes 6148
  9.1 18.6 %collective-permute-start.1 = (bf16[1,8,8,96]{3,2,1,0:T(8,128)(2,1)S(1)}, bf16[1,8,8,96]{3,2,1,0:T(8,128)(2,1)S(1)}, u32[]{:S(2)}, u32[]{:S(2)}) collective-permute-start(bf16[1,8,8,96]{3,2,1,0:T(8,128)(2,1)S(1)} %get-tuple-element.90), channel_id=1, source_target_pairs={{4,0},{8,4},{12,8},{16,12},{20,16},{24,20},{28,24},{5,1},{9,5},{13... | collective-permute-start | bytes 36872 | tf_op jit(solution)/shard_map/ppermute | solution.py:25
  10.4 17.3 %collective-permute-start = (bf16[1,8,8,96]{3,2,1,0:T(8,128)(2,1)S(1)}, bf16[1,8,8,96]{3,2,1,0:T(8,128)(2,1)S(1)}, u32[]{:S(2)}, u32[]{:S(2)}) collective-permute-start(bf16[1,8,8,96]{3,2,1,0:T(8,128)(2,1)S(1)} %get-tuple-element.89), channel_id=1, source_target_pairs={{0,4},{4,8},{8,12},{12,16},{16,20},{20,24},{24,28},{1,5},{5,9},{9,... | collective-permute-start | bytes 36872 | tf_op jit(solution)/shard_map/ppermute | solution.py:24
  18.6 7.5 %copy-start.16 = (f32[4,4,4]{1,2,0:T(4,128)}, f32[4,4,4]{1,2,0:T(4,128)S(1)}, u32[]{:S(2)}) copy-start(f32[4,4,4]{1,2,0:T(4,128)S(1)} %copy.104) | copy-start | bytes 772
  25.1 2.4 copy-start
  26.2 8.1 %collective-permute-start.6 = (f32[1,9,8,96]{3,2,1,0:T(8,128)S(1)}, f32[1,9,8,96]{3,2,1,0:T(8,128)S(1)}, u32[]{:S(2)}, u32[]{:S(2)}) collective-permute-start(f32[1,9,8,96]{3,2,1,0:T(8,128)S(1)} %slice.1019), channel_id=1, source_target_pairs={{4,0},{8,4},{12,8},{16,12},{20,16},{24,20},{28,24},{5,1},{9,5},{13... | collective-permute-start | bytes 82952 | tf_op jit(solution)/shard_map/ppermute | solution.py:33
  27.7 7.9 %copy-start.7 = (bf16[1,8,8,96]{3,2,1,0:T(8,128)(2,1)}, bf16[1,8,8,96]{3,2,1,0:T(8,128)(2,1)S(1)}, u32[]{:S(2)}) copy-start(bf16[1,8,8,96]{3,2,1,0:T(8,128)(2,1)S(1)} %collective-permute-done.1) | copy-start | bytes 36868
  27.7 7.9 %copy-start.9 = (bf16[1,8,8,96]{3,2,1,0:T(8,128)(2,1)}, bf16[1,8,8,96]{3,2,1,0:T(8,128)(2,1)S(1)}, u32[]{:S(2)}) copy-start(bf16[1,8,8,96]{3,2,1,0:T(8,128)(2,1)S(1)} %collective-permute-done) | copy-start | bytes 36868
  27.7 4.4 %collective-permute-start.3 = (bf16[10,1,8,96]{3,2,1,0:T(8,128)(2,1)S(1)}, bf16[10,1,8,96]{3,2,1,0:T(8,128)(2,1)S(1)}, u32[]{:S(2)}, u32[]{:S(2)}) collective-permute-start(bf16[10,1,8,96]{3,2,1,0:T(8,128)(2,1)S(1)} %get-tuple-element.82), channel_id=1, source_target_pairs={{1,0},{2,1},{3,2},{5,4},{6,5},{7,6},{9,8},{10,9},{11,10},{13,12},{... | collective-permute-start | bytes 46088 | tf_op jit(solution)/shard_map/ppermute | solution.py:25
  29.0 3.9 collective-permute-start.2
  34.3 7.2 %collective-permute-start.7 = (f32[8,1,8,96]{3,2,1,0:T(8,128)S(1)}, f32[8,1,8,96]{3,2,1,0:T(8,128)S(1)}, u32[]{:S(2)}, u32[]{:S(2)}) collective-permute-start(f32[8,1,8,96]{3,2,1,0:T(8,128)S(1)} %pad_maximum_fusion.7), channel_id=1, source_target_pairs={{1,0},{2,1},{3,2},{5,4},{6,5},{7,6},{9,8},{10,9},{11,10},{13,12},{... | collective-permute-start | bytes 73736 | tf_op jit(solution)/shard_map/ppermute | solution.py:33
  41.8 13.4 %copy-start.8 = (bf16[1,8,8,96]{3,2,1,0:T(8,128)(2,1)S(1)}, bf16[1,8,8,96]{3,2,1,0:T(8,128)(2,1)}, u32[]{:S(2)}) copy-start(bf16[1,8,8,96]{3,2,1,0:T(8,128)(2,1)} %copy-done.7) | copy-start | bytes 36868
  41.8 13.4 %copy-start.10 = (bf16[1,8,8,96]{3,2,1,0:T(8,128)(2,1)S(1)}, bf16[1,8,8,96]{3,2,1,0:T(8,128)(2,1)}, u32[]{:S(2)}) copy-start(bf16[1,8,8,96]{3,2,1,0:T(8,128)(2,1)} %copy-done.9) | copy-start | bytes 36868
  42.9 79.6 %collective-permute-start.4 = (bf16[1,8,8,96]{3,2,1,0:T(8,128)(2,1)S(1)}, bf16[1,8,8,96]{3,2,1,0:T(8,128)(2,1)S(1)}, u32[]{:S(2)}, u32[]{:S(2)}) collective-permute-start(bf16[1,8,8,96]{3,2,1,0:T(8,128)(2,1)S(1)} %slice.989), channel_id=1, source_target_pairs={{0,4},{4,8},{8,12},{12,16},{16,20},{20,24},{24,28},{1,5},{5,9},{9,... | collective-permute-start | bytes 36872 | tf_op jit(solution)/shard_map/ppermute | solution.py:33
  48.3 75.5 %collective-permute-start.9 = (bf16[1,8,8,96]{3,2,1,0:T(8,128)(2,1)S(1)}, bf16[1,8,8,96]{3,2,1,0:T(8,128)(2,1)S(1)}, u32[]{:S(2)}, u32[]{:S(2)}) collective-permute-start(bf16[1,8,8,96]{3,2,1,0:T(8,128)(2,1)S(1)} %get-tuple-element.86), channel_id=1, source_target_pairs={{4,0},{8,4},{12,8},{16,12},{20,16},{24,20},{28,24},{5,1},{9,5},{13... | collective-permute-start | bytes 36872 | tf_op jit(solution)/shard_map/ppermute | solution.py:25
  49.6 74.2 %collective-permute-start.8 = (bf16[1,8,8,96]{3,2,1,0:T(8,128)(2,1)S(1)}, bf16[1,8,8,96]{3,2,1,0:T(8,128)(2,1)S(1)}, u32[]{:S(2)}, u32[]{:S(2)}) collective-permute-start(bf16[1,8,8,96]{3,2,1,0:T(8,128)(2,1)S(1)} %get-tuple-element.85), channel_id=1, source_target_pairs={{0,4},{4,8},{8,12},{12,16},{16,20},{20,24},{24,28},{1,5},{5,9},{9,... | collective-permute-start | bytes 36872 | tf_op jit(solution)/shard_map/ppermute | solution.py:24
  121.9 139.1 %copy-start.1 = (bf16[27,96,96]{2,1,0:T(8,128)(2,1)S(1)}, bf16[27,96,96]{2,1,0:T(8,128)(2,1)}, u32[]{:S(2)}) copy-start(bf16[27,96,96]{2,1,0:T(8,128)(2,1)} %param.10) | copy-start | bytes 1492996
  122.5 9.4 %collective-permute-start.5 = (bf16[9,1,8,96]{3,2,1,0:T(8,128)(2,1)S(1)}, bf16[9,1,8,96]{3,2,1,0:T(8,128)(2,1)S(1)}, u32[]{:S(2)}, u32[]{:S(2)}) collective-permute-start(bf16[9,1,8,96]{3,2,1,0:T(8,128)(2,1)S(1)} %pad_maximum_fusion.14), channel_id=1, source_target_pairs={{0,1},{1,2},{2,3},{4,5},{5,6},{6,7},{8,9},{9,10},{10,11},{12,13},{... | collective-permute-start | bytes 41480 | tf_op jit(solution)/shard_map/ppermute | solution.py:33
  123.8 8.1 %copy-start.11 = (bf16[1,8,8,96]{3,2,1,0:T(8,128)(2,1)}, bf16[1,8,8,96]{3,2,1,0:T(8,128)(2,1)S(1)}, u32[]{:S(2)}) copy-start(bf16[1,8,8,96]{3,2,1,0:T(8,128)(2,1)S(1)} %collective-permute-done.8) | copy-start | bytes 36868
  124.5 154.6 %collective-permute-start.11 = (bf16[10,1,8,96]{3,2,1,0:T(8,128)(2,1)}, bf16[10,1,8,96]{3,2,1,0:T(8,128)(2,1)}, u32[]{:S(2)}, u32[]{:S(2)}) collective-permute-start(bf16[10,1,8,96]{3,2,1,0:T(8,128)(2,1)} %get-tuple-element.78), channel_id=1, source_target_pairs={{1,0},{2,1},{3,2},{5,4},{6,5},{7,6},{9,8},{10,9},{11,10},{13,12},{... | collective-permute-start | bytes 46088 | tf_op jit(solution)/shard_map/ppermute | solution.py:25
  125.8 153.3 %collective-permute-start.10 = (bf16[10,1,8,96]{3,2,1,0:T(8,128)(2,1)}, bf16[10,1,8,96]{3,2,1,0:T(8,128)(2,1)}, u32[]{:S(2)}, u32[]{:S(2)}) collective-permute-start(bf16[10,1,8,96]{3,2,1,0:T(8,128)(2,1)} %get-tuple-element.77), channel_id=1, source_target_pairs={{0,1},{1,2},{2,3},{4,5},{5,6},{6,7},{8,9},{9,10},{10,11},{12,13},{... | collective-permute-start | bytes 46088 | tf_op jit(solution)/shard_map/ppermute | solution.py:24
  260.0 5.5 %copy-start.40 = (bf16[4,4,4,96]{3,2,1,0:T(4,128)(2,1)S(1)}, bf16[4,4,4,96]{3,2,1,0:T(4,128)(2,1)}, u32[]{:S(2)}) copy-start(bf16[4,4,4,96]{3,2,1,0:T(4,128)(2,1)} %slice.817) | copy-start | bytes 36868
  260.0 6.6 %copy-start.39 = (bf16[4,4,4,96]{3,2,1,0:T(4,128)(2,1)S(1)}, bf16[4,4,4,96]{3,2,1,0:T(4,128)(2,1)}, u32[]{:S(2)}) copy-start(bf16[4,4,4,96]{3,2,1,0:T(4,128)(2,1)} %slice.819) | copy-start | bytes 36868
  260.0 8.6 %copy-start.38 = (bf16[4,4,4,96]{3,2,1,0:T(4,128)(2,1)S(1)}, bf16[4,4,4,96]{3,2,1,0:T(4,128)(2,1)}, u32[]{:S(2)}) copy-start(bf16[4,4,4,96]{3,2,1,0:T(4,128)(2,1)} %slice.821) | copy-start | bytes 36868
  260.0 8.8 %copy-start.15 = (bf16[4,4,4,96]{3,1,2,0:T(4,128)(2,1)S(1)}, bf16[4,4,4,96]{3,1,2,0:T(4,128)(2,1)}, u32[]{:S(2)}) copy-start(bf16[4,4,4,96]{3,1,2,0:T(4,128)(2,1)} %copy-done.14) | copy-start | bytes 36868
  260.0 8.8 %copy-start.37 = (bf16[4,4,4,96]{3,2,1,0:T(4,128)(2,1)S(1)}, bf16[4,4,4,96]{3,2,1,0:T(4,128)(2,1)}, u32[]{:S(2)}) copy-start(bf16[4,4,4,96]{3,2,1,0:T(4,128)(2,1)} %slice.823) | copy-start | bytes 36868
  261.9 7.3 %copy-start.36 = (bf16[4,4,4,96]{3,2,1,0:T(4,128)(2,1)S(1)}, bf16[4,4,4,96]{3,2,1,0:T(4,128)(2,1)}, u32[]{:S(2)}) copy-start(bf16[4,4,4,96]{3,2,1,0:T(4,128)(2,1)} %slice.825) | copy-start | bytes 36868
  263.7 5.8 %copy-start.35 = (bf16[4,4,4,96]{3,2,1,0:T(4,128)(2,1)S(1)}, bf16[4,4,4,96]{3,2,1,0:T(4,128)(2,1)}, u32[]{:S(2)}) copy-start(bf16[4,4,4,96]{3,2,1,0:T(4,128)(2,1)} %slice.827) | copy-start | bytes 36868
  265.5 4.3 %copy-start.34 = (bf16[4,4,4,96]{3,2,1,0:T(4,128)(2,1)S(1)}, bf16[4,4,4,96]{3,2,1,0:T(4,128)(2,1)}, u32[]{:S(2)}) copy-start(bf16[4,4,4,96]{3,2,1,0:T(4,128)(2,1)} %slice.829) | copy-start | bytes 36868
  266.6 3.6 copy-start.33
  267.6 2.9 copy-start.32
  268.7 2.1 copy-start.31
  269.1 2.1 copy-start.30
  269.5 2.1 copy-start.29
  269.8 2.1 copy-start.28
  270.2 2.1 copy-start.27
  270.5 2.1 copy-start.26
  270.9 2.1 copy-start.25
  271.2 2.1 copy-start.24
  271.6 2.1 copy-start.23
  271.9 2.1 copy-start.22
  272.3 2.1 copy-start.21
  272.6 2.1 copy-start.20
  273.7 2.7 copy-start.17
  276.6 2.4 copy-start.3
  415.1 2.6 copy-start.2
  (8 other events, 9.7 us)
Sparse Core Ops, SparseCore 0:
  279.2 135.8 all-reduce.6
where the time goes:
time: 427 us; the launch traced here: 426 us
  local copies, waits for them, and re-layouts  135 us (32%)
  waiting for transfers between devices  128 us (30%)
  matrix products  56.4 us (13%)
  blocking collectives  44.4 us (10%)
  starting transfers between devices  34.6 us (8%)
  between operations  15.4 us (4%)
  other arithmetic  11.6 us (3%)
    slice x27, local copies, waits for them, and re-layouts, stride_window(): lax.slice(padded, (1 + step_x, 1 + step_y, 1 + step_z, 0), (2 + step_x +...  128 us
    psum x1, waiting for transfers between devices, on_device(): lax.psum((grad_conv, grad_bias, grad_stride), ('gx', 'gy'))  127 us
    psum x1, blocking collectives, on_device(): lax.psum((grad_conv, grad_bias, grad_stride), ('gx', 'gy'))  44.4 us
    dot_general x27, matrix products, weight_taps(): jnp.dot(window.reshape(-1, channels).T, flat_grad, preferred_element_type...  22.8 us
    ppermute x4, starting transfers between devices, with_halo(): before = lax.ppermute(last, axis, up)  20.1 us
    dot_general x54, matrix products, conv_same(): jnp.dot(window.reshape(-1, channels), weight[tap_index], preferred_elemen...  10.8 us
    dot_general x27, matrix products, stride_weight(): jnp.dot(window.reshape(-1, channels).T, flat_grad, preferred_element_type...  10.4 us
    ppermute x4, starting transfers between devices, from_behind(): return lax.ppermute(block, axis, route)  9.31 us
  transfers between devices with their start and end apart: 13, of which 2 were waited for; matrix products, arithmetic and copies ran while one was open for 46% of the time, Pallas kernels for 0%

commit v1 on v0

v1 whole, which is shorter than its diff:
```python
import functools
import math

import jax
import jax.numpy as jnp
from jax import lax
from jax.experimental import pallas as pl
from jax.experimental.pallas import tpu as pltpu
from jax.sharding import Mesh
from jax.sharding import PartitionSpec as P

LANES = 128
F32 = jnp.float32
BF16 = jnp.bfloat16
NT = (((1,), (1,)), ((), ()))
TN = (((0,), (0,)), ((), ()))
VMEM_BYTES = 60 * 1024 * 1024


def call(body, outs, scratch=(), cost=None, name=None):
    return pl.pallas_call(
        body,
        out_shape=tuple(jax.ShapeDtypeStruct(s, d) for s, d in outs),
        scratch_shapes=[pltpu.VMEM(s, d) for s, d in scratch],
        compiler_params=pltpu.CompilerParams(vmem_limit_bytes=VMEM_BYTES),
        cost_estimate=cost,
        name=name,
    )


def lane_of(shape):
    return lax.broadcasted_iota(jnp.int32, shape, len(shape) - 1)


def z_of(shape):
    return lax.broadcasted_iota(jnp.int32, shape, len(shape) - 2)


def below(v):
    return jnp.where(z_of(v.shape) == 0, 0.0, pltpu.roll(v, 1, axis=1))


def above(v):
    top = v.shape[1] - 1
    return jnp.where(z_of(v.shape) == top, 0.0, pltpu.roll(v, top, axis=1))


def first_kernel(dims, vox_ref, occ_ref, cot_ref, x_ref, u_ref, core_ref, side_ref, xs, us):
    tx, ty, tz, ch = dims
    hx, hy = tx // 2, ty // 2
    occ = occ_ref[...].astype(F32).reshape(tx * ty, tz, LANES)
    xs[...] = jnp.zeros(xs.shape, F32)
    xs[:, :ch] = vox_ref[...].astype(F32)
    x = xs[...].reshape(tx * ty, tz, LANES)
    x = jnp.where(lane_of(x.shape) == ch, 1.0, x) * occ
    xs[...] = x.reshape(xs.shape)
    x_ref[...] = xs[...].astype(BF16)
    pairs = occ.reshape(hx, 2, hy, 2, tz, LANES)
    pairs = jnp.maximum(pairs[:, 0], pairs[:, 1])
    pairs = jnp.maximum(pairs[:, :, 0], pairs[:, :, 1]).reshape(hx * hy, tz, LANES)
    coarse = jnp.maximum(pairs, pltpu.roll(pairs, tz - 1, axis=1))
    us[...] = jnp.zeros(us.shape, F32)
    cot = jnp.concatenate(
        [cot_ref[...].astype(F32), jnp.zeros((hx * hy * tz // 2, LANES - ch), F32)], axis=1
    )
    us[pl.ds(0, hx * hy * tz // 2, stride=2), :] = cot
    u = us[...].reshape(hx * hy, tz, LANES)
    even = lax.rem(z_of(u.shape), 2) == 0
    u = jnp.where((lane_of(u.shape) == ch) & even, 1.0, u) * coarse
    us[...] = u.reshape(us.shape)
    u_ref[...] = us[...].astype(BF16)
    core = lax.axis_index("core")
    x4, u4 = xs.reshape(tx, ty, tz, LANES), us.reshape(hx, hy, tz, LANES)
    rows = tx * 2 * tz
    for ref, low in ((core_ref, core), (side_ref, 1 - core)):
        start = (1 - low) * (ty - 2)
        ref[:rows] = x4[:, pl.ds(start, 2)].reshape(rows, LANES).astype(BF16)
        ref[rows:] = (
            u4[:, pl.ds((1 - low) * (hy - 1), 1)].reshape(hx * tz, LANES).astype(BF16)
        )


def second_kernel(dims, x_ref, u_ref, core_ref, side_ref, near_ref, far_ref, xe, ue):
    tx, ty, tz, _ = dims
    widen(dims, x_ref, u_ref, core_ref, side_ref, xe, ue, 0, 0)
    odd = lax.rem(lax.axis_index("gx"), 2)
    rows = 2 * (ty + 4) * tz
    hx, hy = tx // 2, ty // 2
    for ref, low in ((near_ref, odd), (far_ref, 1 - odd)):
        ref[:rows] = xe[pl.ds((1 - low) * (tx - 2), 2)].reshape(rows, LANES).astype(BF16)
        ref[rows:] = (
            ue[pl.ds((1 - low) * (hx - 1), 1)].reshape((hy + 2) * tz, LANES).astype(BF16)
        )


def widen(dims, x_ref, u_ref, core_ref, side_ref, xe, ue, x0, u0):
    tx, ty, tz, _ = dims
    hx, hy = tx // 2, ty // 2
    rows = tx * 2 * tz
    core = lax.axis_index("core")
    xe[x0 : x0 + tx, 2 : 2 + ty] = x_ref[...].astype(F32).reshape(tx, ty, tz, LANES)
    ue[u0 : u0 + hx, 1 : 1 + hy] = u_ref[...].astype(F32).reshape(hx, hy, tz, LANES)
    for ref, low in ((core_ref, core), (side_ref, 1 - core)):
        xe[x0 : x0 + tx, pl.ds((1 - low) * (ty + 2), 2)] = (
            ref[:rows].astype(F32).reshape(tx, 2, tz, LANES)
        )
        ue[u0 : u0 + hx, pl.ds((1 - low) * (hy + 1), 1)] = (
            ref[rows:].astype(F32).reshape(hx, 1, tz, LANES)
        )


def pad_weight(ch, w_ref, out):
    out[...] = jnp.zeros(out.shape, BF16)
    for t in range(w_ref.shape[0]):
        out[t // 3, (t % 3) * LANES : (t % 3) * LANES + ch, :ch] = w_ref[t]


def transposed_taps(w, ab):
    return jnp.concatenate([w[ab, e * LANES : (e + 1) * LANES] for e in range(3)], axis=1)


def pack_block(block, ch):
    free = LANES - ch
    keep = ch * ch // LANES
    tail = block[keep:ch]
    parts = [
        pltpu.roll(tail, (LANES - free - p * free) % LANES, axis=1) for p in range(ch // free)
    ]
    parts = jnp.concatenate(parts, axis=0)
    main = block[:keep]
    return jnp.where(lane_of(main.shape) < ch, main, parts)


def unpack_block(packed, ch):
    free = LANES - ch
    keep = ch * ch // LANES
    tall = ch - keep
    lane = lane_of((tall, LANES))
    tail = None
    for p in range(ch // free):
        part = packed[p * tall : (p + 1) * tall]
        part = pltpu.roll(part, (free + p * free) % LANES, axis=1)
        tail = part if tail is None else jnp.where(lane < p * free, tail, part)
    return jnp.concatenate([packed, tail], axis=0)


def main_kernel(
    dims, half_rows, x_ref, u_ref, core_ref, side_ref, near_ref, far_ref, cw_ref, dw_ref, bias_ref,
    keep_ref, send_ref, gp_ref, gs_ref, s_ref,
    xe, ue, z3, u3, s3, acc, gsr, gp, wf, wd, pack,
):
    tx, ty, tz, ch = dims
    hx, hy = tx // 2, ty // 2
    ex, ey = tx + 2, ty + 2
    block_rows = ch * ch // LANES
    core = lax.axis_index("core")
    odd = lax.rem(lax.axis_index("gx"), 2)
    pad_weight(ch, cw_ref, wf)
    pad_weight(ch, dw_ref, wd)
    widen(dims, x_ref, u_ref, core_ref, side_ref, xe, ue, 2, 1)
    rows = 2 * (ty + 4) * tz
    for ref, low in ((near_ref, odd), (far_ref, 1 - odd)):
        xe[pl.ds((1 - low) * (tx + 2), 2)] = ref[:rows].astype(F32).reshape(2, ty + 4, tz, LANES)
        ue[pl.ds((1 - low) * (hx + 1), 1)] = ref[rows:].astype(F32).reshape(1, hy + 2, tz, LANES)

    def shift_x(i, _):
        v = xe[i]
        v = jnp.where(lane_of(v.shape) == ch + 1, 1.0, v)
        z3[i, :, :, :LANES] = below(v)
        z3[i, :, :, LANES : 2 * LANES] = v
        z3[i, :, :, 2 * LANES :] = above(v)
        return 0

    lax.fori_loop(0, tx + 4, shift_x, 0)
    for i in range(hx + 2):
        v = ue[i]
        u3[i, :, :, :LANES] = above(v)
        u3[i, :, :, LANES : 2 * LANES] = v
        u3[i, :, :, 2 * LANES :] = below(v)

    acc[...] = jnp.zeros(acc.shape, F32)

    def forward(ab, _):
        a, b = ab // 3, lax.rem(ab, 3)
        win = z3[pl.ds(a, ex), pl.ds(b, ey)].reshape(ex * ey * tz, 3 * LANES).astype(BF16)
        out = jnp.dot(win, wf[ab], preferred_element_type=F32)
        acc[...] += out.reshape(acc.shape)
        return 0

    lax.fori_loop(0, 9, forward, 0)

    terms = {0: ((2, 0), (0, 1)), 1: ((1, 1),)}
    for px in (0, 1):
        for py in (0, 1):
            total = None
            for a, sx in terms[px]:
                for b, sy in terms[py]:
                    win = u3[sx : sx + hx + 1, sy : sy + hy + 1]
                    win = win.reshape((hx + 1) * (hy + 1) * tz, 3 * LANES).astype(BF16)
                    out = lax.dot_general(
                        win, transposed_taps(wd, a * 3 + b), NT, preferred_element_type=F32
                    )
                    total = out if total is None else total + out
            gsr[:, px, :, py] = total.reshape(hx + 1, hy + 1, tz, LANES)

    def pointwise(i, _):
        v = acc[i] + bias_ref[...].reshape(1, 1, LANES)
        x = xe[i + 1, 1 : 1 + ey]
        live = jnp.broadcast_to(x[:, :, ch : ch + 1], x.shape)
        s = 1.0 / (1.0 + jnp.exp(-v))
        summed = (x + live * (v * s)).astype(BF16).astype(F32)
        for k, t in enumerate((below(summed), summed, above(summed))):
            s3[i // 2, lax.rem(i, 2), :, :, :, k * LANES : (k + 1) * LANES] = t.reshape(
                hy + 1, 2, tz, LANES
            )
        g = gsr[i // 2, lax.rem(i, 2)].reshape(ey, tz, LANES)
        gp[i] = (g * live * s * (1.0 + v * (1.0 - s))).astype(BF16).astype(F32)
        return 0

    lax.fori_loop(0, ex, pointwise, 0)

    pack[...] = jnp.zeros(pack.shape, F32)
    grad = gp[1 : 1 + tx, 1 : 1 + ty].reshape(tx * ty * tz, LANES).astype(BF16)

    def conv_taps(ab, _):
        a, b = ab // 3, lax.rem(ab, 3)
        win = z3[pl.ds(a + 1, tx), pl.ds(b + 1, ty)].reshape(tx * ty * tz, 3 * LANES).astype(BF16)
        out = lax.dot_general(win, grad, TN, preferred_element_type=F32)
        for e in range(3):
            at = pl.multiple_of((ab * 3 + e) * block_rows, 8)
            pack[0, pl.ds(at, block_rows)] = pack_block(out[e * LANES : e * LANES + ch], ch)

        @pl.when(ab == 4)
        def _():
            pack[0, 27 * block_rows : 27 * block_rows + 8] = out[LANES + ch : LANES + ch + 8]

        return 0

    lax.fori_loop(0, 9, conv_taps, 0)
    cot = u3[1 : 1 + hx, 1 : 1 + hy, :, LANES : 2 * LANES].reshape(hx * hy * tz, LANES).astype(BF16)

    def down_taps(ab, _):
        a, b = ab // 3, lax.rem(ab, 3)
        win = s3[pl.ds(a // 2, hx), lax.rem(a, 2), pl.ds(b // 2, hy), lax.rem(b, 2)]
        win = win.reshape(hx * hy * tz, 3 * LANES).astype(BF16)
        out = lax.dot_general(win, cot, TN, preferred_element_type=F32)
        for e in range(3):
            at = pl.multiple_of((ab * 3 + e) * block_rows, 8)
            pack[1, pl.ds(at, block_rows)] = pack_block(out[e * LANES : e * LANES + ch], ch)
        return 0

    lax.fori_loop(0, 9, down_taps, 0)
    keep_ref[...] = pack[core].astype(BF16)
    send_ref[...] = pack[1 - core].astype(BF16)
    gp_ref[...] = gp[...].reshape(ex * ey * tz, LANES).astype(BF16)
    gs_ref[...] = gsr[...].reshape(ex, ey, tz, LANES)[1 : 1 + tx, 1 : 1 + ty].reshape(
        tx * ty * tz, LANES
    )
    s_ref[...] = (
        s3[:, :, :, :, :, LANES : 2 * LANES].reshape(ex * ey * tz, LANES).astype(BF16)
    )


def second_outputs(
    dims, x_ref, u_ref, gp_ref, gs_ref, s_ref, cw_ref, dw_ref, down_ref, gv_ref,
    g3, s3, acc, accd, wf, wd,
):
    tx, ty, tz, ch = dims
    hx, hy = tx // 2, ty // 2
    ex, ey = tx + 2, ty + 2
    pad_weight(ch, cw_ref, wf)
    pad_weight(ch, dw_ref, wd)
    v = gp_ref[...].astype(F32).reshape(ex * ey, tz, LANES)
    for k, t in enumerate((above(v), v, below(v))):
        g3[:, :, :, k * LANES : (k + 1) * LANES] = t.reshape(ex, ey, tz, LANES)
    v = s_ref[...].astype(F32).reshape(ex * ey, tz, LANES)
    for k, t in enumerate((below(v), v, above(v))):
        s3[:, :, :, :, :, k * LANES : (k + 1) * LANES] = t.reshape(hx + 1, 2, hy + 1, 2, tz, LANES)
    acc[...] = gs_ref[...]
    accd[...] = jnp.zeros(accd.shape, F32)

    def taps(ab, _):
        a, b = ab // 3, lax.rem(ab, 3)
        win = g3[pl.ds(2 - a, tx), pl.ds(2 - b, ty)].reshape(tx * ty * tz, 3 * LANES).astype(BF16)
        acc[...] += lax.dot_general(win, transposed_taps(wf, ab), NT, preferred_element_type=F32)
        win = s3[pl.ds(a // 2, hx), lax.rem(a, 2), pl.ds(b // 2, hy), lax.rem(b, 2)]
        win = win.reshape(hx * hy * tz, 3 * LANES).astype(BF16)
        accd[...] += jnp.dot(win, wd[ab], preferred_element_type=F32)
        return 0

    lax.fori_loop(0, 9, taps, 0)
    x = x_ref[...].astype(F32)
    live = jnp.broadcast_to(x[:, ch : ch + 1], x.shape)
    gv_ref[...] = (acc[...] * live)[:, :ch].astype(BF16)
    u = u_ref[...].astype(F32)
    accd[...] = accd[...] * jnp.broadcast_to(u[:, ch : ch + 1], u.shape)
    down_ref[...] = accd[pl.ds(0, hx * hy * tz // 2, stride=2), :][:, :ch].astype(BF16)


def last_kernel(ch, factor, *refs):
    own, other = refs[:4], refs[4:8]
    conv_ref, down_ref, bias_ref, full = refs[8:]
    core = lax.axis_index("core")
    me = lax.rem(lax.axis_index("gx"), 2) * 2 + lax.rem(lax.axis_index("gyc"), 2)
    rows = own[0].shape[0]
    block_rows = ch * ch // LANES
    for k in range(4):
        at = pl.ds(pl.multiple_of((me ^ k) * rows, 16), rows)
        full[core, at] = own[k][...].astype(F32) * factor
        full[1 - core, at] = other[k][...].astype(F32) * factor
    for h, ref in ((0, conv_ref), (1, down_ref)):
        for t in range(27):
            block = unpack_block(full[h, t * block_rows : (t + 1) * block_rows], ch)
            ref[t] = block[:, :ch]
    bias_ref[...] = full[0, 27 * block_rows + 1 : 27 * block_rows + 2, :ch]


def on_device(voxels, occupancy, conv_weight, conv_bias, down_weight, down_cotangent):
    tx, ty, tz, ch = voxels.shape
    hx, hy, hz = tx // 2, ty // 2, tz // 2
    ex, ey = tx + 2, ty + 2
    dims = (tx, ty, tz, ch)
    n_gx, n_gyc = lax.axis_size("gx"), lax.axis_size("gyc")
    fine, coarse = tx * ty * tz, hx * hy * tz

    occ = jnp.broadcast_to(occupancy.astype(BF16)[..., None], (tx, ty, tz, LANES))
    side_rows = tx * 2 * tz + hx * tz
    row_rows = 2 * (ty + 4) * tz + (hy + 2) * tz
    x, u, to_core, to_side = call(
        functools.partial(first_kernel, dims),
        [((fine, LANES), BF16), ((coarse, LANES), BF16)] + [((side_rows, LANES), BF16)] * 2,
        [((fine, LANES), F32), ((coarse, LANES), F32)],
        name="first",
    )(
        voxels.reshape(fine, ch),
        occ.reshape(fine, LANES),
        down_cotangent.reshape(hx * hy * hz, ch),
    )
    swap = [(0, 1), (1, 0)]
    n_gy = n_gyc * 2
    sides = [(i, i + 1) for i in range(1, n_gy - 1, 2)]
    sides += [(j, i) for i, j in sides]
    from_core = lax.ppermute(to_core, "core", swap)
    from_side = lax.ppermute(to_side, ("gyc", "core"), sides)
    to_near, to_far = call(
        functools.partial(second_kernel, dims),
        [((row_rows, LANES), BF16)] * 2,
        [((tx, ty + 4, tz, LANES), F32), ((hx, hy + 2, tz, LANES), F32)],
        name="second",
    )(x, u, from_core, from_side)
    near = [(i, i ^ 1) for i in range(n_gx)]
    far = [(i, i + 1) for i in range(1, n_gx - 1, 2)]
    far += [(j, i) for i, j in far]
    from_near = lax.ppermute(to_near, "gx", near)
    from_far = lax.ppermute(to_far, "gx", far)

    block_rows = ch * ch // LANES
    half_rows = -(-(27 * block_rows + 8) // 64) * 64
    bias = jnp.pad(conv_bias, (0, LANES - ch)).reshape(1, LANES)
    keep, send, gp, gs, s = call(
        functools.partial(main_kernel, dims, half_rows),
        [((half_rows, LANES), BF16)] * 2
        + [((ex * ey * tz, LANES), BF16), ((fine, LANES), F32), ((ex * ey * tz, LANES), BF16)],
        [
            ((tx + 4, ty + 4, tz, LANES), F32),
            ((hx + 2, hy + 2, tz, LANES), F32),
            ((tx + 4, ty + 4, tz, 3 * LANES), F32),
            ((hx + 2, hy + 2, tz, 3 * LANES), F32),
            ((hx + 1, 2, hy + 1, 2, tz, 3 * LANES), F32),
            ((ex, ey, tz, LANES), F32),
            ((hx + 1, 2, hy + 1, 2, tz, LANES), F32),
            ((ex, ey, tz, LANES), F32),
            ((9, 3 * LANES, LANES), BF16),
            ((9, 3 * LANES, LANES), BF16),
            ((2, half_rows, LANES), F32),
        ],
        name="main",
    )(x, u, from_core, from_side, from_near, from_far, conv_weight, down_weight, bias)

    down, grad_voxels = call(
        functools.partial(second_outputs, dims),
        [((hx * hy * hz, ch), BF16), ((fine, ch), BF16)],
        [
            ((ex, ey, tz, 3 * LANES), F32),
            ((hx + 1, 2, hy + 1, 2, tz, 3 * LANES), F32),
            ((fine, LANES), F32),
            ((coarse, LANES), F32),
            ((9, 3 * LANES, LANES), BF16),
            ((9, 3 * LANES, LANES), BF16),
        ],
        cost=pl.CostEstimate(flops=5_000_000_000, bytes_accessed=4_000_000, transcendentals=0),
        name="outputs",
    )(x, u, gp, gs, s, conv_weight, down_weight)

    def plus(a, b):
        return (a.astype(F32) + b.astype(F32)).astype(BF16)

    got = lax.ppermute(send, "core", swap)
    me = lax.rem(lax.axis_index("gx"), 2) * 2 + lax.rem(lax.axis_index("gyc"), 2)
    quarter = half_rows // 4
    keep4, got4 = keep.reshape(4, quarter, LANES), got.reshape(4, quarter, LANES)

    def quarter_of(k):
        pick = functools.partial(lax.dynamic_index_in_dim, index=me ^ k, axis=0, keepdims=False)
        return pick(keep4).astype(F32) + pick(got4).astype(F32)

    def across(value, k):
        route = []
        for i in range(n_gx):
            for j in range(n_gyc):
                route.append((i * n_gyc + j, (i ^ (k >> 1)) * n_gyc + (j ^ (k & 1))))
        return lax.ppermute(value, ("gx", "gyc"), route)

    arrived = [across(quarter_of(k).astype(BF16), k) for k in (1, 2, 3)]
    total = quarter_of(0)
    for piece in arrived:
        total = total + piece.astype(F32)
    total = total.astype(BF16)
    for axis, peers in (("gx", n_gx), ("gyc", n_gyc)):
        step = 2
        while step < peers:
            total = plus(total, lax.ppermute(total, axis, [(i, i ^ step) for i in range(peers)]))
            step *= 2
    own = [total] + [across(total, k) for k in (1, 2, 3)]
    other = [lax.ppermute(piece, "core", swap) for piece in own]
    factor = 1.0 / math.sqrt(tx * n_gx * ty * n_gy * tz)
    grad_conv, grad_down, grad_bias = call(
        functools.partial(last_kernel, ch, factor),
        [((27, ch, ch), F32), ((27, ch, ch), F32), ((1, ch), F32)],
        [((2, half_rows, LANES), F32)],
        name="last",
    )(*own, *other)
    return (
        down.reshape(hx, hy, hz, ch),
        grad_voxels.reshape(tx, ty, tz, ch),
        grad_conv,
        grad_bias.reshape(ch),
        grad_down,
    )


def solution(mesh):
    n_gx, n_gy = mesh.shape["gx"], mesh.shape["gy"]
    split = Mesh(mesh.devices.reshape(n_gx, n_gy // 2, 2), ("gx", "gyc", "core"))
    gy = ("gyc", "core")
    placed = (
        P("gx", gy, None, None),
        P("gx", gy, None),
        P(),
        P(),
        P(),
        P("gx", gy, None, None),
    )
    return jax.shard_map(
        on_device,
        mesh=split,
        in_specs=placed,
        out_specs=(P("gx", gy, None, None), P("gx", gy, None, None), P(), P(), P()),
        check_vma=False,
    )
```

time: 427 us -> 81 us (0.19)
  local copies, waits for them, and re-layouts: 135 us -> 5.29 us
  waiting for transfers between devices: 128 us -> 19.9 us
  matrix products: 56.4 us -> 0 us
  blocking collectives: 44.4 us -> 0 us
  Pallas kernels: 0 us -> 26.8 us
  between operations: 15.4 us -> 0.76 us
  starting transfers between devices: 34.6 us -> 24.8 us
  other arithmetic: 11.6 us -> 2.98 us
    slice x46 -> x0, local copies, waits for them, and re-layouts: 129 us -> none  [the longest x27 128 us: stride_window(): lax.slice(padded, (1 + step_x, 1 + step_y, 1 + step_z, 0), (2 + step_x +...]
    psum x1 -> x0, waiting for transfers between devices: 127 us -> none  [on_device(): lax.psum((grad_conv, grad_bias, grad_stride), ('gx', 'gy'))]
    dot_general x162 -> x0, matrix products: 56.4 us -> none  [the longest x27 22.8 us: weight_taps(): jnp.dot(window.reshape(-1, channels).T, flat_grad, preferred_element_type...]
    psum x1 -> x0, blocking collectives: 44.4 us -> none  [on_device(): lax.psum((grad_conv, grad_bias, grad_stride), ('gx', 'gy'))]
    pallas_call x0 -> x5, Pallas kernels: none -> 26.8 us  [the longest x1 14.3 us: on_device(): call(functools.partial(main_kernel, dims, half_rows), [((half_rows, LANES...]
    ppermute x12 -> x17, waiting for transfers between devices: 0.8 us -> 19.9 us  [the longest x6 9.82 us: across(): return lax.ppermute(value, ('gx', 'gyc'), route)]
    ppermute x12 -> x17, starting transfers between devices: 34.6 us -> 24.8 us  [the longest x6 10.6 us: across(): return lax.ppermute(value, ('gx', 'gyc'), route)]
  transfers between devices with their start and end apart: 13 -> 17, of which waited for: 2 -> 10; matrix products, arithmetic and copies ran while one was open for 46% -> 1% of each run, Pallas kernels for 0% -> 7%
where the time goes in v1:
time: 81 us; the launch traced here: 80.5 us
  Pallas kernels  26.8 us (33%)
  starting transfers between devices  24.8 us (31%)
  waiting for transfers between devices  19.9 us (25%)
  local copies, waits for them, and re-layouts  5.29 us (7%)
  other arithmetic  2.98 us (4%)
    pallas_call x1, Pallas kernels, on_device(): call(functools.partial(main_kernel, dims, half_rows), [((half_rows, LANES...  14.3 us
    ppermute x6, starting transfers between devices, across(): return lax.ppermute(value, ('gx', 'gyc'), route)  10.6 us
    ppermute x6, waiting for transfers between devices, across(): return lax.ppermute(value, ('gx', 'gyc'), route)  9.82 us
    ppermute x2, waiting for transfers between devices, on_device(): lax.ppermute(total, axis, [(i, i ^ step) for i in range(peers)])  7.33 us
    ppermute x2, starting transfers between devices, on_device(): lax.ppermute(total, axis, [(i, i ^ step) for i in range(peers)])  5.8 us
    pallas_call x1, Pallas kernels, on_device(): call(functools.partial(second_outputs, dims), [((hx * hy * hz, ch), BF16)...  5.71 us
    ppermute x1, starting transfers between devices, on_device(): got = lax.ppermute(send, 'core', swap)  3.73 us
    pallas_call x1, Pallas kernels, on_device(): call(functools.partial(last_kernel, ch, factor), [((27, ch, ch), F32), ((...  3.44 us
  transfers between devices with their start and end apart: 17, of which 10 were waited for; matrix products, arithmetic and copies ran while one was open for 1% of the time, Pallas kernels for 7%

profile of v1, /device:TPU:0, one launch (start us, length us, event | category | flops | bytes accessed | tf_op | source)
XLA Modules:
  0.0 80.5 jit_solution(6123106498852537927)
XLA Ops:
  0.6 0.8 convert_element_type.85
  1.4 0.1 broadcast_in_dim.8
  1.5 0.8 broadcast_in_dim.9.occ_ref
  2.3 1.7 %first.1 = (bf16[512,128]{1,0:T(8,128)(2,1)}, bf16[128,128]{1,0:T(8,128)(2,1)}, bf16[160,128]{1,0:T(8,128)(2,1)}, bf16[160,128]{1,0:T(8,128)(2,1)}) custom-call(bf16[512,96]{1,0:T(8,128)(2,1)} %bitcast.27, bf16[512,128]{1,0:T(8,128)(2,1)} %broadcast_in_dim.9.occ_ref, bf16[64,96]{1,0:T(8,128)(2,1)} %bitcast.28), custom_call_target="tpu_custom_call" | custom-call | tf_op jit(solution)/shard_map/first/pallas_call | solution.py:329
  4.0 0.5 collective-permute-start
  4.5 0.7 collective-permute-start.1
  5.2 0.4 collective-permute-done.core_ref
  5.6 0.0 collective-permute-done.1.side_ref
  5.6 0.6 copy-done.1
  6.2 0.0 copy-done.2
  6.2 1.6 %second.1 = (bf16[240,128]{1,0:T(8,128)(2,1)}, bf16[240,128]{1,0:T(8,128)(2,1)}) custom-call(bf16[512,128]{1,0:T(8,128)(2,1)} %get-tuple-element.21.x_ref, bf16[128,128]{1,0:T(8,128)(2,1)} %get-tuple-element.22.u_ref, bf16[160,128]{1,0:T(8,128)(2,1)} %copy-done.1, bf16[160,128]{1,0:T(8,128)(2,1)} %copy-done.2), custom_call_target="tpu_custom_call" | custom-call | tf_op jit(solution)/shard_map/second/pallas_call | solution.py:345
  7.9 2.8 %collective-permute-start.2 = (bf16[240,128]{1,0:T(8,128)(2,1)}, bf16[240,128]{1,0:T(8,128)(2,1)S(1)}, u32[]{:S(2)}, u32[]{:S(2)}) collective-permute-start(bf16[240,128]{1,0:T(8,128)(2,1)} %get-tuple-element.25), channel_id=1, source_target_pairs={{0,4},{4,0},{8,12},{12,8},{16,20},{20,16},{24,28},{28,24},{1,5},{5... | collective-permute-start | bytes 184328 | tf_op jit(solution)/shard_map/ppermute | solution.py:354
  10.7 0.7 collective-permute-start.3
  11.3 1.2 %pad_bitcast_fusion.bias_ref = f32[1,128]{1,0:T(1,128)} fusion(f32[96]{0:T(128)} %param.9), kind=kLoop, calls=%fused_computation.12 | loop fusion | bytes 896 | tf_op jit(solution)/shard_map/reshape | solution.py:359
  12.5 0.6 collective-permute-done.2.near_ref
  13.1 0.0 collective-permute-done.3.far_ref
  13.1 0.6 copy-done.10
  13.7 0.6 copy-done.11
  14.3 14.3 %main.1 = (bf16[1984,128]{1,0:T(8,128)(2,1)}, bf16[1984,128]{1,0:T(8,128)(2,1)}, bf16[800,128]{1,0:T(8,128)(2,1)}, f32[512,128]{1,0:T(8,128)}, bf16[800,128]{1,0:T(8,128)(2,1)}) custom-call(bf16[512,128]{1,0:T(8,128)(2,1)} %get-tuple-element.21.x_ref, bf16[128,128]{1,0:T(8,128)(2,1)} %get-tuple-element.22.u_ref, bf16[160,128]{1,0:T(8,128)(2,1)} %copy-done.1, ...), custom_call_target="tpu_custom_call" | custom-call | tf_op jit(solution)/shard_map/main/pallas_call | solution.py:360
  28.7 3.7 %collective-permute-start.4 = (bf16[1984,128]{1,0:T(8,128)(2,1)}, bf16[1984,128]{1,0:T(8,128)(2,1)S(1)}, u32[]{:S(2)}, u32[]{:S(2)}) collective-permute-start(bf16[1984,128]{1,0:T(8,128)(2,1)} %get-tuple-element.33), channel_id=1, source_target_pairs={{0,1},{1,0},{2,3},{3,2},{4,5},{5,4},{6,7},{7,6},{8,9},{9,8},{10,11... | collective-permute-start | bytes 1523720 | tf_op jit(solution)/shard_map/ppermute | solution.py:398
  32.4 1.7 %collective-permute-done.4 = bf16[1984,128]{1,0:T(8,128)(2,1)S(1)} collective-permute-done((bf16[1984,128]{1,0:T(8,128)(2,1)}, bf16[1984,128]{1,0:T(8,128)(2,1)S(1)}, u32[]{:S(2)}, u32[]{:S(2)}) %collective-permute-start.4) | collective-permute-done | bytes 507936 | tf_op jit(solution)/shard_map/ppermute | solution.py:398
  34.1 1.1 %fusion.3 = (bf16[496,128]{1,0:T(8,128)(2,1)S(1)}, bf16[496,128]{1,0:T(8,128)(2,1)S(1)}, bf16[496,128]{1,0:T(8,128)(2,1)S(1)}) fusion(bf16[4,496,128]{2,1,0:T(8,128)(2,1)S(1)} %bitcast.25, s32[]{:T(128)S(6)} %select_n.18, bf16[4,496,128]{2,1,0:T(8,128)(2,1)} %bitcast.23, s32[]{:T(128)S(6)} %select_n.20, s32[]{:T(128)S(6)} %select_n.19), kind=kLoop, calls=%fused_computation.9 | loop fusion | flops 761856 | bytes 1142796 | tf_op jit(solution)/shard_map/convert_element_type | solution.py:414
  35.3 2.8 %collective-permute-start.5 = (bf16[496,128]{1,0:T(8,128)(2,1)S(1)}, bf16[496,128]{1,0:T(8,128)(2,1)S(1)}, u32[]{:S(2)}, u32[]{:S(2)}) collective-permute-start(bf16[496,128]{1,0:T(8,128)(2,1)S(1)} %get-tuple-element.37), channel_id=1, source_target_pairs={{0,2},{2,0},{4,6},{6,4},{8,10},{10,8},{12,14},{14,12},{16,18},{18,... | collective-permute-start | bytes 380936 | tf_op jit(solution)/shard_map/ppermute | solution.py:412
  38.1 3.7 %collective-permute-start.7 = (bf16[496,128]{1,0:T(8,128)(2,1)S(1)}, bf16[496,128]{1,0:T(8,128)(2,1)S(1)}, u32[]{:S(2)}, u32[]{:S(2)}) collective-permute-start(bf16[496,128]{1,0:T(8,128)(2,1)S(1)} %get-tuple-element.38), channel_id=1, source_target_pairs={{0,6},{2,4},{4,2},{6,0},{8,14},{10,12},{12,10},{14,8},{16,22},{18,... | collective-permute-start | bytes 380936 | tf_op jit(solution)/shard_map/ppermute | solution.py:412
  41.8 0.5 collective-permute-start.6
  42.3 3.4 %collective-permute-done.7 = bf16[496,128]{1,0:T(8,128)(2,1)S(1)} collective-permute-done((bf16[496,128]{1,0:T(8,128)(2,1)S(1)}, bf16[496,128]{1,0:T(8,128)(2,1)S(1)}, u32[]{:S(2)}, u32[]{:S(2)}) %collective-permute-start.7) | collective-permute-done | bytes 127008 | tf_op jit(solution)/shard_map/ppermute | solution.py:412
  45.6 2.8 %collective-permute-done.6 = bf16[496,128]{1,0:T(8,128)(2,1)S(1)} collective-permute-done((bf16[496,128]{1,0:T(8,128)(2,1)S(1)}, bf16[496,128]{1,0:T(8,128)(2,1)S(1)}, u32[]{:S(2)}, u32[]{:S(2)}) %collective-permute-start.6) | collective-permute-done | bytes 127008 | tf_op jit(solution)/shard_map/ppermute | solution.py:412
  48.4 1.0 %fusion.2 = bf16[496,128]{1,0:T(8,128)(2,1)S(1)} fusion(bf16[496,128]{1,0:T(8,128)(2,1)S(1)} %collective-permute-done.7, bf16[496,128]{1,0:T(8,128)(2,1)S(1)} %collective-permute-done.6, bf16[496,128]{1,0:T(8,128)(2,1)S(1)} %collective-permute-done.5, bf16[4,496,128]{2,1,0:T(8,128)(2,1)S(1)} %bitcast.26, s32[]{:T(128)S(6)} %select_n.17, ...), kind=kLoop, calls=%fused_computation.3 | loop fusion | flops 634880 | bytes 761860 | tf_op jit(solution)/shard_map/convert_element_type | solution.py:418
  49.4 2.7 %collective-permute-start.8 = (bf16[496,128]{1,0:T(8,128)(2,1)S(1)}, bf16[496,128]{1,0:T(8,128)(2,1)S(1)}, u32[]{:S(2)}, u32[]{:S(2)}) collective-permute-start(bf16[496,128]{1,0:T(8,128)(2,1)S(1)} %fusion.2), channel_id=1, source_target_pairs={{0,8},{4,12},{8,0},{12,4},{16,24},{20,28},{24,16},{28,20},{1,9},{5... | collective-permute-start | bytes 380936 | tf_op jit(solution)/shard_map/ppermute | solution.py:422
  52.1 2.9 %collective-permute-done.8 = bf16[496,128]{1,0:T(8,128)(2,1)S(1)} collective-permute-done((bf16[496,128]{1,0:T(8,128)(2,1)S(1)}, bf16[496,128]{1,0:T(8,128)(2,1)S(1)}, u32[]{:S(2)}, u32[]{:S(2)}) %collective-permute-start.8) | collective-permute-done | bytes 127008 | tf_op jit(solution)/shard_map/ppermute | solution.py:422
  55.1 3.1 %collective-permute-start.9 = (bf16[496,128]{1,0:T(8,128)(2,1)S(1)}, bf16[496,128]{1,0:T(8,128)(2,1)S(1)}, u32[]{:S(2)}, u32[]{:S(2)}) collective-permute-start(bf16[496,128]{1,0:T(8,128)(2,1)S(1)} %add_convert_fusion.1), channel_id=1, source_target_pairs={{0,16},{4,20},{8,24},{12,28},{16,0},{20,4},{24,8},{28,12},{1,17},{... | collective-permute-start | bytes 380936 | tf_op jit(solution)/shard_map/ppermute | solution.py:422
  58.2 4.4 %collective-permute-done.9 = bf16[496,128]{1,0:T(8,128)(2,1)S(1)} collective-permute-done((bf16[496,128]{1,0:T(8,128)(2,1)S(1)}, bf16[496,128]{1,0:T(8,128)(2,1)S(1)}, u32[]{:S(2)}, u32[]{:S(2)}) %collective-permute-start.9) | collective-permute-done | bytes 127008 | tf_op jit(solution)/shard_map/ppermute | solution.py:422
  62.6 1.9 %collective-permute-start.12 = (bf16[496,128]{1,0:T(8,128)(2,1)S(1)}, bf16[496,128]{1,0:T(8,128)(2,1)S(1)}, u32[]{:S(2)}, u32[]{:S(2)}) collective-permute-start(bf16[496,128]{1,0:T(8,128)(2,1)S(1)} %add_convert_fusion.refs_0_), channel_id=1, source_target_pairs={{0,6},{2,4},{4,2},{6,0},{8,14},{10,12},{12,10},{14,8},{16,22},{18,... | collective-permute-start | bytes 380936 | tf_op jit(solution)/shard_map/ppermute | solution.py:412
  64.5 1.7 %collective-permute-start.10 = (bf16[496,128]{1,0:T(8,128)(2,1)S(1)}, bf16[496,128]{1,0:T(8,128)(2,1)S(1)}, u32[]{:S(2)}, u32[]{:S(2)}) collective-permute-start(bf16[496,128]{1,0:T(8,128)(2,1)S(1)} %add_convert_fusion.refs_0_), channel_id=1, source_target_pairs={{0,2},{2,0},{4,6},{6,4},{8,10},{10,8},{12,14},{14,12},{16,18},{18,... | collective-permute-start | bytes 380936 | tf_op jit(solution)/shard_map/ppermute | solution.py:412
  66.2 0.0 collective-permute-start.13
  66.2 2.4 %collective-permute-done.12.refs_3_ = bf16[496,128]{1,0:T(8,128)(2,1)S(1)} collective-permute-done((bf16[496,128]{1,0:T(8,128)(2,1)S(1)}, bf16[496,128]{1,0:T(8,128)(2,1)S(1)}, u32[]{:S(2)}, u32[]{:S(2)}) %collective-permute-start.12) | collective-permute-done | bytes 127008 | tf_op jit(solution)/shard_map/ppermute | solution.py:412
  68.6 0.0 collective-permute-start.16
  68.6 0.8 %collective-permute-done.11.refs_2_ = bf16[496,128]{1,0:T(8,128)(2,1)S(1)} collective-permute-done((bf16[496,128]{1,0:T(8,128)(2,1)S(1)}, bf16[496,128]{1,0:T(8,128)(2,1)S(1)}, u32[]{:S(2)}, u32[]{:S(2)}) %collective-permute-start.11) | collective-permute-done | bytes 127008 | tf_op jit(solution)/shard_map/ppermute | solution.py:412
  69.4 0.5 collective-permute-done.10.refs_1_
  69.9 0.0 collective-permute-start.14
  69.9 5.7 %outputs.1 = (bf16[64,96]{1,0:T(8,128)(2,1)}, bf16[512,96]{1,0:T(8,128)(2,1)}) custom-call(bf16[512,128]{1,0:T(8,128)(2,1)} %get-tuple-element.21.x_ref, bf16[128,128]{1,0:T(8,128)(2,1)} %get-tuple-element.22.u_ref, bf16[800,128]{1,0:T(8,128)(2,1)} %get-tuple-element.27.gp_ref, f32[512,128]{1,0:T(8,128)} %get-tuple-element.28.gs_ref, ...), custom_call_target="tpu_custom_call" | custom-call | flops 5000000000 | bytes 4000000 | tf_op jit(solution)/shard_map/outputs/pallas_call | solution.py:380
  75.7 0.0 collective-permute-done.16.refs_7_
  75.7 0.0 collective-permute-done.15.refs_6_
  75.7 0.6 copy-done.6
  76.3 0.1 copy-done.7
  76.4 0.1 copy-done.8
  76.4 0.6 copy-done.9
  77.1 3.4 %last.1 = (f32[27,96,96]{2,1,0:T(8,128)}, f32[27,96,96]{2,1,0:T(8,128)}, f32[1,96]{1,0:T(1,128)}) custom-call(bf16[496,128]{1,0:T(8,128)(2,1)} %copy-done, bf16[496,128]{1,0:T(8,128)(2,1)} %copy-done.5, bf16[496,128]{1,0:T(8,128)(2,1)} %copy-done.4, bf16[496,128]{1,0:T(8,128)(2,1)} %copy-done.3, bf16[496,128]{1,0:T(8,128)(2,1)} %copy-done.6, ...), custom_call_target="tpu_custom_call" | custom-call | tf_op jit(solution)/shard_map/last/pallas_call | solution.py:427
  (23 shorter events, 0.1 us)
Async XLA Ops:
  4.0 1.6 %collective-permute-start = (bf16[160,128]{1,0:T(8,128)(2,1)}, bf16[160,128]{1,0:T(8,128)(2,1)S(1)}, u32[]{:S(2)}, u32[]{:S(2)}) collective-permute-start(bf16[160,128]{1,0:T(8,128)(2,1)} %get-tuple-element.23), channel_id=1, source_target_pairs={{0,1},{1,0},{2,3},{3,2},{4,5},{5,4},{6,7},{7,6},{8,9},{9,8},{10,11... | collective-permute-start | bytes 122888 | tf_op jit(solution)/shard_map/ppermute | solution.py:343
  4.5 1.1 %collective-permute-start.1 = (bf16[160,128]{1,0:T(8,128)(2,1)}, bf16[160,128]{1,0:T(8,128)(2,1)S(1)}, u32[]{:S(2)}, u32[]{:S(2)}) collective-permute-start(bf16[160,128]{1,0:T(8,128)(2,1)} %get-tuple-element.24), channel_id=1, source_target_pairs={{1,2},{2,1},{5,6},{6,5},{9,10},{10,9},{13,14},{14,13},{17,18},{18,... | collective-permute-start | bytes 122888 | tf_op jit(solution)/shard_map/ppermute | solution.py:344
  5.6 0.6 copy-start.1
  5.6 0.6 copy-start.2
  7.9 5.2 %collective-permute-start.2 = (bf16[240,128]{1,0:T(8,128)(2,1)}, bf16[240,128]{1,0:T(8,128)(2,1)S(1)}, u32[]{:S(2)}, u32[]{:S(2)}) collective-permute-start(bf16[240,128]{1,0:T(8,128)(2,1)} %get-tuple-element.25), channel_id=1, source_target_pairs={{0,4},{4,0},{8,12},{12,8},{16,20},{20,16},{24,28},{28,24},{1,5},{5... | collective-permute-start | bytes 184328 | tf_op jit(solution)/shard_map/ppermute | solution.py:354
  10.7 2.4 %collective-permute-start.3 = (bf16[240,128]{1,0:T(8,128)(2,1)}, bf16[240,128]{1,0:T(8,128)(2,1)S(1)}, u32[]{:S(2)}, u32[]{:S(2)}) collective-permute-start(bf16[240,128]{1,0:T(8,128)(2,1)} %get-tuple-element.26), channel_id=1, source_target_pairs={{4,8},{12,16},{20,24},{8,4},{16,12},{24,20},{5,9},{13,17},{21,25},... | collective-permute-start | bytes 184328 | tf_op jit(solution)/shard_map/ppermute | solution.py:355
  13.1 0.6 copy-start.10
  13.7 0.6 copy-start.11
  28.7 5.5 %collective-permute-start.4 = (bf16[1984,128]{1,0:T(8,128)(2,1)}, bf16[1984,128]{1,0:T(8,128)(2,1)S(1)}, u32[]{:S(2)}, u32[]{:S(2)}) collective-permute-start(bf16[1984,128]{1,0:T(8,128)(2,1)} %get-tuple-element.33), channel_id=1, source_target_pairs={{0,1},{1,0},{2,3},{3,2},{4,5},{5,4},{6,7},{7,6},{8,9},{9,8},{10,11... | collective-permute-start | bytes 1523720 | tf_op jit(solution)/shard_map/ppermute | solution.py:398
  35.3 7.0 %collective-permute-start.5 = (bf16[496,128]{1,0:T(8,128)(2,1)S(1)}, bf16[496,128]{1,0:T(8,128)(2,1)S(1)}, u32[]{:S(2)}, u32[]{:S(2)}) collective-permute-start(bf16[496,128]{1,0:T(8,128)(2,1)S(1)} %get-tuple-element.37), channel_id=1, source_target_pairs={{0,2},{2,0},{4,6},{6,4},{8,10},{10,8},{12,14},{14,12},{16,18},{18,... | collective-permute-start | bytes 380936 | tf_op jit(solution)/shard_map/ppermute | solution.py:412
  38.1 7.5 %collective-permute-start.7 = (bf16[496,128]{1,0:T(8,128)(2,1)S(1)}, bf16[496,128]{1,0:T(8,128)(2,1)S(1)}, u32[]{:S(2)}, u32[]{:S(2)}) collective-permute-start(bf16[496,128]{1,0:T(8,128)(2,1)S(1)} %get-tuple-element.38), channel_id=1, source_target_pairs={{0,6},{2,4},{4,2},{6,0},{8,14},{10,12},{12,10},{14,8},{16,22},{18,... | collective-permute-start | bytes 380936 | tf_op jit(solution)/shard_map/ppermute | solution.py:412
  41.8 6.6 %collective-permute-start.6 = (bf16[496,128]{1,0:T(8,128)(2,1)S(1)}, bf16[496,128]{1,0:T(8,128)(2,1)S(1)}, u32[]{:S(2)}, u32[]{:S(2)}) collective-permute-start(bf16[496,128]{1,0:T(8,128)(2,1)S(1)} %get-tuple-element.39), channel_id=1, source_target_pairs={{0,4},{2,6},{4,0},{6,2},{8,12},{10,14},{12,8},{14,10},{16,20},{18,... | collective-permute-start | bytes 380936 | tf_op jit(solution)/shard_map/ppermute | solution.py:412
  49.4 5.6 %collective-permute-start.8 = (bf16[496,128]{1,0:T(8,128)(2,1)S(1)}, bf16[496,128]{1,0:T(8,128)(2,1)S(1)}, u32[]{:S(2)}, u32[]{:S(2)}) collective-permute-start(bf16[496,128]{1,0:T(8,128)(2,1)S(1)} %fusion.2), channel_id=1, source_target_pairs={{0,8},{4,12},{8,0},{12,4},{16,24},{20,28},{24,16},{28,20},{1,9},{5... | collective-permute-start | bytes 380936 | tf_op jit(solution)/shard_map/ppermute | solution.py:422
  55.1 7.5 %collective-permute-start.9 = (bf16[496,128]{1,0:T(8,128)(2,1)S(1)}, bf16[496,128]{1,0:T(8,128)(2,1)S(1)}, u32[]{:S(2)}, u32[]{:S(2)}) collective-permute-start(bf16[496,128]{1,0:T(8,128)(2,1)S(1)} %add_convert_fusion.1), channel_id=1, source_target_pairs={{0,16},{4,20},{8,24},{12,28},{16,0},{20,4},{24,8},{28,12},{1,17},{... | collective-permute-start | bytes 380936 | tf_op jit(solution)/shard_map/ppermute | solution.py:422
  62.6 13.0 %copy-start = (bf16[496,128]{1,0:T(8,128)(2,1)}, bf16[496,128]{1,0:T(8,128)(2,1)S(1)}, u32[]{:S(2)}) copy-start(bf16[496,128]{1,0:T(8,128)(2,1)S(1)} %add_convert_fusion.refs_0_) | copy-start | bytes 380932
  62.6 5.9 %collective-permute-start.12 = (bf16[496,128]{1,0:T(8,128)(2,1)S(1)}, bf16[496,128]{1,0:T(8,128)(2,1)S(1)}, u32[]{:S(2)}, u32[]{:S(2)}) collective-permute-start(bf16[496,128]{1,0:T(8,128)(2,1)S(1)} %add_convert_fusion.refs_0_), channel_id=1, source_target_pairs={{0,6},{2,4},{4,2},{6,0},{8,14},{10,12},{12,10},{14,8},{16,22},{18,... | collective-permute-start | bytes 380936 | tf_op jit(solution)/shard_map/ppermute | solution.py:412
  64.5 4.9 %collective-permute-start.11 = (bf16[496,128]{1,0:T(8,128)(2,1)S(1)}, bf16[496,128]{1,0:T(8,128)(2,1)S(1)}, u32[]{:S(2)}, u32[]{:S(2)}) collective-permute-start(bf16[496,128]{1,0:T(8,128)(2,1)S(1)} %add_convert_fusion.refs_0_), channel_id=1, source_target_pairs={{0,4},{2,6},{4,0},{6,2},{8,12},{10,14},{12,8},{14,10},{16,20},{18,... | collective-permute-start | bytes 380936 | tf_op jit(solution)/shard_map/ppermute | solution.py:412
  64.5 5.4 %collective-permute-start.10 = (bf16[496,128]{1,0:T(8,128)(2,1)S(1)}, bf16[496,128]{1,0:T(8,128)(2,1)S(1)}, u32[]{:S(2)}, u32[]{:S(2)}) collective-permute-start(bf16[496,128]{1,0:T(8,128)(2,1)S(1)} %add_convert_fusion.refs_0_), channel_id=1, source_target_pairs={{0,2},{2,0},{4,6},{6,4},{8,10},{10,8},{12,14},{14,12},{16,18},{18,... | collective-permute-start | bytes 380936 | tf_op jit(solution)/shard_map/ppermute | solution.py:412
  66.2 9.5 %collective-permute-start.13 = (bf16[496,128]{1,0:T(8,128)(2,1)S(1)}, bf16[496,128]{1,0:T(8,128)(2,1)S(1)}, u32[]{:S(2)}, u32[]{:S(2)}) collective-permute-start(bf16[496,128]{1,0:T(8,128)(2,1)S(1)} %add_convert_fusion.refs_0_), channel_id=1, source_target_pairs={{0,1},{1,0},{2,3},{3,2},{4,5},{5,4},{6,7},{7,6},{8,9},{9,8},{10,11... | collective-permute-start | bytes 380936 | tf_op jit(solution)/shard_map/ppermute | solution.py:425
  68.6 7.1 %copy-start.3 = (bf16[496,128]{1,0:T(8,128)(2,1)}, bf16[496,128]{1,0:T(8,128)(2,1)S(1)}, u32[]{:S(2)}) copy-start(bf16[496,128]{1,0:T(8,128)(2,1)S(1)} %collective-permute-done.12.refs_3_) | copy-start | bytes 380932
  68.6 7.1 %collective-permute-start.16 = (bf16[496,128]{1,0:T(8,128)(2,1)S(1)}, bf16[496,128]{1,0:T(8,128)(2,1)S(1)}, u32[]{:S(2)}, u32[]{:S(2)}) collective-permute-start(bf16[496,128]{1,0:T(8,128)(2,1)S(1)} %collective-permute-done.12.refs_3_), channel_id=1, source_target_pairs={{0,1},{1,0},{2,3},{3,2},{4,5},{5,4},{6,7},{7,6},{8,9},{9,8},{10,11... | collective-permute-start | bytes 380936 | tf_op jit(solution)/shard_map/ppermute | solution.py:425
  69.4 6.2 %copy-start.4 = (bf16[496,128]{1,0:T(8,128)(2,1)}, bf16[496,128]{1,0:T(8,128)(2,1)S(1)}, u32[]{:S(2)}) copy-start(bf16[496,128]{1,0:T(8,128)(2,1)S(1)} %collective-permute-done.11.refs_2_) | copy-start | bytes 380932
  69.4 6.3 %collective-permute-start.15 = (bf16[496,128]{1,0:T(8,128)(2,1)S(1)}, bf16[496,128]{1,0:T(8,128)(2,1)S(1)}, u32[]{:S(2)}, u32[]{:S(2)}) collective-permute-start(bf16[496,128]{1,0:T(8,128)(2,1)S(1)} %collective-permute-done.11.refs_2_), channel_id=1, source_target_pairs={{0,1},{1,0},{2,3},{3,2},{4,5},{5,4},{6,7},{7,6},{8,9},{9,8},{10,11... | collective-permute-start | bytes 380936 | tf_op jit(solution)/shard_map/ppermute | solution.py:425
  69.9 5.8 %copy-start.5 = (bf16[496,128]{1,0:T(8,128)(2,1)}, bf16[496,128]{1,0:T(8,128)(2,1)S(1)}, u32[]{:S(2)}) copy-start(bf16[496,128]{1,0:T(8,128)(2,1)S(1)} %collective-permute-done.10.refs_1_) | copy-start | bytes 380932
  69.9 5.8 %collective-permute-start.14 = (bf16[496,128]{1,0:T(8,128)(2,1)S(1)}, bf16[496,128]{1,0:T(8,128)(2,1)S(1)}, u32[]{:S(2)}, u32[]{:S(2)}) collective-permute-start(bf16[496,128]{1,0:T(8,128)(2,1)S(1)} %collective-permute-done.10.refs_1_), channel_id=1, source_target_pairs={{0,1},{1,0},{2,3},{3,2},{4,5},{5,4},{6,7},{7,6},{8,9},{9,8},{10,11... | collective-permute-start | bytes 380936 | tf_op jit(solution)/shard_map/ppermute | solution.py:425
  75.7 0.6 copy-start.6
  75.7 0.7 copy-start.7
  75.7 0.7 copy-start.8
  76.4 0.6 copy-start.9

commit v2 on v1

v2 whole, which is shorter than its diff:
```python
import functools
import math

import jax
import jax.numpy as jnp
from jax import lax
from jax.experimental import pallas as pl
from jax.experimental.pallas import tpu as pltpu
from jax.sharding import Mesh
from jax.sharding import PartitionSpec as P

LANES = 128
F32 = jnp.float32
BF16 = jnp.bfloat16
NT = (((1,), (1,)), ((), ()))
TN = (((0,), (0,)), ((), ()))
MIB = 1024 * 1024


def call(body, outs, args, scratch=(), cost=None, name=None, vmem=8, in_hbm=False, sems=()):
    in_place = pl.BlockSpec(memory_space=pltpu.VMEM)
    placed = pl.BlockSpec(memory_space=pl.ANY) if in_hbm else in_place
    return pl.pallas_call(
        body,
        out_shape=tuple(jax.ShapeDtypeStruct(s, d) for s, d in outs),
        in_specs=[in_place] * len(args),
        out_specs=tuple(placed for _ in outs),
        scratch_shapes=[pltpu.VMEM(s, d) for s, d in scratch] + list(sems),
        compiler_params=pltpu.CompilerParams(vmem_limit_bytes=vmem * MIB),
        cost_estimate=cost,
        name=name,
    )(*args)


def lane_of(shape):
    return lax.broadcasted_iota(jnp.int32, shape, len(shape) - 1)


def z_of(shape):
    return lax.broadcasted_iota(jnp.int32, shape, len(shape) - 2)


def below(v):
    return jnp.where(z_of(v.shape) == 0, 0.0, pltpu.roll(v, 1, axis=1))


def above(v):
    top = v.shape[1] - 1
    return jnp.where(z_of(v.shape) == top, 0.0, pltpu.roll(v, top, axis=1))


def first_kernel(dims, vox_ref, occ_ref, cot_ref, x_ref, u_ref, core_ref, side_ref, xs, us):
    tx, ty, tz, ch = dims
    hx, hy = tx // 2, ty // 2
    occ = jnp.broadcast_to(occ_ref[...].astype(F32)[:, :, None], (tx * ty, tz, LANES))
    xs[...] = jnp.zeros(xs.shape, F32)
    xs[:, :ch] = vox_ref[...].astype(F32)
    x = xs[...].reshape(tx * ty, tz, LANES)
    x = jnp.where(lane_of(x.shape) == ch, 1.0, x) * occ
    xs[...] = x.reshape(xs.shape)
    x_ref[...] = xs[...].astype(BF16)
    pairs = occ.reshape(hx, 2, hy, 2, tz, LANES)
    pairs = jnp.maximum(pairs[:, 0], pairs[:, 1])
    pairs = jnp.maximum(pairs[:, :, 0], pairs[:, :, 1]).reshape(hx * hy, tz, LANES)
    coarse = jnp.maximum(pairs, pltpu.roll(pairs, tz - 1, axis=1))
    us[...] = jnp.zeros(us.shape, F32)
    cot = jnp.concatenate(
        [cot_ref[...].astype(F32), jnp.zeros((hx * hy * tz // 2, LANES - ch), F32)], axis=1
    )
    us[pl.ds(0, hx * hy * tz // 2, stride=2), :] = cot
    u = us[...].reshape(hx * hy, tz, LANES)
    even = lax.rem(z_of(u.shape), 2) == 0
    u = jnp.where((lane_of(u.shape) == ch) & even, 1.0, u) * coarse
    us[...] = u.reshape(us.shape)
    u_ref[...] = us[...].astype(BF16)
    core = lax.axis_index("core")
    x4, u4 = xs.reshape(tx, ty, tz, LANES), us.reshape(hx, hy, tz, LANES)
    rows = tx * 2 * tz
    for ref, low in ((core_ref, core), (side_ref, 1 - core)):
        start = (1 - low) * (ty - 2)
        ref[:rows] = x4[:, pl.ds(start, 2)].reshape(rows, LANES).astype(BF16)
        ref[rows:] = (
            u4[:, pl.ds((1 - low) * (hy - 1), 1)].reshape(hx * tz, LANES).astype(BF16)
        )


def second_kernel(dims, x_ref, u_ref, core_ref, side_ref, near_ref, far_ref, xe, ue):
    tx, ty, tz, _ = dims
    widen(dims, x_ref, u_ref, core_ref, side_ref, xe, ue, 0, 0)
    odd = lax.rem(lax.axis_index("gx"), 2)
    rows = 2 * (ty + 4) * tz
    hx, hy = tx // 2, ty // 2
    for ref, low in ((near_ref, odd), (far_ref, 1 - odd)):
        ref[:rows] = xe[pl.ds((1 - low) * (tx - 2), 2)].reshape(rows, LANES).astype(BF16)
        ref[rows:] = (
            ue[pl.ds((1 - low) * (hx - 1), 1)].reshape((hy + 2) * tz, LANES).astype(BF16)
        )


def widen(dims, x_ref, u_ref, core_ref, side_ref, xe, ue, x0, u0):
    tx, ty, tz, _ = dims
    hx, hy = tx // 2, ty // 2
    rows = tx * 2 * tz
    core = lax.axis_index("core")
    xe[x0 : x0 + tx, 2 : 2 + ty] = x_ref[...].astype(F32).reshape(tx, ty, tz, LANES)
    ue[u0 : u0 + hx, 1 : 1 + hy] = u_ref[...].astype(F32).reshape(hx, hy, tz, LANES)
    for ref, low in ((core_ref, core), (side_ref, 1 - core)):
        xe[x0 : x0 + tx, pl.ds((1 - low) * (ty + 2), 2)] = (
            ref[:rows].astype(F32).reshape(tx, 2, tz, LANES)
        )
        ue[u0 : u0 + hx, pl.ds((1 - low) * (hy + 1), 1)] = (
            ref[rows:].astype(F32).reshape(hx, 1, tz, LANES)
        )


def taps_in_rows(ch, w_ref, out):
    out[...] = jnp.zeros(out.shape, BF16)
    for t in range(w_ref.shape[0]):
        out[t // 3, (t % 3) * LANES : (t % 3) * LANES + ch, :ch] = w_ref[t]


def taps_in_lanes(ch, w_ref, out):
    out[...] = jnp.zeros(out.shape, BF16)
    for t in range(w_ref.shape[0]):
        at, lane = t // 3 * LANES, t % 3 * LANES
        out[at : at + ch, lane : lane + ch] = w_ref[t]


def three(v):
    return v[:, :, :LANES], v[:, :, LANES : 2 * LANES], v[:, :, 2 * LANES :]


def pack_block(block, ch):
    free = LANES - ch
    keep = ch * ch // LANES
    tail = block[keep:ch]
    parts = [
        pltpu.roll(tail, (LANES - free - p * free) % LANES, axis=1) for p in range(ch // free)
    ]
    parts = jnp.concatenate(parts, axis=0)
    main = block[:keep]
    return jnp.where(lane_of(main.shape) < ch, main, parts)


def unpack_block(packed, ch):
    free = LANES - ch
    keep = ch * ch // LANES
    tall = ch - keep
    lane = lane_of((tall, LANES))
    tail = None
    for p in range(ch // free):
        part = packed[p * tall : (p + 1) * tall]
        part = pltpu.roll(part, (free + p * free) % LANES, axis=1)
        tail = part if tail is None else jnp.where(lane < p * free, tail, part)
    return jnp.concatenate([packed, tail], axis=0)


def main_kernel(
    dims, x_ref, u_ref, core_ref, side_ref, near_ref, far_ref, cw_ref, dw_ref, bias_ref,
    keep_ref, send_ref, gp_ref, gs_ref, s_ref,
    xe, ue, ss, acc, gsr, gp, wf, wd, pack, bias,
):
    tx, ty, tz, ch = dims
    hx, hy = tx // 2, ty // 2
    ex, ey = tx + 2, ty + 2
    block_rows = ch * ch // LANES
    core = lax.axis_index("core")
    odd = lax.rem(lax.axis_index("gx"), 2)
    taps_in_lanes(ch, cw_ref, wf)
    taps_in_rows(ch, dw_ref, wd)
    bias[...] = jnp.zeros(bias.shape, F32)
    bias[:, :ch] = bias_ref[...]
    widen(dims, x_ref, u_ref, core_ref, side_ref, xe, ue, 2, 1)
    rows = 2 * (ty + 4) * tz
    for ref, low in ((near_ref, odd), (far_ref, 1 - odd)):
        xe[pl.ds((1 - low) * (tx + 2), 2)] = ref[:rows].astype(F32).reshape(2, ty + 4, tz, LANES)
        ue[pl.ds((1 - low) * (hx + 1), 1)] = ref[rows:].astype(F32).reshape(1, hy + 2, tz, LANES)

    part = ex // 2

    def forward(h, _):
        wins = [
            xe[pl.ds(h * part + a, part), b : b + ey].reshape(part * ey * tz, LANES).astype(BF16)
            for a in range(3)
            for b in range(3)
        ]
        out = jnp.dot(jnp.concatenate(wins, axis=1), wf[...], preferred_element_type=F32)
        lower, same, upper = three(out.reshape(part * ey, tz, 3 * LANES))
        out = below(lower) + same + above(upper)
        acc[pl.ds(h * part, part)] = out.reshape(part, ey, tz, LANES)
        return 0

    lax.fori_loop(0, 2, forward, 0)

    terms = {0: ((2, 0), (0, 1)), 1: ((1, 1),)}
    for px in (0, 1):
        for py in (0, 1):
            wins, taps = [], []
            for a, sx in terms[px]:
                for b, sy in terms[py]:
                    win = ue[sx : sx + hx + 1, sy : sy + hy + 1]
                    wins.append(win.reshape((hx + 1) * (hy + 1) * tz, LANES).astype(BF16))
                    taps.append(wd[a * 3 + b])
            out = lax.dot_general(
                jnp.concatenate(wins, axis=1), jnp.concatenate(taps, axis=1), NT,
                preferred_element_type=F32,
            )
            lower, same, upper = three(out.reshape((hx + 1) * (hy + 1), tz, 3 * LANES))
            out = above(lower) + same + below(upper)
            gsr[:, px, :, py] = out.reshape(hx + 1, hy + 1, tz, LANES)

    def pointwise(i, _):
        v = acc[i] + bias[...].reshape(1, 1, LANES)
        x = xe[i + 1, 1 : 1 + ey]
        live = jnp.broadcast_to(x[:, :, ch : ch + 1], x.shape)
        s = 1.0 / (1.0 + jnp.exp(-v))
        summed = (x + live * (v * s)).astype(BF16).astype(F32)
        ss[i // 2, lax.rem(i, 2)] = summed.reshape(hy + 1, 2, tz, LANES)
        g = gsr[i // 2, lax.rem(i, 2)].reshape(ey, tz, LANES)
        gp[i] = (g * live * s * (1.0 + v * (1.0 - s))).astype(BF16).astype(F32)
        return 0

    lax.fori_loop(0, ex, pointwise, 0)

    def gradients(h, wins, other):
        cells = other.shape[0] * other.shape[1]
        other = jnp.concatenate([above(other), other, below(other)], axis=2)
        other = other.reshape(cells, 3 * LANES).astype(BF16)
        for a in range(3):
            win = jnp.concatenate([wins(a, b) for b in range(3)], axis=1)
            out = lax.dot_general(win, other, TN, preferred_element_type=F32)
            for b in range(3):
                for e in range(3):
                    at = (a * 9 + b * 3 + e) * block_rows
                    block = out[b * LANES : b * LANES + ch, e * LANES : (e + 1) * LANES]
                    pack[h, at : at + block_rows] = pack_block(block, ch)
            if a == 1:
                at = 27 * block_rows
                pack[h, at : at + 8] = out[LANES + ch : LANES + ch + 8, LANES : 2 * LANES]
        at = 27 * block_rows + 8
        pack[h, at:] = jnp.zeros((pack.shape[1] - at, LANES), F32)

    def fine_window(a, b):
        win = xe[a + 1 : a + 1 + tx, b + 1 : b + 1 + ty]
        if a == 1 and b == 1:
            win = jnp.where(lane_of(win.shape) == ch + 1, 1.0, win)
        return win.reshape(tx * ty * tz, LANES).astype(BF16)

    def coarse_window(a, b):
        win = ss[a // 2 : a // 2 + hx, a % 2, b // 2 : b // 2 + hy, b % 2]
        return win.reshape(hx * hy * tz, LANES).astype(BF16)

    gradients(0, fine_window, gp[1 : 1 + tx, 1 : 1 + ty].reshape(tx * ty, tz, LANES))
    gradients(1, coarse_window, ue[1 : 1 + hx, 1 : 1 + hy].reshape(hx * hy, tz, LANES))
    keep_ref[...] = pack[core]
    send_ref[...] = pack[1 - core].astype(BF16)
    gp_ref[...] = gp[...].reshape(ex * ey * tz, LANES).astype(BF16)
    gs_ref[...] = gsr[...].reshape(ex, ey, tz, LANES)[1 : 1 + tx, 1 : 1 + ty].reshape(
        tx * ty * tz, LANES
    )
    s_ref[...] = ss[...].reshape(ex * ey * tz, LANES).astype(BF16)


def second_outputs(
    dims, x_ref, u_ref, gp_ref, gs_ref, s_ref, cw_ref, dw_ref, down_ref, gv_ref,
    ge, ss, accd, wf, wd,
):
    tx, ty, tz, ch = dims
    hx, hy = tx // 2, ty // 2
    ex, ey = tx + 2, ty + 2
    taps_in_rows(ch, cw_ref, wf)
    taps_in_lanes(ch, dw_ref, wd)
    ge[...] = gp_ref[...].astype(F32).reshape(ex, ey, tz, LANES)
    ss[...] = s_ref[...].astype(F32).reshape(hx + 1, 2, hy + 1, 2, tz, LANES)
    wins = [
        ss[a // 2 : a // 2 + hx, a % 2, b // 2 : b // 2 + hy, b % 2]
        .reshape(hx * hy * tz, LANES)
        .astype(BF16)
        for a in range(3)
        for b in range(3)
    ]
    out = jnp.dot(jnp.concatenate(wins, axis=1), wd[...], preferred_element_type=F32)
    lower, same, upper = three(out.reshape(hx * hy, tz, 3 * LANES))
    out = (below(lower) + same + above(upper)).reshape(hx * hy * tz, LANES)
    u = u_ref[...].astype(F32)
    accd[...] = out * jnp.broadcast_to(u[:, ch : ch + 1], u.shape)
    down_ref[...] = accd[pl.ds(0, hx * hy * tz // 2, stride=2), :][:, :ch].astype(BF16)

    wins = [
        ge[2 - a : 2 - a + tx, 2 - b : 2 - b + ty].reshape(tx * ty * tz, LANES).astype(BF16)
        for a in range(3)
        for b in range(3)
    ]
    taps = jnp.concatenate([wf[ab] for ab in range(9)], axis=1)
    out = lax.dot_general(
        jnp.concatenate(wins, axis=1), taps, NT, preferred_element_type=F32
    )
    lower, same, upper = three(out.reshape(tx * ty, tz, 3 * LANES))
    out = (above(lower) + same + below(upper)).reshape(tx * ty * tz, LANES)
    x = x_ref[...].astype(F32)
    live = jnp.broadcast_to(x[:, ch : ch + 1], x.shape)
    gv_ref[...] = ((gs_ref[...] + out) * live)[:, :ch].astype(BF16)


def last_kernel(ch, factor, *refs):
    own, other = refs[:4], refs[4:8]
    conv_ref, down_ref, bias_ref, full, conv_out, down_out, bias_out, sems = refs[8:]
    core = lax.axis_index("core")
    me = lax.rem(lax.axis_index("gx"), 2) * 2 + lax.rem(lax.axis_index("gyc"), 2)
    rows = own[0].shape[0]
    block_rows = ch * ch // LANES
    for k in range(4):
        at = pl.ds(pl.multiple_of((me ^ k) * rows, 16), rows)
        full[core, at] = own[k][...].astype(F32) * factor
        full[1 - core, at] = other[k][...].astype(F32) * factor
    bias_out[...] = full[0, 27 * block_rows + 1 : 27 * block_rows + 2, :ch]
    copies = [pltpu.make_async_copy(bias_out, bias_ref, sems.at[0])]
    copies[0].start()
    for h, ref, out in ((0, conv_ref, conv_out), (1, down_ref, down_out)):
        for a in range(3):
            for t in range(a * 9, a * 9 + 9):
                block = unpack_block(full[h, t * block_rows : (t + 1) * block_rows], ch)
                out[t] = block[:, :ch]
            part = pl.ds(a * 9, 9)
            copy = pltpu.make_async_copy(out.at[part], ref.at[part], sems.at[1 + h * 3 + a])
            copy.start()
            copies.append(copy)
    for copy in copies:
        copy.wait()


def on_device(voxels, occupancy, conv_weight, conv_bias, down_weight, down_cotangent):
    tx, ty, tz, ch = voxels.shape
    hx, hy, hz = tx // 2, ty // 2, tz // 2
    ex, ey = tx + 2, ty + 2
    dims = (tx, ty, tz, ch)
    n_gx, n_gyc = lax.axis_size("gx"), lax.axis_size("gyc")
    fine, coarse = tx * ty * tz, hx * hy * tz

    side_rows = tx * 2 * tz + hx * tz
    row_rows = 2 * (ty + 4) * tz + (hy + 2) * tz
    x, u, to_core, to_side = call(
        functools.partial(first_kernel, dims),
        [((fine, LANES), BF16), ((coarse, LANES), BF16)] + [((side_rows, LANES), BF16)] * 2,
        (
            voxels.reshape(fine, ch),
            occupancy.reshape(tx * ty, tz),
            down_cotangent.reshape(hx * hy * hz, ch),
        ),
        [((fine, LANES), F32), ((coarse, LANES), F32)],
        name="first",
        vmem=4,
    )
    swap = [(0, 1), (1, 0)]
    n_gy = n_gyc * 2
    sides = [(i, i + 1) for i in range(1, n_gy - 1, 2)]
    sides += [(j, i) for i, j in sides]
    from_core = lax.ppermute(to_core, "core", swap)
    from_side = lax.ppermute(to_side, ("gyc", "core"), sides)
    to_near, to_far = call(
        functools.partial(second_kernel, dims),
        [((row_rows, LANES), BF16)] * 2,
        (x, u, from_core, from_side),
        [((tx, ty + 4, tz, LANES), F32), ((hx, hy + 2, tz, LANES), F32)],
        name="second",
        vmem=4,
    )
    near = [(i, i ^ 1) for i in range(n_gx)]
    far = [(i, i + 1) for i in range(1, n_gx - 1, 2)]
    far += [(j, i) for i, j in far]
    from_near = lax.ppermute(to_near, "gx", near)
    from_far = lax.ppermute(to_far, "gx", far)

    block_rows = ch * ch // LANES
    half_rows = -(-(27 * block_rows + 8) // 64) * 64
    keep, send, gp, gs, s = call(
        functools.partial(main_kernel, dims),
        [((half_rows, LANES), F32), ((half_rows, LANES), BF16)]
        + [((ex * ey * tz, LANES), BF16), ((fine, LANES), F32), ((ex * ey * tz, LANES), BF16)],
        (
            x, u, from_core, from_side, from_near, from_far, conv_weight, down_weight,
            conv_bias.reshape(1, ch),
        ),
        [
            ((tx + 4, ty + 4, tz, LANES), F32),
            ((hx + 2, hy + 2, tz, LANES), F32),
            ((hx + 1, 2, hy + 1, 2, tz, LANES), F32),
            ((ex, ey, tz, LANES), F32),
            ((hx + 1, 2, hy + 1, 2, tz, LANES), F32),
            ((ex, ey, tz, LANES), F32),
            ((9 * LANES, 3 * LANES), BF16),
            ((9, 3 * LANES, LANES), BF16),
            ((2, half_rows, LANES), F32),
            ((1, LANES), F32),
        ],
        name="main",
        vmem=24,
    )

    down, grad_voxels = call(
        functools.partial(second_outputs, dims),
        [((hx * hy * hz, ch), BF16), ((fine, ch), BF16)],
        (x, u, gp, gs, s, conv_weight, down_weight),
        [
            ((ex, ey, tz, LANES), F32),
            ((hx + 1, 2, hy + 1, 2, tz, LANES), F32),
            ((coarse, LANES), F32),
            ((9, 3 * LANES, LANES), BF16),
            ((9 * LANES, 3 * LANES), BF16),
        ],
        cost=pl.CostEstimate(flops=5_000_000_000, bytes_accessed=4_000_000, transcendentals=0),
        name="outputs",
        vmem=24,
    )

    def plus(a, b):
        return (a.astype(F32) + b.astype(F32)).astype(BF16)

    got = lax.ppermute(send, "core", swap)
    me = lax.rem(lax.axis_index("gx"), 2) * 2 + lax.rem(lax.axis_index("gyc"), 2)
    quarter = half_rows // 4
    keep4, got4 = keep.reshape(4, quarter, LANES), got.reshape(4, quarter, LANES)

    def quarter_of(k):
        pick = functools.partial(lax.dynamic_index_in_dim, index=me ^ k, axis=0, keepdims=False)
        return pick(keep4).astype(F32) + pick(got4).astype(F32)

    def across(value, k):
        route = []
        for i in range(n_gx):
            for j in range(n_gyc):
                route.append((i * n_gyc + j, (i ^ (k >> 1)) * n_gyc + (j ^ (k & 1))))
        return lax.ppermute(value, ("gx", "gyc"), route)

    arrived = [across(quarter_of(k).astype(BF16), k) for k in (1, 2, 3)]
    *arrived, down, grad_voxels = lax.optimization_barrier((*arrived, down, grad_voxels))
    total = quarter_of(0)
    for piece in arrived:
        total = total + piece.astype(F32)
    total = total.astype(BF16)
    for axis, peers in (("gx", n_gx), ("gyc", n_gyc)):
        step = 2
        while step < peers:
            total = plus(total, lax.ppermute(total, axis, [(i, i ^ step) for i in range(peers)]))
            step *= 2
    own = [total] + [across(total, k) for k in (1, 2, 3)]
    other = [lax.ppermute(piece, "core", swap) for piece in own]
    factor = 1.0 / math.sqrt(tx * n_gx * ty * n_gy * tz)
    grad_conv, grad_down, grad_bias = call(
        functools.partial(last_kernel, ch, factor),
        [((27, ch, ch), F32), ((27, ch, ch), F32), ((1, ch), F32)],
        (*own, *other),
        [
            ((2, half_rows, LANES), F32),
            ((27, ch, ch), F32),
            ((27, ch, ch), F32),
            ((1, ch), F32),
        ],
        name="last",
        vmem=12,
        in_hbm=True,
        sems=[pltpu.SemaphoreType.DMA((7,))],
    )
    return (
        down.reshape(hx, hy, hz, ch),
        grad_voxels.reshape(tx, ty, tz, ch),
        grad_conv,
        grad_bias.reshape(ch),
        grad_down,
    )


def solution(mesh):
    n_gx, n_gy = mesh.shape["gx"], mesh.shape["gy"]
    split = Mesh(mesh.devices.reshape(n_gx, n_gy // 2, 2), ("gx", "gyc", "core"))
    gy = ("gyc", "core")
    placed = (
        P("gx", gy, None, None),
        P("gx", gy, None),
        P(),
        P(),
        P(),
        P("gx", gy, None, None),
    )
    return jax.shard_map(
        on_device,
        mesh=split,
        in_specs=placed,
        out_specs=(P("gx", gy, None, None), P("gx", gy, None, None), P(), P(), P()),
        check_vma=False,
    )
```

time: 81 us -> 65.8 us (0.81)
  Pallas kernels: 26.8 us -> 8.64 us
  starting transfers between devices: 24.8 us -> 27.3 us
  other arithmetic: 2.98 us -> 2.17 us
    pallas_call x5, Pallas kernels: 26.8 us -> 8.64 us  [call(): pl.pallas_call(body, out_shape=tuple((jax.ShapeDtypeStruct(s, d) for s, d...]
    unnamed x24 -> x20, local copies, waits for them, and re-layouts: 3.22 us -> 5.89 us
    ppermute x6, starting transfers between devices: 10.6 us -> 12.3 us  [across(): return lax.ppermute(value, ('gx', 'gyc'), route)]
    reshape x1 -> x0, local copies, waits for them, and re-layouts: 1.17 us -> none  [on_device(): bias = jnp.pad(conv_bias, (0, LANES - ch)).reshape(1, LANES)]
    ppermute x4, waiting for transfers between devices: 0.01 us -> 1.01 us  [on_device(): other = [lax.ppermute(piece, 'core', swap) for piece in own]]
    ppermute x1, waiting for transfers between devices: 0.58 us -> 1.54 us  [on_device(): from_near = lax.ppermute(to_near, 'gx', near)]
    broadcast_in_dim x2 -> x0, local copies, waits for them, and re-layouts: 0.9 us -> none  [on_device(): jnp.broadcast_to(occupancy.astype(BF16)[..., None], (tx, ty, tz, LANES))]
    ppermute x6, waiting for transfers between devices: 9.82 us -> 8.98 us  [across(): return lax.ppermute(value, ('gx', 'gyc'), route)]
  transfers between devices with their start and end apart: 17 -> 17, of which waited for: 10 -> 12; matrix products, arithmetic and copies ran while one was open for 1% -> 0% of each run, Pallas kernels for 7% -> 3%
where the time goes in v2:
time: 65.8 us; the launch traced here: 65.4 us
  starting transfers between devices  27.3 us (41%)
  waiting for transfers between devices  20.7 us (31%)
  Pallas kernels  8.64 us (13%)
  local copies, waits for them, and re-layouts  5.89 us (9%)
  other arithmetic  2.17 us (3%)
  between operations  0.72 us (1%)
    ppermute x6, starting transfers between devices, across(): return lax.ppermute(value, ('gx', 'gyc'), route)  12.3 us
    ppermute x6, waiting for transfers between devices, across(): return lax.ppermute(value, ('gx', 'gyc'), route)  8.98 us
    pallas_call x5, Pallas kernels, call(): pl.pallas_call(body, out_shape=tuple((jax.ShapeDtypeStruct(s, d) for s, d...  8.64 us
    ppermute x2, waiting for transfers between devices, on_device(): lax.ppermute(total, axis, [(i, i ^ step) for i in range(peers)])  7.33 us
    ppermute x2, starting transfers between devices, on_device(): lax.ppermute(total, axis, [(i, i ^ step) for i in range(peers)])  5.96 us
    unnamed x20, local copies, waits for them, and re-layouts  5.89 us
    ppermute x1, starting transfers between devices, on_device(): got = lax.ppermute(send, 'core', swap)  3.72 us
    ppermute x1, starting transfers between devices, on_device(): from_near = lax.ppermute(to_near, 'gx', near)  2.89 us
  transfers between devices with their start and end apart: 17, of which 12 were waited for; matrix products, arithmetic and copies ran while one was open for 0% of the time, Pallas kernels for 3%

profile of v2, /device:TPU:0, one launch (start us, length us, event | category | flops | bytes accessed | tf_op | source)
XLA Modules:
  0.0 65.4 jit_solution(2921606989066802709)
XLA Ops:
  0.6 0.9 %copy-done.4 = bf16[8,8,8,96]{3,2,1,0:T(8,128)(2,1)S(1)} copy-done((bf16[8,8,8,96]{3,2,1,0:T(8,128)(2,1)S(1)}, bf16[8,8,8,96]{3,2,1,0:T(8,128)(2,1)}, u32[]{:S(2)}) %copy-start.4) | copy-done | bytes 98328
  1.5 0.8 %copy-done.5 = s32[8,8,8]{2,1,0:T(8,128)S(1)} copy-done((s32[8,8,8]{2,1,0:T(8,128)S(1)}, s32[8,8,8]{2,1,0:T(8,128)}, u32[]{:S(2)}) %copy-start.5) | copy-done | bytes 2072
  2.3 0.7 %copy-done.6 = bf16[4,4,4,96]{3,2,1,0:T(4,128)(2,1)S(1)} copy-done((bf16[4,4,4,96]{3,2,1,0:T(4,128)(2,1)S(1)}, bf16[4,4,4,96]{3,2,1,0:T(4,128)(2,1)}, u32[]{:S(2)}) %copy-start.6) | copy-done | bytes 12312
  3.0 0.2 first.1
  3.2 0.6 collective-permute-start
  3.7 0.7 collective-permute-start.1
  4.4 0.2 collective-permute-done.core_ref
  4.6 0.0 collective-permute-done.1.side_ref
  4.7 2.9 %collective-permute-start.2 = (bf16[240,128]{1,0:T(8,128)(2,1)S(1)}, bf16[240,128]{1,0:T(8,128)(2,1)S(1)}, u32[]{:S(2)}, u32[]{:S(2)}) collective-permute-start(bf16[240,128]{1,0:T(8,128)(2,1)S(1)} %get-tuple-element.30), channel_id=1, source_target_pairs={{0,4},{4,0},{8,12},{12,8},{16,20},{20,16},{24,28},{28,24},{1,5},{5... | collective-permute-start | bytes 184328 | tf_op jit(solution)/shard_map/ppermute | solution.py:371
  7.5 0.7 collective-permute-start.3
  8.2 1.5 %collective-permute-done.2.near_ref = bf16[240,128]{1,0:T(8,128)(2,1)S(1)} collective-permute-done((bf16[240,128]{1,0:T(8,128)(2,1)S(1)}, bf16[240,128]{1,0:T(8,128)(2,1)S(1)}, u32[]{:S(2)}, u32[]{:S(2)}) %collective-permute-start.2) | collective-permute-done | bytes 61472 | tf_op jit(solution)/shard_map/ppermute | solution.py:371
  9.7 0.0 collective-permute-done.3.far_ref
  9.8 1.1 %copy-done = bf16[27,96,96]{2,1,0:T(8,128)(2,1)S(1)} copy-done((bf16[27,96,96]{2,1,0:T(8,128)(2,1)S(1)}, bf16[27,96,96]{2,1,0:T(8,128)(2,1)}, u32[]{:S(2)}) %copy-start) | copy-done | bytes 497688
  10.8 1.1 %copy-done.2 = bf16[27,96,96]{2,1,0:T(8,128)(2,1)S(1)} copy-done((bf16[27,96,96]{2,1,0:T(8,128)(2,1)S(1)}, bf16[27,96,96]{2,1,0:T(8,128)(2,1)}, u32[]{:S(2)}) %copy-start.2) | copy-done | bytes 497688
  11.9 0.7 copy-done.7
  12.6 4.7 %main.1 = (f32[1984,128]{1,0:T(8,128)S(1)}, bf16[1984,128]{1,0:T(8,128)(2,1)S(1)}, bf16[800,128]{1,0:T(8,128)(2,1)S(1)}, f32[512,128]{1,0:T(8,128)S(1)}, bf16[800,128]{1,0:T(8,128)(2,1)S(1)}) custom-call(bf16[512,128]{1,0:T(8,128)(2,1)S(1)} %get-tuple-element.26.x_ref, bf16[128,128]{1,0:T(8,128)(2,1)S(1)} %get-tuple-element.27.u_ref, ...), custom_call_target="tpu_custom_call" | custom-call | tf_op jit(solution)/shard_map/main/pallas_call | solution.py:23
  17.3 0.0 copy-start.8
  17.3 0.7 %copy-done.8 = bf16[800,128]{1,0:T(8,128)(2,1)} copy-done((bf16[800,128]{1,0:T(8,128)(2,1)}, bf16[800,128]{1,0:T(8,128)(2,1)S(1)}, u32[]{:S(2)}) %copy-start.8) | copy-done | bytes 204824
  17.9 3.7 %collective-permute-start.4 = (bf16[1984,128]{1,0:T(8,128)(2,1)S(1)}, bf16[1984,128]{1,0:T(8,128)(2,1)}, u32[]{:S(2)}, u32[]{:S(2)}) collective-permute-start(bf16[1984,128]{1,0:T(8,128)(2,1)S(1)} %get-tuple-element.33), channel_id=1, source_target_pairs={{0,1},{1,0},{2,3},{3,2},{4,5},{5,4},{6,7},{7,6},{8,9},{9,8},{10,11... | collective-permute-start | bytes 1523720 | tf_op jit(solution)/shard_map/ppermute | solution.py:419
  21.7 1.6 %collective-permute-done.4 = bf16[1984,128]{1,0:T(8,128)(2,1)} collective-permute-done((bf16[1984,128]{1,0:T(8,128)(2,1)S(1)}, bf16[1984,128]{1,0:T(8,128)(2,1)}, u32[]{:S(2)}, u32[]{:S(2)}) %collective-permute-start.4) | collective-permute-done | bytes 507936 | tf_op jit(solution)/shard_map/ppermute | solution.py:419
  23.3 1.1 %fusion.5 = (bf16[496,128]{1,0:T(8,128)(2,1)S(1)}, bf16[496,128]{1,0:T(8,128)(2,1)S(1)}, bf16[496,128]{1,0:T(8,128)(2,1)S(1)}) fusion(f32[4,496,128]{2,1,0:T(8,128)S(1)} %bitcast.23, s32[]{:T(128)S(6)} %select_n.20, bf16[4,496,128]{2,1,0:T(8,128)(2,1)} %bitcast.5, s32[]{:T(128)S(6)} %select_n.19, s32[]{:T(128)S(6)} %select_n.18), kind=kLoop, calls=%fused_computation.11 | loop fusion | flops 571392 | bytes 1523724 | tf_op jit(solution)/shard_map/convert_element_type | solution.py:435
  24.4 7.1 %collective-permute-start.7 = (bf16[496,128]{1,0:T(8,128)(2,1)S(1)}, bf16[496,128]{1,0:T(8,128)(2,1)S(1)}, u32[]{:S(2)}, u32[]{:S(2)}) collective-permute-start(bf16[496,128]{1,0:T(8,128)(2,1)S(1)} %get-tuple-element.47), channel_id=1, source_target_pairs={{0,6},{2,4},{4,2},{6,0},{8,14},{10,12},{12,10},{14,8},{16,22},{18,... | collective-permute-start | bytes 380936 | tf_op jit(solution)/shard_map/ppermute | solution.py:433
  31.5 0.0 collective-permute-start.6
  31.5 0.6 collective-permute-start.5
  32.2 1.9 %outputs.1 = (bf16[64,96]{1,0:T(8,128)(2,1)}, bf16[512,96]{1,0:T(8,128)(2,1)}) custom-call(bf16[512,128]{1,0:T(8,128)(2,1)S(1)} %get-tuple-element.26.x_ref, bf16[128,128]{1,0:T(8,128)(2,1)S(1)} %get-tuple-element.27.u_ref, bf16[800,128]{1,0:T(8,128)(2,1)S(1)} %get-tuple-element.34.gp_ref, f32[512,128]{1,0:T(8,128)S(1)} %get-tuple-element.35.gs_ref, ...), custom_call_target="tpu_custom_call" | custom-call | flops 5000000000 | bytes 4000000 | tf_op jit(solution)/shard_map/outputs/pallas_call | solution.py:23
  34.1 1.7 %collective-permute-done.7 = bf16[496,128]{1,0:T(8,128)(2,1)S(1)} collective-permute-done((bf16[496,128]{1,0:T(8,128)(2,1)S(1)}, bf16[496,128]{1,0:T(8,128)(2,1)S(1)}, u32[]{:S(2)}, u32[]{:S(2)}) %collective-permute-start.7) | collective-permute-done | bytes 127008 | tf_op jit(solution)/shard_map/ppermute | solution.py:433
  35.8 1.4 %collective-permute-done.6 = bf16[496,128]{1,0:T(8,128)(2,1)S(1)} collective-permute-done((bf16[496,128]{1,0:T(8,128)(2,1)S(1)}, bf16[496,128]{1,0:T(8,128)(2,1)S(1)}, u32[]{:S(2)}, u32[]{:S(2)}) %collective-permute-start.6) | collective-permute-done | bytes 127008 | tf_op jit(solution)/shard_map/ppermute | solution.py:433
  37.2 0.7 %collective-permute-done.5 = bf16[496,128]{1,0:T(8,128)(2,1)S(1)} collective-permute-done((bf16[496,128]{1,0:T(8,128)(2,1)S(1)}, bf16[496,128]{1,0:T(8,128)(2,1)S(1)}, u32[]{:S(2)}, u32[]{:S(2)}) %collective-permute-start.5) | collective-permute-done | bytes 127008 | tf_op jit(solution)/shard_map/ppermute | solution.py:433
  38.0 1.0 %fusion.2 = bf16[496,128]{1,0:T(8,128)(2,1)S(1)} fusion(bf16[496,128]{1,0:T(8,128)(2,1)S(1)} %collective-permute-done.7, bf16[496,128]{1,0:T(8,128)(2,1)S(1)} %collective-permute-done.6, bf16[496,128]{1,0:T(8,128)(2,1)S(1)} %collective-permute-done.5, f32[4,496,128]{2,1,0:T(8,128)S(1)} %bitcast.24, s32[]{:T(128)S(6)} %select_n.21, bf16[4,496,128]{2,1,0:T(8,128)(2,1)} %bitcast.5), kind=kLoop, calls=%fused_computation.3 | loop fusion | flops 571392 | bytes 888836 | tf_op jit(solution)/shard_map/convert_element_type | solution.py:440
  39.0 2.9 %collective-permute-start.8 = (bf16[496,128]{1,0:T(8,128)(2,1)S(1)}, bf16[496,128]{1,0:T(8,128)(2,1)S(1)}, u32[]{:S(2)}, u32[]{:S(2)}) collective-permute-start(bf16[496,128]{1,0:T(8,128)(2,1)S(1)} %fusion.2), channel_id=1, source_target_pairs={{0,8},{4,12},{8,0},{12,4},{16,24},{20,28},{24,16},{28,20},{1,9},{5... | collective-permute-start | bytes 380936 | tf_op jit(solution)/shard_map/ppermute | solution.py:444
  41.8 2.9 %collective-permute-done.8 = bf16[496,128]{1,0:T(8,128)(2,1)S(1)} collective-permute-done((bf16[496,128]{1,0:T(8,128)(2,1)S(1)}, bf16[496,128]{1,0:T(8,128)(2,1)S(1)}, u32[]{:S(2)}, u32[]{:S(2)}) %collective-permute-start.8) | collective-permute-done | bytes 127008 | tf_op jit(solution)/shard_map/ppermute | solution.py:444
  44.8 3.1 %collective-permute-start.9 = (bf16[496,128]{1,0:T(8,128)(2,1)S(1)}, bf16[496,128]{1,0:T(8,128)(2,1)S(1)}, u32[]{:S(2)}, u32[]{:S(2)}) collective-permute-start(bf16[496,128]{1,0:T(8,128)(2,1)S(1)} %add_convert_fusion.1), channel_id=1, source_target_pairs={{0,16},{4,20},{8,24},{12,28},{16,0},{20,4},{24,8},{28,12},{1,17},{... | collective-permute-start | bytes 380936 | tf_op jit(solution)/shard_map/ppermute | solution.py:444
  47.9 4.4 %collective-permute-done.9 = bf16[496,128]{1,0:T(8,128)(2,1)S(1)} collective-permute-done((bf16[496,128]{1,0:T(8,128)(2,1)S(1)}, bf16[496,128]{1,0:T(8,128)(2,1)S(1)}, u32[]{:S(2)}, u32[]{:S(2)}) %collective-permute-start.9) | collective-permute-done | bytes 127008 | tf_op jit(solution)/shard_map/ppermute | solution.py:444
  52.3 3.0 %collective-permute-start.12 = (bf16[496,128]{1,0:T(8,128)(2,1)S(1)}, bf16[496,128]{1,0:T(8,128)(2,1)S(1)}, u32[]{:S(2)}, u32[]{:S(2)}) collective-permute-start(bf16[496,128]{1,0:T(8,128)(2,1)S(1)} %add_convert_fusion.refs_0_), channel_id=1, source_target_pairs={{0,6},{2,4},{4,2},{6,0},{8,14},{10,12},{12,10},{14,8},{16,22},{18,... | collective-permute-start | bytes 380936 | tf_op jit(solution)/shard_map/ppermute | solution.py:433
  55.3 1.6 %collective-permute-start.11 = (bf16[496,128]{1,0:T(8,128)(2,1)S(1)}, bf16[496,128]{1,0:T(8,128)(2,1)S(1)}, u32[]{:S(2)}, u32[]{:S(2)}) collective-permute-start(bf16[496,128]{1,0:T(8,128)(2,1)S(1)} %add_convert_fusion.refs_0_), channel_id=1, source_target_pairs={{0,4},{2,6},{4,0},{6,2},{8,12},{10,14},{12,8},{14,10},{16,20},{18,... | collective-permute-start | bytes 380936 | tf_op jit(solution)/shard_map/ppermute | solution.py:433
  56.9 0.0 collective-permute-start.10
  56.9 0.0 collective-permute-start.13
  56.9 2.6 %collective-permute-done.12.refs_3_ = bf16[496,128]{1,0:T(8,128)(2,1)S(1)} collective-permute-done((bf16[496,128]{1,0:T(8,128)(2,1)S(1)}, bf16[496,128]{1,0:T(8,128)(2,1)S(1)}, u32[]{:S(2)}, u32[]{:S(2)}) %collective-permute-start.12) | collective-permute-done | bytes 127008 | tf_op jit(solution)/shard_map/ppermute | solution.py:433
  59.5 0.0 collective-permute-start.16
  59.5 2.5 %collective-permute-done.11.refs_2_ = bf16[496,128]{1,0:T(8,128)(2,1)S(1)} collective-permute-done((bf16[496,128]{1,0:T(8,128)(2,1)S(1)}, bf16[496,128]{1,0:T(8,128)(2,1)S(1)}, u32[]{:S(2)}, u32[]{:S(2)}) %collective-permute-start.11) | collective-permute-done | bytes 127008 | tf_op jit(solution)/shard_map/ppermute | solution.py:433
  62.0 0.0 collective-permute-start.15
  62.0 0.0 collective-permute-done.10.refs_1_
  62.0 0.5 collective-permute-start.14
  62.5 0.0 collective-permute-done.13.refs_4_
  62.5 0.0 collective-permute-done.16.refs_7_
  62.5 0.8 %collective-permute-done.15.refs_6_ = bf16[496,128]{1,0:T(8,128)(2,1)S(1)} collective-permute-done((bf16[496,128]{1,0:T(8,128)(2,1)S(1)}, bf16[496,128]{1,0:T(8,128)(2,1)S(1)}, u32[]{:S(2)}, u32[]{:S(2)}) %collective-permute-start.15) | collective-permute-done | bytes 127008 | tf_op jit(solution)/shard_map/ppermute | solution.py:447
  63.4 0.2 collective-permute-done.14.refs_5_
  63.5 1.9 %last.1 = (f32[27,96,96]{2,1,0:T(8,128)}, f32[27,96,96]{2,1,0:T(8,128)}, f32[1,96]{1,0:T(1,128)}) custom-call(bf16[496,128]{1,0:T(8,128)(2,1)S(1)} %add_convert_fusion.refs_0_, bf16[496,128]{1,0:T(8,128)(2,1)S(1)} %collective-permute-done.10.refs_1_, bf16[496,128]{1,0:T(8,128)(2,1)S(1)} %collective-permute-done.11.refs_2_, ...), custom_call_target="tpu_custom_call" | custom-call | tf_op jit(solution)/shard_map/last/pallas_call | solution.py:23
  (15 shorter events, 0.1 us)
Async XLA Ops:
  0.6 0.9 %copy-start.4 = (bf16[8,8,8,96]{3,2,1,0:T(8,128)(2,1)S(1)}, bf16[8,8,8,96]{3,2,1,0:T(8,128)(2,1)}, u32[]{:S(2)}) copy-start(bf16[8,8,8,96]{3,2,1,0:T(8,128)(2,1)} %param.6) | copy-start | bytes 294916
  1.5 0.8 %copy-start.5 = (s32[8,8,8]{2,1,0:T(8,128)S(1)}, s32[8,8,8]{2,1,0:T(8,128)}, u32[]{:S(2)}) copy-start(s32[8,8,8]{2,1,0:T(8,128)} %param.7) | copy-start | bytes 6148
  2.3 0.7 %copy-start.6 = (bf16[4,4,4,96]{3,2,1,0:T(4,128)(2,1)S(1)}, bf16[4,4,4,96]{3,2,1,0:T(4,128)(2,1)}, u32[]{:S(2)}) copy-start(bf16[4,4,4,96]{3,2,1,0:T(4,128)(2,1)} %param.11) | copy-start | bytes 36868
  3.2 1.4 %collective-permute-start = (bf16[160,128]{1,0:T(8,128)(2,1)S(1)}, bf16[160,128]{1,0:T(8,128)(2,1)S(1)}, u32[]{:S(2)}, u32[]{:S(2)}) collective-permute-start(bf16[160,128]{1,0:T(8,128)(2,1)S(1)} %get-tuple-element.28), channel_id=1, source_target_pairs={{0,1},{1,0},{2,3},{3,2},{4,5},{5,4},{6,7},{7,6},{8,9},{9,8},{10,11... | collective-permute-start | bytes 122888 | tf_op jit(solution)/shard_map/ppermute | solution.py:358
  3.7 0.9 %collective-permute-start.1 = (bf16[160,128]{1,0:T(8,128)(2,1)S(1)}, bf16[160,128]{1,0:T(8,128)(2,1)S(1)}, u32[]{:S(2)}, u32[]{:S(2)}) collective-permute-start(bf16[160,128]{1,0:T(8,128)(2,1)S(1)} %get-tuple-element.29), channel_id=1, source_target_pairs={{1,2},{2,1},{5,6},{6,5},{9,10},{10,9},{13,14},{14,13},{17,18},{18,... | collective-permute-start | bytes 122888 | tf_op jit(solution)/shard_map/ppermute | solution.py:359
  4.7 5.1 %collective-permute-start.2 = (bf16[240,128]{1,0:T(8,128)(2,1)S(1)}, bf16[240,128]{1,0:T(8,128)(2,1)S(1)}, u32[]{:S(2)}, u32[]{:S(2)}) collective-permute-start(bf16[240,128]{1,0:T(8,128)(2,1)S(1)} %get-tuple-element.30), channel_id=1, source_target_pairs={{0,4},{4,0},{8,12},{12,8},{16,20},{20,16},{24,28},{28,24},{1,5},{5... | collective-permute-start | bytes 184328 | tf_op jit(solution)/shard_map/ppermute | solution.py:371
  7.5 2.2 %collective-permute-start.3 = (bf16[240,128]{1,0:T(8,128)(2,1)S(1)}, bf16[240,128]{1,0:T(8,128)(2,1)S(1)}, u32[]{:S(2)}, u32[]{:S(2)}) collective-permute-start(bf16[240,128]{1,0:T(8,128)(2,1)S(1)} %get-tuple-element.31), channel_id=1, source_target_pairs={{4,8},{12,16},{20,24},{8,4},{16,12},{24,20},{5,9},{13,17},{21,25},... | collective-permute-start | bytes 184328 | tf_op jit(solution)/shard_map/ppermute | solution.py:372
  9.7 1.1 %copy-start = (bf16[27,96,96]{2,1,0:T(8,128)(2,1)S(1)}, bf16[27,96,96]{2,1,0:T(8,128)(2,1)}, u32[]{:S(2)}) copy-start(bf16[27,96,96]{2,1,0:T(8,128)(2,1)} %cw_ref.3) | copy-start | bytes 1492996
  10.8 1.1 %copy-start.2 = (bf16[27,96,96]{2,1,0:T(8,128)(2,1)S(1)}, bf16[27,96,96]{2,1,0:T(8,128)(2,1)}, u32[]{:S(2)}) copy-start(bf16[27,96,96]{2,1,0:T(8,128)(2,1)} %dw_ref.3) | copy-start | bytes 1492996
  11.9 0.7 %copy-start.7 = (f32[96]{0:T(128)S(1)}, f32[96]{0:T(128)}, u32[]{:S(2)}) copy-start(f32[96]{0:T(128)} %param.9) | copy-start | bytes 1156
  12.6 19.6 %copy-start.1 = (bf16[27,96,96]{2,1,0:T(8,128)(2,1)S(1)}, bf16[27,96,96]{2,1,0:T(8,128)(2,1)}, u32[]{:S(2)}) copy-start(bf16[27,96,96]{2,1,0:T(8,128)(2,1)} %cw_ref.3) | copy-start | bytes 1492996
  12.6 19.6 %copy-start.3 = (bf16[27,96,96]{2,1,0:T(8,128)(2,1)S(1)}, bf16[27,96,96]{2,1,0:T(8,128)(2,1)}, u32[]{:S(2)}) copy-start(bf16[27,96,96]{2,1,0:T(8,128)(2,1)} %dw_ref.3) | copy-start | bytes 1492996
  17.3 0.7 %copy-start.8 = (bf16[800,128]{1,0:T(8,128)(2,1)}, bf16[800,128]{1,0:T(8,128)(2,1)S(1)}, u32[]{:S(2)}) copy-start(bf16[800,128]{1,0:T(8,128)(2,1)S(1)} %get-tuple-element.36.s_ref) | copy-start | bytes 614404
  17.9 5.4 %collective-permute-start.4 = (bf16[1984,128]{1,0:T(8,128)(2,1)S(1)}, bf16[1984,128]{1,0:T(8,128)(2,1)}, u32[]{:S(2)}, u32[]{:S(2)}) collective-permute-start(bf16[1984,128]{1,0:T(8,128)(2,1)S(1)} %get-tuple-element.33), channel_id=1, source_target_pairs={{0,1},{1,0},{2,3},{3,2},{4,5},{5,4},{6,7},{7,6},{8,9},{9,8},{10,11... | collective-permute-start | bytes 1523720 | tf_op jit(solution)/shard_map/ppermute | solution.py:419
  21.7 10.5 %copy-start.9 = (bf16[800,128]{1,0:T(8,128)(2,1)S(1)}, bf16[800,128]{1,0:T(8,128)(2,1)}, u32[]{:S(2)}) copy-start(bf16[800,128]{1,0:T(8,128)(2,1)} %copy-done.8) | copy-start | bytes 614404
  24.4 11.4 %collective-permute-start.7 = (bf16[496,128]{1,0:T(8,128)(2,1)S(1)}, bf16[496,128]{1,0:T(8,128)(2,1)S(1)}, u32[]{:S(2)}, u32[]{:S(2)}) collective-permute-start(bf16[496,128]{1,0:T(8,128)(2,1)S(1)} %get-tuple-element.47), channel_id=1, source_target_pairs={{0,6},{2,4},{4,2},{6,0},{8,14},{10,12},{12,10},{14,8},{16,22},{18,... | collective-permute-start | bytes 380936 | tf_op jit(solution)/shard_map/ppermute | solution.py:433
  31.5 5.7 %collective-permute-start.6 = (bf16[496,128]{1,0:T(8,128)(2,1)S(1)}, bf16[496,128]{1,0:T(8,128)(2,1)S(1)}, u32[]{:S(2)}, u32[]{:S(2)}) collective-permute-start(bf16[496,128]{1,0:T(8,128)(2,1)S(1)} %get-tuple-element.48), channel_id=1, source_target_pairs={{0,4},{2,6},{4,0},{6,2},{8,12},{10,14},{12,8},{14,10},{16,20},{18,... | collective-permute-start | bytes 380936 | tf_op jit(solution)/shard_map/ppermute | solution.py:433
  31.5 6.4 %collective-permute-start.5 = (bf16[496,128]{1,0:T(8,128)(2,1)S(1)}, bf16[496,128]{1,0:T(8,128)(2,1)S(1)}, u32[]{:S(2)}, u32[]{:S(2)}) collective-permute-start(bf16[496,128]{1,0:T(8,128)(2,1)S(1)} %get-tuple-element.49), channel_id=1, source_target_pairs={{0,2},{2,0},{4,6},{6,4},{8,10},{10,8},{12,14},{14,12},{16,18},{18,... | collective-permute-start | bytes 380936 | tf_op jit(solution)/shard_map/ppermute | solution.py:433
  39.0 5.8 %collective-permute-start.8 = (bf16[496,128]{1,0:T(8,128)(2,1)S(1)}, bf16[496,128]{1,0:T(8,128)(2,1)S(1)}, u32[]{:S(2)}, u32[]{:S(2)}) collective-permute-start(bf16[496,128]{1,0:T(8,128)(2,1)S(1)} %fusion.2), channel_id=1, source_target_pairs={{0,8},{4,12},{8,0},{12,4},{16,24},{20,28},{24,16},{28,20},{1,9},{5... | collective-permute-start | bytes 380936 | tf_op jit(solution)/shard_map/ppermute | solution.py:444
  44.8 7.5 %collective-permute-start.9 = (bf16[496,128]{1,0:T(8,128)(2,1)S(1)}, bf16[496,128]{1,0:T(8,128)(2,1)S(1)}, u32[]{:S(2)}, u32[]{:S(2)}) collective-permute-start(bf16[496,128]{1,0:T(8,128)(2,1)S(1)} %add_convert_fusion.1), channel_id=1, source_target_pairs={{0,16},{4,20},{8,24},{12,28},{16,0},{20,4},{24,8},{28,12},{1,17},{... | collective-permute-start | bytes 380936 | tf_op jit(solution)/shard_map/ppermute | solution.py:444
  52.3 7.2 %collective-permute-start.12 = (bf16[496,128]{1,0:T(8,128)(2,1)S(1)}, bf16[496,128]{1,0:T(8,128)(2,1)S(1)}, u32[]{:S(2)}, u32[]{:S(2)}) collective-permute-start(bf16[496,128]{1,0:T(8,128)(2,1)S(1)} %add_convert_fusion.refs_0_), channel_id=1, source_target_pairs={{0,6},{2,4},{4,2},{6,0},{8,14},{10,12},{12,10},{14,8},{16,22},{18,... | collective-permute-start | bytes 380936 | tf_op jit(solution)/shard_map/ppermute | solution.py:433
  55.3 6.7 %collective-permute-start.11 = (bf16[496,128]{1,0:T(8,128)(2,1)S(1)}, bf16[496,128]{1,0:T(8,128)(2,1)S(1)}, u32[]{:S(2)}, u32[]{:S(2)}) collective-permute-start(bf16[496,128]{1,0:T(8,128)(2,1)S(1)} %add_convert_fusion.refs_0_), channel_id=1, source_target_pairs={{0,4},{2,6},{4,0},{6,2},{8,12},{10,14},{12,8},{14,10},{16,20},{18,... | collective-permute-start | bytes 380936 | tf_op jit(solution)/shard_map/ppermute | solution.py:433
  56.9 5.1 %collective-permute-start.10 = (bf16[496,128]{1,0:T(8,128)(2,1)S(1)}, bf16[496,128]{1,0:T(8,128)(2,1)S(1)}, u32[]{:S(2)}, u32[]{:S(2)}) collective-permute-start(bf16[496,128]{1,0:T(8,128)(2,1)S(1)} %add_convert_fusion.refs_0_), channel_id=1, source_target_pairs={{0,2},{2,0},{4,6},{6,4},{8,10},{10,8},{12,14},{14,12},{16,18},{18,... | collective-permute-start | bytes 380936 | tf_op jit(solution)/shard_map/ppermute | solution.py:433
  56.9 5.6 %collective-permute-start.13 = (bf16[496,128]{1,0:T(8,128)(2,1)S(1)}, bf16[496,128]{1,0:T(8,128)(2,1)S(1)}, u32[]{:S(2)}, u32[]{:S(2)}) collective-permute-start(bf16[496,128]{1,0:T(8,128)(2,1)S(1)} %add_convert_fusion.refs_0_), channel_id=1, source_target_pairs={{0,1},{1,0},{2,3},{3,2},{4,5},{5,4},{6,7},{7,6},{8,9},{9,8},{10,11... | collective-permute-start | bytes 380936 | tf_op jit(solution)/shard_map/ppermute | solution.py:447
  59.5 3.1 %collective-permute-start.16 = (bf16[496,128]{1,0:T(8,128)(2,1)S(1)}, bf16[496,128]{1,0:T(8,128)(2,1)S(1)}, u32[]{:S(2)}, u32[]{:S(2)}) collective-permute-start(bf16[496,128]{1,0:T(8,128)(2,1)S(1)} %collective-permute-done.12.refs_3_), channel_id=1, source_target_pairs={{0,1},{1,0},{2,3},{3,2},{4,5},{5,4},{6,7},{7,6},{8,9},{9,8},{10,11... | collective-permute-start | bytes 380936 | tf_op jit(solution)/shard_map/ppermute | solution.py:447
  62.0 1.3 %collective-permute-start.15 = (bf16[496,128]{1,0:T(8,128)(2,1)S(1)}, bf16[496,128]{1,0:T(8,128)(2,1)S(1)}, u32[]{:S(2)}, u32[]{:S(2)}) collective-permute-start(bf16[496,128]{1,0:T(8,128)(2,1)S(1)} %collective-permute-done.11.refs_2_), channel_id=1, source_target_pairs={{0,1},{1,0},{2,3},{3,2},{4,5},{5,4},{6,7},{7,6},{8,9},{9,8},{10,11... | collective-permute-start | bytes 380936 | tf_op jit(solution)/shard_map/ppermute | solution.py:447
  62.0 1.5 %collective-permute-start.14 = (bf16[496,128]{1,0:T(8,128)(2,1)S(1)}, bf16[496,128]{1,0:T(8,128)(2,1)S(1)}, u32[]{:S(2)}, u32[]{:S(2)}) collective-permute-start(bf16[496,128]{1,0:T(8,128)(2,1)S(1)} %collective-permute-done.10.refs_1_), channel_id=1, source_target_pairs={{0,1},{1,0},{2,3},{3,2},{4,5},{5,4},{6,7},{7,6},{8,9},{9,8},{10,11... | collective-permute-start | bytes 380936 | tf_op jit(solution)/shard_map/ppermute | solution.py:447

commit v3 on v2

--- a/solution.py
+++ b/solution.py
@@ -17,21 +17,34 @@
 MIB = 1024 * 1024
 
 
-def call(body, outs, args, scratch=(), cost=None, name=None, vmem=8, in_hbm=False, sems=()):
-    in_place = pl.BlockSpec(memory_space=pltpu.VMEM)
-    placed = pl.BlockSpec(memory_space=pl.ANY) if in_hbm else in_place
+def call(body, outs, args, scratch=(), cost=None, name=None, vmem=8, far=(), far_outs=False, sems=0):
+    near_spec = pl.BlockSpec(memory_space=pltpu.VMEM)
+    far_spec = pl.BlockSpec(memory_space=pltpu.HBM)
+    args = [
+        pltpu.with_memory_space_constraint(a, pltpu.HBM) if i in far else a
+        for i, a in enumerate(args)
+    ]
     return pl.pallas_call(
         body,
         out_shape=tuple(jax.ShapeDtypeStruct(s, d) for s, d in outs),
-        in_specs=[in_place] * len(args),
-        out_specs=tuple(placed for _ in outs),
-        scratch_shapes=[pltpu.VMEM(s, d) for s, d in scratch] + list(sems),
+        in_specs=[far_spec if i in far else near_spec for i in range(len(args))],
+        out_specs=tuple(far_spec if far_outs else near_spec for _ in outs),
+        scratch_shapes=[pltpu.VMEM(s, d) for s, d in scratch]
+        + ([pltpu.SemaphoreType.DMA((sems,))] if sems else []),
         compiler_params=pltpu.CompilerParams(vmem_limit_bytes=vmem * MIB),
         cost_estimate=cost,
         name=name,
     )(*args)
 
 
+def fetch(pairs, sems):
+    copies = [pltpu.make_async_copy(a, b, sems.at[i]) for i, (a, b) in enumerate(pairs)]
+    for copy in copies:
+        copy.start()
+    for copy in copies:
+        copy.wait()
+
+
 def lane_of(shape):
     return lax.broadcasted_iota(jnp.int32, shape, len(shape) - 1)
 
@@ -49,8 +62,12 @@
     return jnp.where(z_of(v.shape) == top, 0.0, pltpu.roll(v, top, axis=1))
 
 
-def first_kernel(dims, vox_ref, occ_ref, cot_ref, x_ref, u_ref, core_ref, side_ref, xs, us):
+def first_kernel(
+    dims, vox_far, occ_far, cot_far, x_ref, u_ref, core_ref, side_ref,
+    xs, us, vox_ref, occ_ref, cot_ref, sems,
+):
     tx, ty, tz, ch = dims
+    fetch(((vox_far, vox_ref), (occ_far, occ_ref), (cot_far, cot_ref)), sems)
     hx, hy = tx // 2, ty // 2
     occ = jnp.broadcast_to(occ_ref[...].astype(F32)[:, :, None], (tx * ty, tz, LANES))
     xs[...] = jnp.zeros(xs.shape, F32)
@@ -126,6 +143,19 @@
         out[at : at + ch, lane : lane + ch] = w_ref[t]
 
 
+def weights_kernel(ch, cw_far, dw_far, bias_far, cl_ref, dr_ref, b_ref, cw, dw, bias, sems):
+    fetch(((cw_far, cw), (dw_far, dw), (bias_far, bias)), sems)
+    taps_in_lanes(ch, cw, cl_ref)
+    taps_in_rows(ch, dw, dr_ref)
+    b_ref[...] = jnp.zeros(b_ref.shape, F32)
+    b_ref[:, :ch] = bias[...]
+
+
+def other_weights_kernel(ch, cw, dw, cr_ref, dl_ref):
+    taps_in_rows(ch, cw, cr_ref)
+    taps_in_lanes(ch, dw, dl_ref)
+
+
 def three(v):
     return v[:, :, :LANES], v[:, :, LANES : 2 * LANES], v[:, :, 2 * LANES :]
 
@@ -156,9 +186,9 @@
 
 
 def main_kernel(
-    dims, x_ref, u_ref, core_ref, side_ref, near_ref, far_ref, cw_ref, dw_ref, bias_ref,
+    dims, x_ref, u_ref, core_ref, side_ref, near_ref, far_ref, wf, wd, bias,
     keep_ref, send_ref, gp_ref, gs_ref, s_ref,
-    xe, ue, ss, acc, gsr, gp, wf, wd, pack, bias,
+    xe, ue, ss, acc, gsr, gp, pack,
 ):
     tx, ty, tz, ch = dims
     hx, hy = tx // 2, ty // 2
@@ -166,10 +196,6 @@
     block_rows = ch * ch // LANES
     core = lax.axis_index("core")
     odd = lax.rem(lax.axis_index("gx"), 2)
-    taps_in_lanes(ch, cw_ref, wf)
-    taps_in_rows(ch, dw_ref, wd)
-    bias[...] = jnp.zeros(bias.shape, F32)
-    bias[:, :ch] = bias_ref[...]
     widen(dims, x_ref, u_ref, core_ref, side_ref, xe, ue, 2, 1)
     rows = 2 * (ty + 4) * tz
     for ref, low in ((near_ref, odd), (far_ref, 1 - odd)):
@@ -262,14 +288,12 @@
 
 
 def second_outputs(
-    dims, x_ref, u_ref, gp_ref, gs_ref, s_ref, cw_ref, dw_ref, down_ref, gv_ref,
-    ge, ss, accd, wf, wd,
+    dims, x_ref, u_ref, gp_ref, gs_ref, s_ref, wf, wd, down_ref, gv_ref,
+    ge, ss, accd,
 ):
     tx, ty, tz, ch = dims
     hx, hy = tx // 2, ty // 2
     ex, ey = tx + 2, ty + 2
-    taps_in_rows(ch, cw_ref, wf)
-    taps_in_lanes(ch, dw_ref, wd)
     ge[...] = gp_ref[...].astype(F32).reshape(ex, ey, tz, LANES)
     ss[...] = s_ref[...].astype(F32).reshape(hx + 1, 2, hy + 1, 2, tz, LANES)
     wins = [
@@ -300,6 +324,20 @@
     x = x_ref[...].astype(F32)
     live = jnp.broadcast_to(x[:, ch : ch + 1], x.shape)
     gv_ref[...] = ((gs_ref[...] + out) * live)[:, :ch].astype(BF16)
+
+
+def split_kernel(keep_ref, got_ref, own_ref, *to_refs):
+    me = lax.rem(lax.axis_index("gx"), 2) * 2 + lax.rem(lax.axis_index("gyc"), 2)
+    rows = own_ref.shape[0]
+    for k, ref in enumerate((own_ref, *to_refs)):
+        at = pl.ds(pl.multiple_of((me ^ k) * rows, 16), rows)
+        ref[...] = (keep_ref[at] + got_ref[at].astype(F32)).astype(ref.dtype)
+
+
+def sum_kernel(own_ref, a_ref, b_ref, c_ref, out_ref):
+    out_ref[...] = (
+        own_ref[...] + a_ref[...].astype(F32) + b_ref[...].astype(F32) + c_ref[...].astype(F32)
+    ).astype(BF16)
 
 
 def last_kernel(ch, factor, *refs):
@@ -347,9 +385,17 @@
             occupancy.reshape(tx * ty, tz),
             down_cotangent.reshape(hx * hy * hz, ch),
         ),
-        [((fine, LANES), F32), ((coarse, LANES), F32)],
+        [
+            ((fine, LANES), F32),
+            ((coarse, LANES), F32),
+            ((fine, ch), BF16),
+            ((tx * ty, tz), jnp.int32),
+            ((hx * hy * hz, ch), BF16),
+        ],
         name="first",
         vmem=4,
+        far=(0, 1, 2),
+        sems=3,
     )
     swap = [(0, 1), (1, 0)]
     n_gy = n_gyc * 2
@@ -357,6 +403,19 @@
     sides += [(j, i) for i, j in sides]
     from_core = lax.ppermute(to_core, "core", swap)
     from_side = lax.ppermute(to_side, ("gyc", "core"), sides)
+    in_lanes, in_rows = ((9 * LANES, 3 * LANES), BF16), ((9, 3 * LANES, LANES), BF16)
+    weights = call(
+        functools.partial(weights_kernel, ch),
+        [in_lanes, in_rows, ((1, LANES), F32), ((27, ch, ch), BF16), ((27, ch, ch), BF16)],
+        (conv_weight, down_weight, conv_bias.reshape(1, ch)),
+        [((1, ch), F32)],
+        name="weights",
+        vmem=4,
+        far=(0, 1, 2),
+        sems=3,
+    )
+    from_core, from_side, *weights = lax.optimization_barrier((from_core, from_side, *weights))
+    conv_lanes, down_rows, bias, raw_conv, raw_down = weights
     to_near, to_far = call(
         functools.partial(second_kernel, dims),
         [((row_rows, LANES), BF16)] * 2,
@@ -368,8 +427,8 @@
     near = [(i, i ^ 1) for i in range(n_gx)]
     far = [(i, i + 1) for i in range(1, n_gx - 1, 2)]
     far += [(j, i) for i, j in far]
+    from_far = lax.ppermute(to_far, "gx", far)
     from_near = lax.ppermute(to_near, "gx", near)
-    from_far = lax.ppermute(to_far, "gx", far)
 
     block_rows = ch * ch // LANES
     half_rows = -(-(27 * block_rows + 8) // 64) * 64
@@ -378,8 +437,7 @@
         [((half_rows, LANES), F32), ((half_rows, LANES), BF16)]
         + [((ex * ey * tz, LANES), BF16), ((fine, LANES), F32), ((ex * ey * tz, LANES), BF16)],
         (
-            x, u, from_core, from_side, from_near, from_far, conv_weight, down_weight,
-            conv_bias.reshape(1, ch),
+            x, u, from_core, from_side, from_near, from_far, conv_lanes, down_rows, bias,
         ),
         [
             ((tx + 4, ty + 4, tz, LANES), F32),
@@ -388,42 +446,46 @@
             ((ex, ey, tz, LANES), F32),
             ((hx + 1, 2, hy + 1, 2, tz, LANES), F32),
             ((ex, ey, tz, LANES), F32),
-            ((9 * LANES, 3 * LANES), BF16),
-            ((9, 3 * LANES, LANES), BF16),
             ((2, half_rows, LANES), F32),
-            ((1, LANES), F32),
         ],
         name="main",
-        vmem=24,
-    )
-
+        vmem=16,
+    )
+
+    rest = call(
+        functools.partial(other_weights_kernel, ch),
+        [in_rows, in_lanes],
+        (raw_conv, raw_down),
+        name="weights2",
+        vmem=4,
+    )
+    conv_rows, down_lanes = rest
     down, grad_voxels = call(
         functools.partial(second_outputs, dims),
         [((hx * hy * hz, ch), BF16), ((fine, ch), BF16)],
-        (x, u, gp, gs, s, conv_weight, down_weight),
+        (x, u, gp, gs, s, conv_rows, down_lanes),
         [
             ((ex, ey, tz, LANES), F32),
             ((hx + 1, 2, hy + 1, 2, tz, LANES), F32),
             ((coarse, LANES), F32),
-            ((9, 3 * LANES, LANES), BF16),
-            ((9 * LANES, 3 * LANES), BF16),
         ],
         cost=pl.CostEstimate(flops=5_000_000_000, bytes_accessed=4_000_000, transcendentals=0),
         name="outputs",
-        vmem=24,
+        vmem=12,
     )
 
     def plus(a, b):
         return (a.astype(F32) + b.astype(F32)).astype(BF16)
 
     got = lax.ppermute(send, "core", swap)
-    me = lax.rem(lax.axis_index("gx"), 2) * 2 + lax.rem(lax.axis_index("gyc"), 2)
     quarter = half_rows // 4
-    keep4, got4 = keep.reshape(4, quarter, LANES), got.reshape(4, quarter, LANES)
-
-    def quarter_of(k):
-        pick = functools.partial(lax.dynamic_index_in_dim, index=me ^ k, axis=0, keepdims=False)
-        return pick(keep4).astype(F32) + pick(got4).astype(F32)
+    mine, *pieces = call(
+        split_kernel,
+        [((quarter, LANES), F32)] + [((quarter, LANES), BF16)] * 3,
+        (keep, got),
+        name="split",
+        vmem=2,
+    )
 
     def across(value, k):
         route = []
@@ -432,12 +494,15 @@
                 route.append((i * n_gyc + j, (i ^ (k >> 1)) * n_gyc + (j ^ (k & 1))))
         return lax.ppermute(value, ("gx", "gyc"), route)
 
-    arrived = [across(quarter_of(k).astype(BF16), k) for k in (1, 2, 3)]
+    arrived = [across(piece, k) for k, piece in zip((1, 2, 3), pieces)]
     *arrived, down, grad_voxels = lax.optimization_barrier((*arrived, down, grad_voxels))
-    total = quarter_of(0)
-    for piece in arrived:
-        total = total + piece.astype(F32)
-    total = total.astype(BF16)
+    (total,) = call(
+        sum_kernel,
+        [((quarter, LANES), BF16)],
+        (mine, *arrived),
+        name="sum",
+        vmem=2,
+    )
     for axis, peers in (("gx", n_gx), ("gyc", n_gyc)):
         step = 2
         while step < peers:
@@ -457,9 +522,9 @@
             ((1, ch), F32),
         ],
         name="last",
-        vmem=12,
-        in_hbm=True,
-        sems=[pltpu.SemaphoreType.DMA((7,))],
+        vmem=10,
+        far_outs=True,
+        sems=7,
     )
     return (
         down.reshape(hx, hy, hz, ch),

time: 65.8 us -> 55.7 us (0.85)
  local copies, waits for them, and re-layouts: 5.89 us -> 0 us
  starting transfers between devices: 27.3 us -> 24.2 us
  Pallas kernels: 8.64 us -> 11.2 us
  other arithmetic: 2.17 us -> 0.07 us
  waiting for transfers between devices: 20.7 us -> 19.2 us
    unnamed x20 -> x0, local copies, waits for them, and re-layouts: 5.89 us -> none
    pallas_call x5 -> x9, Pallas kernels: 8.64 us -> 11.2 us  [call(): pl.pallas_call(body, out_shape=tuple((jax.ShapeDtypeStruct(s, d) for s, d...]
    convert_element_type x2 -> x0, other arithmetic: 2.09 us -> none  [the longest x1 1.11 us: on_device(): arrived = [across(quarter_of(k).astype(BF16), k) for k in (1, 2, 3)]]
    ppermute x1, starting transfers between devices: 3.72 us -> 2.58 us  [on_device(): got = lax.ppermute(send, 'core', swap)]
    ppermute x6, starting transfers between devices: 12.3 us -> 11.2 us  [across(): return lax.ppermute(value, ('gx', 'gyc'), route)]
    ppermute x6, waiting for transfers between devices: 8.98 us -> 7.93 us  [across(): return lax.ppermute(value, ('gx', 'gyc'), route)]
  transfers between devices with their start and end apart: 17 -> 17, of which waited for: 12 -> 11; matrix products, arithmetic and copies ran while one was open for 0% -> 0% of each run, Pallas kernels for 3% -> 7%
where the time goes in v3:
time: 55.7 us; the launch traced here: 55.5 us
  starting transfers between devices  24.2 us (43%)
  waiting for transfers between devices  19.2 us (34%)
  Pallas kernels  11.2 us (20%)
  between operations  0.72 us (1%)
    pallas_call x9, Pallas kernels, call(): pl.pallas_call(body, out_shape=tuple((jax.ShapeDtypeStruct(s, d) for s, d...  11.2 us
    ppermute x6, starting transfers between devices, across(): return lax.ppermute(value, ('gx', 'gyc'), route)  11.2 us
    ppermute x6, waiting for transfers between devices, across(): return lax.ppermute(value, ('gx', 'gyc'), route)  7.93 us
    ppermute x2, waiting for transfers between devices, on_device(): lax.ppermute(total, axis, [(i, i ^ step) for i in range(peers)])  7.33 us
    ppermute x2, starting transfers between devices, on_device(): lax.ppermute(total, axis, [(i, i ^ step) for i in range(peers)])  5.95 us
    ppermute x1, starting transfers between devices, on_device(): got = lax.ppermute(send, 'core', swap)  2.58 us
    ppermute x1, starting transfers between devices, on_device(): from_near = lax.ppermute(to_near, 'gx', near)  2.56 us
    ppermute x1, waiting for transfers between devices, on_device(): from_near = lax.ppermute(to_near, 'gx', near)  1.54 us
  transfers between devices with their start and end apart: 17, of which 11 were waited for; matrix products, arithmetic and copies ran while one was open for 0% of the time, Pallas kernels for 7%

profile of v3, /device:TPU:0, one launch (start us, length us, event | category | flops | bytes accessed | tf_op | source)
XLA Modules:
  0.0 55.5 jit_solution(8367483712734815666)
XLA Ops:
  0.6 1.1 %first.1 = (bf16[512,128]{1,0:T(8,128)(2,1)S(1)}, bf16[128,128]{1,0:T(8,128)(2,1)S(1)}, bf16[160,128]{1,0:T(8,128)(2,1)S(1)}, bf16[160,128]{1,0:T(8,128)(2,1)S(1)}) custom-call(bf16[512,96]{1,0:T(8,128)(2,1)} %bitcast.7, s32[64,8]{1,0:T(8,128)} %bitcast.8, bf16[64,96]{1,0:T(8,128)(2,1)} %bitcast.9), custom_call_target="tpu_custom_call" | custom-call | tf_op jit(solution)/shard_map/first/pallas_call | solution.py:27
  1.7 0.6 %collective-permute-start = (bf16[160,128]{1,0:T(8,128)(2,1)S(1)}, bf16[160,128]{1,0:T(8,128)(2,1)S(1)}, u32[]{:S(2)}, u32[]{:S(2)}) collective-permute-start(bf16[160,128]{1,0:T(8,128)(2,1)S(1)} %get-tuple-element.46), channel_id=1, source_target_pairs={{0,1},{1,0},{2,3},{3,2},{4,5},{5,4},{6,7},{7,6},{8,9},{9,8},{10,11... | collective-permute-start | bytes 122888 | tf_op jit(solution)/shard_map/ppermute | solution.py:404
  2.3 0.7 %collective-permute-start.1 = (bf16[160,128]{1,0:T(8,128)(2,1)S(1)}, bf16[160,128]{1,0:T(8,128)(2,1)S(1)}, u32[]{:S(2)}, u32[]{:S(2)}) collective-permute-start(bf16[160,128]{1,0:T(8,128)(2,1)S(1)} %get-tuple-element.47), channel_id=1, source_target_pairs={{1,2},{2,1},{5,6},{6,5},{9,10},{10,9},{13,14},{14,13},{17,18},{18,... | collective-permute-start | bytes 122888 | tf_op jit(solution)/shard_map/ppermute | solution.py:405
  2.9 1.7 %weights.1 = (bf16[1152,384]{1,0:T(8,128)(2,1)S(1)}, bf16[9,384,128]{2,1,0:T(8,128)(2,1)S(1)}, f32[1,128]{1,0:T(1,128)S(1)}, bf16[27,96,96]{2,1,0:T(8,128)(2,1)S(1)}, bf16[27,96,96]{2,1,0:T(8,128)(2,1)S(1)}) custom-call(bf16[27,96,96]{2,1,0:T(8,128)(2,1)} %cw_far.1, bf16[27,96,96]{2,1,0:T(8,128)(2,1)} %dw_far.1, f32[1,96]{1,0:T(1,128)} %bitcast.10), custom_call_target="tpu_custom_call" | custom-call | tf_op jit(solution)/shard_map/weights/pallas_call | solution.py:27
  4.7 0.0 collective-permute-done.core_ref
  4.7 0.0 collective-permute-done.1.side_ref
  4.7 0.1 second.1
  4.8 2.6 %collective-permute-start.2 = (bf16[240,128]{1,0:T(8,128)(2,1)S(1)}, bf16[240,128]{1,0:T(8,128)(2,1)S(1)}, u32[]{:S(2)}, u32[]{:S(2)}) collective-permute-start(bf16[240,128]{1,0:T(8,128)(2,1)S(1)} %get-tuple-element.55), channel_id=1, source_target_pairs={{0,4},{4,0},{8,12},{12,8},{16,20},{20,16},{24,28},{28,24},{1,5},{5... | collective-permute-start | bytes 184328 | tf_op jit(solution)/shard_map/ppermute | solution.py:431
  7.3 0.7 %collective-permute-start.3 = (bf16[240,128]{1,0:T(8,128)(2,1)S(1)}, bf16[240,128]{1,0:T(8,128)(2,1)S(1)}, u32[]{:S(2)}, u32[]{:S(2)}) collective-permute-start(bf16[240,128]{1,0:T(8,128)(2,1)S(1)} %get-tuple-element.56), channel_id=1, source_target_pairs={{4,8},{12,16},{20,24},{8,4},{16,12},{24,20},{5,9},{13,17},{21,25},... | collective-permute-start | bytes 184328 | tf_op jit(solution)/shard_map/ppermute | solution.py:430
  8.0 1.5 %collective-permute-done.2.near_ref = bf16[240,128]{1,0:T(8,128)(2,1)S(1)} collective-permute-done((bf16[240,128]{1,0:T(8,128)(2,1)S(1)}, bf16[240,128]{1,0:T(8,128)(2,1)S(1)}, u32[]{:S(2)}, u32[]{:S(2)}) %collective-permute-start.2) | collective-permute-done | bytes 61472 | tf_op jit(solution)/shard_map/ppermute | solution.py:431
  9.5 0.0 collective-permute-done.3.far_ref
  9.5 4.2 %main.1 = (f32[1984,128]{1,0:T(8,128)S(1)}, bf16[1984,128]{1,0:T(8,128)(2,1)S(1)}, bf16[800,128]{1,0:T(8,128)(2,1)S(1)}, f32[512,128]{1,0:T(8,128)S(1)}, bf16[800,128]{1,0:T(8,128)(2,1)S(1)}) custom-call(bf16[512,128]{1,0:T(8,128)(2,1)S(1)} %get-tuple-element.44.x_ref, bf16[128,128]{1,0:T(8,128)(2,1)S(1)} %get-tuple-element.45.u_ref, ...), custom_call_target="tpu_custom_call" | custom-call | tf_op jit(solution)/shard_map/main/pallas_call | solution.py:27
  13.8 2.6 %collective-permute-start.4 = (bf16[1984,128]{1,0:T(8,128)(2,1)S(1)}, bf16[1984,128]{1,0:T(8,128)(2,1)S(1)}, u32[]{:S(2)}, u32[]{:S(2)}) collective-permute-start(bf16[1984,128]{1,0:T(8,128)(2,1)S(1)} %get-tuple-element.61), channel_id=1, source_target_pairs={{0,1},{1,0},{2,3},{3,2},{4,5},{5,4},{6,7},{7,6},{8,9},{9,8},{10,11... | collective-permute-start | bytes 1523720 | tf_op jit(solution)/shard_map/ppermute | solution.py:480
  16.4 0.4 weights2.1
  16.8 1.1 %collective-permute-done.4.got_ref = bf16[1984,128]{1,0:T(8,128)(2,1)S(1)} collective-permute-done((bf16[1984,128]{1,0:T(8,128)(2,1)S(1)}, bf16[1984,128]{1,0:T(8,128)(2,1)S(1)}, u32[]{:S(2)}, u32[]{:S(2)}) %collective-permute-start.4) | collective-permute-done | bytes 507936 | tf_op jit(solution)/shard_map/ppermute | solution.py:480
  17.9 0.1 split.1
  18.0 2.9 %collective-permute-start.5 = (bf16[496,128]{1,0:T(8,128)(2,1)S(1)}, bf16[496,128]{1,0:T(8,128)(2,1)S(1)}, u32[]{:S(2)}, u32[]{:S(2)}) collective-permute-start(bf16[496,128]{1,0:T(8,128)(2,1)S(1)} %get-tuple-element.62), channel_id=1, source_target_pairs={{0,2},{2,0},{4,6},{6,4},{8,10},{10,8},{12,14},{14,12},{16,18},{18,... | collective-permute-start | bytes 380936 | tf_op jit(solution)/shard_map/ppermute | solution.py:495
  20.9 4.8 %collective-permute-start.6 = (bf16[496,128]{1,0:T(8,128)(2,1)S(1)}, bf16[496,128]{1,0:T(8,128)(2,1)S(1)}, u32[]{:S(2)}, u32[]{:S(2)}) collective-permute-start(bf16[496,128]{1,0:T(8,128)(2,1)S(1)} %get-tuple-element.63), channel_id=1, source_target_pairs={{0,4},{2,6},{4,0},{6,2},{8,12},{10,14},{12,8},{14,10},{16,20},{18,... | collective-permute-start | bytes 380936 | tf_op jit(solution)/shard_map/ppermute | solution.py:495
  25.6 0.0 collective-permute-start.7
  25.6 1.7 %outputs.1 = (bf16[64,96]{1,0:T(8,128)(2,1)}, bf16[512,96]{1,0:T(8,128)(2,1)}) custom-call(bf16[512,128]{1,0:T(8,128)(2,1)S(1)} %get-tuple-element.44.x_ref, bf16[128,128]{1,0:T(8,128)(2,1)S(1)} %get-tuple-element.45.u_ref, bf16[800,128]{1,0:T(8,128)(2,1)S(1)} %get-tuple-element.65.gp_ref, f32[512,128]{1,0:T(8,128)S(1)} %get-tuple-element.66.gs_ref, ...), custom_call_target="tpu_custom_call" | custom-call | flops 5000000000 | bytes 4000000 | tf_op jit(solution)/shard_map/outputs/pallas_call | solution.py:27
  27.3 0.0 collective-permute-done.5.a_ref
  27.3 2.6 %collective-permute-done.6.b_ref = bf16[496,128]{1,0:T(8,128)(2,1)S(1)} collective-permute-done((bf16[496,128]{1,0:T(8,128)(2,1)S(1)}, bf16[496,128]{1,0:T(8,128)(2,1)S(1)}, u32[]{:S(2)}, u32[]{:S(2)}) %collective-permute-start.6) | collective-permute-done | bytes 127008 | tf_op jit(solution)/shard_map/ppermute | solution.py:495
  29.9 1.7 %collective-permute-done.7.c_ref = bf16[496,128]{1,0:T(8,128)(2,1)S(1)} collective-permute-done((bf16[496,128]{1,0:T(8,128)(2,1)S(1)}, bf16[496,128]{1,0:T(8,128)(2,1)S(1)}, u32[]{:S(2)}, u32[]{:S(2)}) %collective-permute-start.7) | collective-permute-done | bytes 127008 | tf_op jit(solution)/shard_map/ppermute | solution.py:495
  31.6 0.1 sum.1
  31.7 2.9 %collective-permute-start.8 = (bf16[496,128]{1,0:T(8,128)(2,1)S(1)}, bf16[496,128]{1,0:T(8,128)(2,1)S(1)}, u32[]{:S(2)}, u32[]{:S(2)}) collective-permute-start(bf16[496,128]{1,0:T(8,128)(2,1)S(1)} %sum.1), channel_id=1, source_target_pairs={{0,8},{4,12},{8,0},{12,4},{16,24},{20,28},{24,16},{28,20},{1,9},{5... | collective-permute-start | bytes 380936 | tf_op jit(solution)/shard_map/ppermute | solution.py:509
  34.5 2.9 %collective-permute-done.8 = bf16[496,128]{1,0:T(8,128)(2,1)S(1)} collective-permute-done((bf16[496,128]{1,0:T(8,128)(2,1)S(1)}, bf16[496,128]{1,0:T(8,128)(2,1)S(1)}, u32[]{:S(2)}, u32[]{:S(2)}) %collective-permute-start.8) | collective-permute-done | bytes 127008 | tf_op jit(solution)/shard_map/ppermute | solution.py:509
  37.5 3.1 %collective-permute-start.9 = (bf16[496,128]{1,0:T(8,128)(2,1)S(1)}, bf16[496,128]{1,0:T(8,128)(2,1)S(1)}, u32[]{:S(2)}, u32[]{:S(2)}) collective-permute-start(bf16[496,128]{1,0:T(8,128)(2,1)S(1)} %add_convert_fusion.1), channel_id=1, source_target_pairs={{0,16},{4,20},{8,24},{12,28},{16,0},{20,4},{24,8},{28,12},{1,17},{... | collective-permute-start | bytes 380936 | tf_op jit(solution)/shard_map/ppermute | solution.py:509
  40.6 4.4 %collective-permute-done.9 = bf16[496,128]{1,0:T(8,128)(2,1)S(1)} collective-permute-done((bf16[496,128]{1,0:T(8,128)(2,1)S(1)}, bf16[496,128]{1,0:T(8,128)(2,1)S(1)}, u32[]{:S(2)}, u32[]{:S(2)}) %collective-permute-start.9) | collective-permute-done | bytes 127008 | tf_op jit(solution)/shard_map/ppermute | solution.py:509
  45.0 1.9 %collective-permute-start.12 = (bf16[496,128]{1,0:T(8,128)(2,1)S(1)}, bf16[496,128]{1,0:T(8,128)(2,1)S(1)}, u32[]{:S(2)}, u32[]{:S(2)}) collective-permute-start(bf16[496,128]{1,0:T(8,128)(2,1)S(1)} %add_convert_fusion.refs_0_), channel_id=1, source_target_pairs={{0,6},{2,4},{4,2},{6,0},{8,14},{10,12},{12,10},{14,8},{16,22},{18,... | collective-permute-start | bytes 380936 | tf_op jit(solution)/shard_map/ppermute | solution.py:495
  46.9 0.0 collective-permute-start.11
  46.9 1.7 %collective-permute-start.10 = (bf16[496,128]{1,0:T(8,128)(2,1)S(1)}, bf16[496,128]{1,0:T(8,128)(2,1)S(1)}, u32[]{:S(2)}, u32[]{:S(2)}) collective-permute-start(bf16[496,128]{1,0:T(8,128)(2,1)S(1)} %add_convert_fusion.refs_0_), channel_id=1, source_target_pairs={{0,2},{2,0},{4,6},{6,4},{8,10},{10,8},{12,14},{14,12},{16,18},{18,... | collective-permute-start | bytes 380936 | tf_op jit(solution)/shard_map/ppermute | solution.py:495
  48.6 0.0 collective-permute-start.13
  48.6 2.4 %collective-permute-done.12.refs_3_ = bf16[496,128]{1,0:T(8,128)(2,1)S(1)} collective-permute-done((bf16[496,128]{1,0:T(8,128)(2,1)S(1)}, bf16[496,128]{1,0:T(8,128)(2,1)S(1)}, u32[]{:S(2)}, u32[]{:S(2)}) %collective-permute-start.12) | collective-permute-done | bytes 127008 | tf_op jit(solution)/shard_map/ppermute | solution.py:495
  51.0 0.0 collective-permute-start.16
  51.0 0.9 %collective-permute-done.11.refs_2_ = bf16[496,128]{1,0:T(8,128)(2,1)S(1)} collective-permute-done((bf16[496,128]{1,0:T(8,128)(2,1)S(1)}, bf16[496,128]{1,0:T(8,128)(2,1)S(1)}, u32[]{:S(2)}, u32[]{:S(2)}) %collective-permute-start.11) | collective-permute-done | bytes 127008 | tf_op jit(solution)/shard_map/ppermute | solution.py:495
  51.8 0.0 collective-permute-start.15
  51.8 0.4 collective-permute-done.10.refs_1_
  52.3 0.1 collective-permute-start.14
  52.3 0.0 collective-permute-done.13.refs_4_
  52.3 0.0 collective-permute-done.16.refs_7_
  52.3 0.8 %collective-permute-done.15.refs_6_ = bf16[496,128]{1,0:T(8,128)(2,1)S(1)} collective-permute-done((bf16[496,128]{1,0:T(8,128)(2,1)S(1)}, bf16[496,128]{1,0:T(8,128)(2,1)S(1)}, u32[]{:S(2)}, u32[]{:S(2)}) %collective-permute-start.15) | collective-permute-done | bytes 127008 | tf_op jit(solution)/shard_map/ppermute | solution.py:512
  53.2 0.5 collective-permute-done.14.refs_5_
  53.6 1.9 %last.1 = (f32[27,96,96]{2,1,0:T(8,128)}, f32[27,96,96]{2,1,0:T(8,128)}, f32[1,96]{1,0:T(1,128)}) custom-call(bf16[496,128]{1,0:T(8,128)(2,1)S(1)} %add_convert_fusion.refs_0_, bf16[496,128]{1,0:T(8,128)(2,1)S(1)} %collective-permute-done.10.refs_1_, bf16[496,128]{1,0:T(8,128)(2,1)S(1)} %collective-permute-done.11.refs_2_, ...), custom_call_target="tpu_custom_call" | custom-call | tf_op jit(solution)/shard_map/last/pallas_call | solution.py:27
  (2 shorter events, 0.1 us)
Async XLA Ops:
  1.7 3.0 %collective-permute-start = (bf16[160,128]{1,0:T(8,128)(2,1)S(1)}, bf16[160,128]{1,0:T(8,128)(2,1)S(1)}, u32[]{:S(2)}, u32[]{:S(2)}) collective-permute-start(bf16[160,128]{1,0:T(8,128)(2,1)S(1)} %get-tuple-element.46), channel_id=1, source_target_pairs={{0,1},{1,0},{2,3},{3,2},{4,5},{5,4},{6,7},{7,6},{8,9},{9,8},{10,11... | collective-permute-start | bytes 122888 | tf_op jit(solution)/shard_map/ppermute | solution.py:404
  2.3 2.4 %collective-permute-start.1 = (bf16[160,128]{1,0:T(8,128)(2,1)S(1)}, bf16[160,128]{1,0:T(8,128)(2,1)S(1)}, u32[]{:S(2)}, u32[]{:S(2)}) collective-permute-start(bf16[160,128]{1,0:T(8,128)(2,1)S(1)} %get-tuple-element.47), channel_id=1, source_target_pairs={{1,2},{2,1},{5,6},{6,5},{9,10},{10,9},{13,14},{14,13},{17,18},{18,... | collective-permute-start | bytes 122888 | tf_op jit(solution)/shard_map/ppermute | solution.py:405
  4.8 4.8 %collective-permute-start.2 = (bf16[240,128]{1,0:T(8,128)(2,1)S(1)}, bf16[240,128]{1,0:T(8,128)(2,1)S(1)}, u32[]{:S(2)}, u32[]{:S(2)}) collective-permute-start(bf16[240,128]{1,0:T(8,128)(2,1)S(1)} %get-tuple-element.55), channel_id=1, source_target_pairs={{0,4},{4,0},{8,12},{12,8},{16,20},{20,16},{24,28},{28,24},{1,5},{5... | collective-permute-start | bytes 184328 | tf_op jit(solution)/shard_map/ppermute | solution.py:431
  7.3 2.2 %collective-permute-start.3 = (bf16[240,128]{1,0:T(8,128)(2,1)S(1)}, bf16[240,128]{1,0:T(8,128)(2,1)S(1)}, u32[]{:S(2)}, u32[]{:S(2)}) collective-permute-start(bf16[240,128]{1,0:T(8,128)(2,1)S(1)} %get-tuple-element.56), channel_id=1, source_target_pairs={{4,8},{12,16},{20,24},{8,4},{16,12},{24,20},{5,9},{13,17},{21,25},... | collective-permute-start | bytes 184328 | tf_op jit(solution)/shard_map/ppermute | solution.py:430
  13.8 4.1 %collective-permute-start.4 = (bf16[1984,128]{1,0:T(8,128)(2,1)S(1)}, bf16[1984,128]{1,0:T(8,128)(2,1)S(1)}, u32[]{:S(2)}, u32[]{:S(2)}) collective-permute-start(bf16[1984,128]{1,0:T(8,128)(2,1)S(1)} %get-tuple-element.61), channel_id=1, source_target_pairs={{0,1},{1,0},{2,3},{3,2},{4,5},{5,4},{6,7},{7,6},{8,9},{9,8},{10,11... | collective-permute-start | bytes 1523720 | tf_op jit(solution)/shard_map/ppermute | solution.py:480
  18.0 9.4 %collective-permute-start.5 = (bf16[496,128]{1,0:T(8,128)(2,1)S(1)}, bf16[496,128]{1,0:T(8,128)(2,1)S(1)}, u32[]{:S(2)}, u32[]{:S(2)}) collective-permute-start(bf16[496,128]{1,0:T(8,128)(2,1)S(1)} %get-tuple-element.62), channel_id=1, source_target_pairs={{0,2},{2,0},{4,6},{6,4},{8,10},{10,8},{12,14},{14,12},{16,18},{18,... | collective-permute-start | bytes 380936 | tf_op jit(solution)/shard_map/ppermute | solution.py:495
  20.9 9.1 %collective-permute-start.6 = (bf16[496,128]{1,0:T(8,128)(2,1)S(1)}, bf16[496,128]{1,0:T(8,128)(2,1)S(1)}, u32[]{:S(2)}, u32[]{:S(2)}) collective-permute-start(bf16[496,128]{1,0:T(8,128)(2,1)S(1)} %get-tuple-element.63), channel_id=1, source_target_pairs={{0,4},{2,6},{4,0},{6,2},{8,12},{10,14},{12,8},{14,10},{16,20},{18,... | collective-permute-start | bytes 380936 | tf_op jit(solution)/shard_map/ppermute | solution.py:495
  25.6 5.9 %collective-permute-start.7 = (bf16[496,128]{1,0:T(8,128)(2,1)S(1)}, bf16[496,128]{1,0:T(8,128)(2,1)S(1)}, u32[]{:S(2)}, u32[]{:S(2)}) collective-permute-start(bf16[496,128]{1,0:T(8,128)(2,1)S(1)} %get-tuple-element.64), channel_id=1, source_target_pairs={{0,6},{2,4},{4,2},{6,0},{8,14},{10,12},{12,10},{14,8},{16,22},{18,... | collective-permute-start | bytes 380936 | tf_op jit(solution)/shard_map/ppermute | solution.py:495
  31.7 5.8 %collective-permute-start.8 = (bf16[496,128]{1,0:T(8,128)(2,1)S(1)}, bf16[496,128]{1,0:T(8,128)(2,1)S(1)}, u32[]{:S(2)}, u32[]{:S(2)}) collective-permute-start(bf16[496,128]{1,0:T(8,128)(2,1)S(1)} %sum.1), channel_id=1, source_target_pairs={{0,8},{4,12},{8,0},{12,4},{16,24},{20,28},{24,16},{28,20},{1,9},{5... | collective-permute-start | bytes 380936 | tf_op jit(solution)/shard_map/ppermute | solution.py:509
  37.5 7.5 %collective-permute-start.9 = (bf16[496,128]{1,0:T(8,128)(2,1)S(1)}, bf16[496,128]{1,0:T(8,128)(2,1)S(1)}, u32[]{:S(2)}, u32[]{:S(2)}) collective-permute-start(bf16[496,128]{1,0:T(8,128)(2,1)S(1)} %add_convert_fusion.1), channel_id=1, source_target_pairs={{0,16},{4,20},{8,24},{12,28},{16,0},{20,4},{24,8},{28,12},{1,17},{... | collective-permute-start | bytes 380936 | tf_op jit(solution)/shard_map/ppermute | solution.py:509
  45.0 5.9 %collective-permute-start.12 = (bf16[496,128]{1,0:T(8,128)(2,1)S(1)}, bf16[496,128]{1,0:T(8,128)(2,1)S(1)}, u32[]{:S(2)}, u32[]{:S(2)}) collective-permute-start(bf16[496,128]{1,0:T(8,128)(2,1)S(1)} %add_convert_fusion.refs_0_), channel_id=1, source_target_pairs={{0,6},{2,4},{4,2},{6,0},{8,14},{10,12},{12,10},{14,8},{16,22},{18,... | collective-permute-start | bytes 380936 | tf_op jit(solution)/shard_map/ppermute | solution.py:495
  46.9 4.9 %collective-permute-start.11 = (bf16[496,128]{1,0:T(8,128)(2,1)S(1)}, bf16[496,128]{1,0:T(8,128)(2,1)S(1)}, u32[]{:S(2)}, u32[]{:S(2)}) collective-permute-start(bf16[496,128]{1,0:T(8,128)(2,1)S(1)} %add_convert_fusion.refs_0_), channel_id=1, source_target_pairs={{0,4},{2,6},{4,0},{6,2},{8,12},{10,14},{12,8},{14,10},{16,20},{18,... | collective-permute-start | bytes 380936 | tf_op jit(solution)/shard_map/ppermute | solution.py:495
  46.9 5.4 %collective-permute-start.10 = (bf16[496,128]{1,0:T(8,128)(2,1)S(1)}, bf16[496,128]{1,0:T(8,128)(2,1)S(1)}, u32[]{:S(2)}, u32[]{:S(2)}) collective-permute-start(bf16[496,128]{1,0:T(8,128)(2,1)S(1)} %add_convert_fusion.refs_0_), channel_id=1, source_target_pairs={{0,2},{2,0},{4,6},{6,4},{8,10},{10,8},{12,14},{14,12},{16,18},{18,... | collective-permute-start | bytes 380936 | tf_op jit(solution)/shard_map/ppermute | solution.py:495
  48.6 3.8 %collective-permute-start.13 = (bf16[496,128]{1,0:T(8,128)(2,1)S(1)}, bf16[496,128]{1,0:T(8,128)(2,1)S(1)}, u32[]{:S(2)}, u32[]{:S(2)}) collective-permute-start(bf16[496,128]{1,0:T(8,128)(2,1)S(1)} %add_convert_fusion.refs_0_), channel_id=1, source_target_pairs={{0,1},{1,0},{2,3},{3,2},{4,5},{5,4},{6,7},{7,6},{8,9},{9,8},{10,11... | collective-permute-start | bytes 380936 | tf_op jit(solution)/shard_map/ppermute | solution.py:512
  51.0 1.4 %collective-permute-start.16 = (bf16[496,128]{1,0:T(8,128)(2,1)S(1)}, bf16[496,128]{1,0:T(8,128)(2,1)S(1)}, u32[]{:S(2)}, u32[]{:S(2)}) collective-permute-start(bf16[496,128]{1,0:T(8,128)(2,1)S(1)} %collective-permute-done.12.refs_3_), channel_id=1, source_target_pairs={{0,1},{1,0},{2,3},{3,2},{4,5},{5,4},{6,7},{7,6},{8,9},{9,8},{10,11... | collective-permute-start | bytes 380936 | tf_op jit(solution)/shard_map/ppermute | solution.py:512
  51.8 1.3 %collective-permute-start.15 = (bf16[496,128]{1,0:T(8,128)(2,1)S(1)}, bf16[496,128]{1,0:T(8,128)(2,1)S(1)}, u32[]{:S(2)}, u32[]{:S(2)}) collective-permute-start(bf16[496,128]{1,0:T(8,128)(2,1)S(1)} %collective-permute-done.11.refs_2_), channel_id=1, source_target_pairs={{0,1},{1,0},{2,3},{3,2},{4,5},{5,4},{6,7},{7,6},{8,9},{9,8},{10,11... | collective-permute-start | bytes 380936 | tf_op jit(solution)/shard_map/ppermute | solution.py:512
  52.3 1.3 %collective-permute-start.14 = (bf16[496,128]{1,0:T(8,128)(2,1)S(1)}, bf16[496,128]{1,0:T(8,128)(2,1)S(1)}, u32[]{:S(2)}, u32[]{:S(2)}) collective-permute-start(bf16[496,128]{1,0:T(8,128)(2,1)S(1)} %collective-permute-done.10.refs_1_), channel_id=1, source_target_pairs={{0,1},{1,0},{2,3},{3,2},{4,5},{5,4},{6,7},{7,6},{8,9},{9,8},{10,11... | collective-permute-start | bytes 380936 | tf_op jit(solution)/shard_map/ppermute | solution.py:512

commit v4 on v3

--- a/solution.py
+++ b/solution.py
@@ -9,6 +9,7 @@
 from jax.sharding import Mesh
 from jax.sharding import PartitionSpec as P
 
+
 LANES = 128
 F32 = jnp.float32
 BF16 = jnp.bfloat16
@@ -17,7 +18,7 @@
 MIB = 1024 * 1024
 
 
-def call(body, outs, args, scratch=(), cost=None, name=None, vmem=8, far=(), far_outs=False, sems=0):
+def call(body, outs, args, scratch=(), cost=None, vmem=8, far=(), far_outs=False, sems=0):
     near_spec = pl.BlockSpec(memory_space=pltpu.VMEM)
     far_spec = pl.BlockSpec(memory_space=pltpu.HBM)
     args = [
@@ -33,7 +34,6 @@
         + ([pltpu.SemaphoreType.DMA((sems,))] if sems else []),
         compiler_params=pltpu.CompilerParams(vmem_limit_bytes=vmem * MIB),
         cost_estimate=cost,
-        name=name,
     )(*args)
 
 
@@ -185,14 +185,106 @@
     return jnp.concatenate([packed, tail], axis=0)
 
 
+def fine_gradient(rows, wd, picks):
+    wins = [win.reshape(rows, LANES).astype(BF16) for _, win, _ in picks]
+    taps = [wd[a * 3 + b] for a, _, b in picks]
+    return lax.dot_general(
+        jnp.concatenate(wins, axis=1), jnp.concatenate(taps, axis=1), NT,
+        preferred_element_type=F32,
+    )
+
+
+def z_sum(out, lower, upper):
+    low, same, high = three(out)
+    return lower(low) + same + upper(high)
+
+
+def unit(v, bias, x, g, ch):
+    v = v + bias[...].reshape(1, 1, LANES)
+    live = jnp.broadcast_to(x[:, :, ch : ch + 1], x.shape)
+    s = 1.0 / (1.0 + jnp.exp(-v))
+    summed = (x + live * (v * s)).astype(BF16).astype(F32)
+    grad = (g * live * s * (1.0 + v * (1.0 - s))).astype(BF16).astype(F32)
+    return summed, grad
+
+
+def with_ones(win, a, b, ch):
+    if a == 1 and b == 1:
+        win = jnp.where(lane_of(win.shape) == ch + 1, 1.0, win)
+    return win
+
+
+def z_taps(other):
+    cells = other.shape[0] * other.shape[1]
+    other = jnp.concatenate([above(other), other, below(other)], axis=2)
+    return other.reshape(cells, 3 * LANES).astype(BF16)
+
+
+TERMS = {0: ((2, 0), (0, 1)), 1: ((1, 1),)}
+
+
+def inner_kernel(
+    dims, x_ref, u_ref, core_ref, side_ref, wf, wd, bias, gp_ref, s_ref, gs_ref, acc_ref,
+    xe, ue, pre, gsr, gp,
+):
+    tx, ty, tz, ch = dims
+    hx, hy = tx // 2, ty // 2
+    ey, inner = ty + 2, tx - 2
+    widen(dims, x_ref, u_ref, core_ref, side_ref, xe, ue, 0, 0)
+    wins = [
+        xe[a : a + inner, b : b + ey].reshape(inner * ey * tz, LANES).astype(BF16)
+        for a in range(3)
+        for b in range(3)
+    ]
+    out = jnp.dot(jnp.concatenate(wins, axis=1), wf[...], preferred_element_type=F32)
+    out = z_sum(out.reshape(inner * ey, tz, 3 * LANES), below, above)
+    pre[...] = out.reshape(inner, ey, tz, LANES)
+    for px in (0, 1):
+        for py in (0, 1):
+            picks = [
+                (a, ue[sx : sx + hx - 1, sy : sy + hy + 1], b)
+                for a, sx in TERMS[px]
+                for b, sy in TERMS[py]
+            ]
+            out = fine_gradient((hx - 1) * (hy + 1) * tz, wd, picks)
+            out = z_sum(out.reshape((hx - 1) * (hy + 1), tz, 3 * LANES), above, below)
+            gsr[:, px, :, py] = out.reshape(hx - 1, hy + 1, tz, LANES)
+
+    def pointwise(i, _):
+        g = gsr[i // 2, lax.rem(i, 2)].reshape(ey, tz, LANES)
+        summed, grad = unit(pre[i], bias, xe[i + 1, 1 : 1 + ey], g, ch)
+        at = pl.ds(pl.multiple_of(i * ey * tz, 16), ey * tz)
+        s_ref[at] = summed.reshape(ey * tz, LANES).astype(BF16)
+        gp_ref[at] = grad.reshape(ey * tz, LANES).astype(BF16)
+        gp[i] = grad
+        return 0
+
+    lax.fori_loop(0, inner, pointwise, 0)
+    gs_ref[...] = gsr[...].reshape(inner, ey, tz, LANES)[:, 1 : 1 + ty].reshape(
+        inner * ty * tz, LANES
+    )
+    other = z_taps(gp[:, 1 : 1 + ty].reshape(inner * ty, tz, LANES))
+    for a in range(3):
+        wins = [
+            with_ones(xe[a : a + inner, b + 1 : b + 1 + ty], a, b, ch)
+            .reshape(inner * ty * tz, LANES)
+            .astype(BF16)
+            for b in range(3)
+        ]
+        acc_ref[a * 3 * LANES : (a + 1) * 3 * LANES] = lax.dot_general(
+            jnp.concatenate(wins, axis=1), other, TN, preferred_element_type=F32
+        )
+
+
 def main_kernel(
-    dims, x_ref, u_ref, core_ref, side_ref, near_ref, far_ref, wf, wd, bias,
-    keep_ref, send_ref, gp_ref, gs_ref, s_ref,
-    xe, ue, ss, acc, gsr, gp, pack,
+    dims, x_ref, u_ref, core_ref, side_ref, near_ref, far_ref, wf, wd, bias, gpa_ref, sa_ref, acc_ref,
+    keep_ref, send_ref, gpb_ref, sb_ref, gsb_ref,
+    xe, ue, ss, pre, gsr, edge, pack,
 ):
     tx, ty, tz, ch = dims
     hx, hy = tx // 2, ty // 2
     ex, ey = tx + 2, ty + 2
+    slab = ey * tz
     block_rows = ch * ch // LANES
     core = lax.axis_index("core")
     odd = lax.rem(lax.axis_index("gx"), 2)
@@ -201,60 +293,47 @@
     for ref, low in ((near_ref, odd), (far_ref, 1 - odd)):
         xe[pl.ds((1 - low) * (tx + 2), 2)] = ref[:rows].astype(F32).reshape(2, ty + 4, tz, LANES)
         ue[pl.ds((1 - low) * (hx + 1), 1)] = ref[rows:].astype(F32).reshape(1, hy + 2, tz, LANES)
-
-    part = ex // 2
-
-    def forward(h, _):
-        wins = [
-            xe[pl.ds(h * part + a, part), b : b + ey].reshape(part * ey * tz, LANES).astype(BF16)
-            for a in range(3)
-            for b in range(3)
-        ]
-        out = jnp.dot(jnp.concatenate(wins, axis=1), wf[...], preferred_element_type=F32)
-        lower, same, upper = three(out.reshape(part * ey, tz, 3 * LANES))
-        out = below(lower) + same + above(upper)
-        acc[pl.ds(h * part, part)] = out.reshape(part, ey, tz, LANES)
-        return 0
-
-    lax.fori_loop(0, 2, forward, 0)
-
-    terms = {0: ((2, 0), (0, 1)), 1: ((1, 1),)}
+    ss[1:hx] = sa_ref[...].astype(F32).reshape(hx - 1, 2, hy + 1, 2, tz, LANES)
+
+    def edges(v, a, lower, upper):
+        return jnp.concatenate([v[lower + a : lower + a + 2], v[upper + a : upper + a + 2]], axis=0)
+
+    wins = [
+        edges(xe, a, 0, ex - 2)[:, b : b + ey].reshape(4 * slab, LANES).astype(BF16)
+        for a in range(3)
+        for b in range(3)
+    ]
+    out = jnp.dot(jnp.concatenate(wins, axis=1), wf[...], preferred_element_type=F32)
+    out = z_sum(out.reshape(4 * ey, tz, 3 * LANES), below, above)
+    pre[...] = out.reshape(4, ey, tz, LANES)
     for px in (0, 1):
         for py in (0, 1):
-            wins, taps = [], []
-            for a, sx in terms[px]:
-                for b, sy in terms[py]:
-                    win = ue[sx : sx + hx + 1, sy : sy + hy + 1]
-                    wins.append(win.reshape((hx + 1) * (hy + 1) * tz, LANES).astype(BF16))
-                    taps.append(wd[a * 3 + b])
-            out = lax.dot_general(
-                jnp.concatenate(wins, axis=1), jnp.concatenate(taps, axis=1), NT,
-                preferred_element_type=F32,
-            )
-            lower, same, upper = three(out.reshape((hx + 1) * (hy + 1), tz, 3 * LANES))
-            out = above(lower) + same + below(upper)
-            gsr[:, px, :, py] = out.reshape(hx + 1, hy + 1, tz, LANES)
-
-    def pointwise(i, _):
-        v = acc[i] + bias[...].reshape(1, 1, LANES)
-        x = xe[i + 1, 1 : 1 + ey]
-        live = jnp.broadcast_to(x[:, :, ch : ch + 1], x.shape)
-        s = 1.0 / (1.0 + jnp.exp(-v))
-        summed = (x + live * (v * s)).astype(BF16).astype(F32)
-        ss[i // 2, lax.rem(i, 2)] = summed.reshape(hy + 1, 2, tz, LANES)
-        g = gsr[i // 2, lax.rem(i, 2)].reshape(ey, tz, LANES)
-        gp[i] = (g * live * s * (1.0 + v * (1.0 - s))).astype(BF16).astype(F32)
-        return 0
-
-    lax.fori_loop(0, ex, pointwise, 0)
-
-    def gradients(h, wins, other):
-        cells = other.shape[0] * other.shape[1]
-        other = jnp.concatenate([above(other), other, below(other)], axis=2)
-        other = other.reshape(cells, 3 * LANES).astype(BF16)
+            picks = []
+            for a, sx in TERMS[px]:
+                for b, sy in TERMS[py]:
+                    win = jnp.concatenate(
+                        [ue[sx, sy : sy + hy + 1], ue[hx + sx, sy : sy + hy + 1]], axis=0
+                    )
+                    picks.append((a, win, b))
+            out = fine_gradient(2 * (hy + 1) * tz, wd, picks)
+            out = z_sum(out.reshape(2 * (hy + 1), tz, 3 * LANES), above, below)
+            gsr[:, px, :, py] = out.reshape(2, hy + 1, tz, LANES)
+    for j, i in enumerate((0, 1, ex - 2, ex - 1)):
+        g = gsr[j // 2, j % 2].reshape(ey, tz, LANES)
+        summed, grad = unit(pre[j], bias, xe[i + 1, 1 : 1 + ey], g, ch)
+        ss[i // 2, i % 2] = summed.reshape(hy + 1, 2, tz, LANES)
+        sb_ref[j * slab : (j + 1) * slab] = summed.reshape(slab, LANES).astype(BF16)
+        gpb_ref[j * slab : (j + 1) * slab] = grad.reshape(slab, LANES).astype(BF16)
+        if j in (1, 2):
+            edge[j - 1] = grad[1 : 1 + ty]
+            gsb_ref[(j - 1) * ty * tz : j * ty * tz] = g[1 : 1 + ty].reshape(ty * tz, LANES)
+
+    def gradients(h, wins, other, before):
         for a in range(3):
             win = jnp.concatenate([wins(a, b) for b in range(3)], axis=1)
             out = lax.dot_general(win, other, TN, preferred_element_type=F32)
+            if before is not None:
+                out = out + before[a * 3 * LANES : (a + 1) * 3 * LANES]
             for b in range(3):
                 for e in range(3):
                     at = (a * 9 + b * 3 + e) * block_rows
@@ -267,35 +346,37 @@
         pack[h, at:] = jnp.zeros((pack.shape[1] - at, LANES), F32)
 
     def fine_window(a, b):
-        win = xe[a + 1 : a + 1 + tx, b + 1 : b + 1 + ty]
-        if a == 1 and b == 1:
-            win = jnp.where(lane_of(win.shape) == ch + 1, 1.0, win)
-        return win.reshape(tx * ty * tz, LANES).astype(BF16)
+        win = jnp.concatenate(
+            [xe[a + 1, b + 1 : b + 1 + ty], xe[tx + a, b + 1 : b + 1 + ty]], axis=0
+        )
+        return with_ones(win, a, b, ch).reshape(2 * ty * tz, LANES).astype(BF16)
 
     def coarse_window(a, b):
         win = ss[a // 2 : a // 2 + hx, a % 2, b // 2 : b // 2 + hy, b % 2]
         return win.reshape(hx * hy * tz, LANES).astype(BF16)
 
-    gradients(0, fine_window, gp[1 : 1 + tx, 1 : 1 + ty].reshape(tx * ty, tz, LANES))
-    gradients(1, coarse_window, ue[1 : 1 + hx, 1 : 1 + hy].reshape(hx * hy, tz, LANES))
+    gradients(0, fine_window, z_taps(edge[...].reshape(2 * ty, tz, LANES)), acc_ref)
+    own = ue[1 : 1 + hx, 1 : 1 + hy].reshape(hx * hy, tz, LANES)
+    gradients(1, coarse_window, z_taps(own), None)
     keep_ref[...] = pack[core]
     send_ref[...] = pack[1 - core].astype(BF16)
-    gp_ref[...] = gp[...].reshape(ex * ey * tz, LANES).astype(BF16)
-    gs_ref[...] = gsr[...].reshape(ex, ey, tz, LANES)[1 : 1 + tx, 1 : 1 + ty].reshape(
-        tx * ty * tz, LANES
-    )
-    s_ref[...] = ss[...].reshape(ex * ey * tz, LANES).astype(BF16)
 
 
 def second_outputs(
-    dims, x_ref, u_ref, gp_ref, gs_ref, s_ref, wf, wd, down_ref, gv_ref,
+    dims, x_ref, u_ref, gpa_ref, gpb_ref, gsa_ref, gsb_ref, sa_ref, sb_ref, wf, wd, down_ref, gv_ref,
     ge, ss, accd,
 ):
     tx, ty, tz, ch = dims
     hx, hy = tx // 2, ty // 2
     ex, ey = tx + 2, ty + 2
-    ge[...] = gp_ref[...].astype(F32).reshape(ex, ey, tz, LANES)
-    ss[...] = s_ref[...].astype(F32).reshape(hx + 1, 2, hy + 1, 2, tz, LANES)
+    slab = ey * tz
+    ge[2:tx] = gpa_ref[...].astype(F32).reshape(tx - 2, ey, tz, LANES)
+    ss[1:hx] = sa_ref[...].astype(F32).reshape(hx - 1, 2, hy + 1, 2, tz, LANES)
+    for j, i in enumerate((0, 1, ex - 2, ex - 1)):
+        ge[i] = gpb_ref[j * slab : (j + 1) * slab].astype(F32).reshape(ey, tz, LANES)
+        ss[i // 2, i % 2] = (
+            sb_ref[j * slab : (j + 1) * slab].astype(F32).reshape(hy + 1, 2, tz, LANES)
+        )
     wins = [
         ss[a // 2 : a // 2 + hx, a % 2, b // 2 : b // 2 + hy, b % 2]
         .reshape(hx * hy * tz, LANES)
@@ -304,8 +385,7 @@
         for b in range(3)
     ]
     out = jnp.dot(jnp.concatenate(wins, axis=1), wd[...], preferred_element_type=F32)
-    lower, same, upper = three(out.reshape(hx * hy, tz, 3 * LANES))
-    out = (below(lower) + same + above(upper)).reshape(hx * hy * tz, LANES)
+    out = z_sum(out.reshape(hx * hy, tz, 3 * LANES), below, above).reshape(hx * hy * tz, LANES)
     u = u_ref[...].astype(F32)
     accd[...] = out * jnp.broadcast_to(u[:, ch : ch + 1], u.shape)
     down_ref[...] = accd[pl.ds(0, hx * hy * tz // 2, stride=2), :][:, :ch].astype(BF16)
@@ -316,14 +396,13 @@
         for b in range(3)
     ]
     taps = jnp.concatenate([wf[ab] for ab in range(9)], axis=1)
-    out = lax.dot_general(
-        jnp.concatenate(wins, axis=1), taps, NT, preferred_element_type=F32
-    )
-    lower, same, upper = three(out.reshape(tx * ty, tz, 3 * LANES))
-    out = (above(lower) + same + below(upper)).reshape(tx * ty * tz, LANES)
+    out = lax.dot_general(jnp.concatenate(wins, axis=1), taps, NT, preferred_element_type=F32)
+    out = z_sum(out.reshape(tx * ty, tz, 3 * LANES), above, below).reshape(tx * ty * tz, LANES)
     x = x_ref[...].astype(F32)
     live = jnp.broadcast_to(x[:, ch : ch + 1], x.shape)
-    gv_ref[...] = ((gs_ref[...] + out) * live)[:, :ch].astype(BF16)
+    column = ty * tz
+    grad = jnp.concatenate([gsb_ref[:column], gsa_ref[...], gsb_ref[column:]], axis=0)
+    gv_ref[...] = ((grad + out) * live)[:, :ch].astype(BF16)
 
 
 def split_kernel(keep_ref, got_ref, own_ref, *to_refs):
@@ -392,7 +471,6 @@
             ((tx * ty, tz), jnp.int32),
             ((hx * hy * hz, ch), BF16),
         ],
-        name="first",
         vmem=4,
         far=(0, 1, 2),
         sems=3,
@@ -409,7 +487,6 @@
         [in_lanes, in_rows, ((1, LANES), F32), ((27, ch, ch), BF16), ((27, ch, ch), BF16)],
         (conv_weight, down_weight, conv_bias.reshape(1, ch)),
         [((1, ch), F32)],
-        name="weights",
         vmem=4,
         far=(0, 1, 2),
         sems=3,
@@ -421,34 +498,52 @@
         [((row_rows, LANES), BF16)] * 2,
         (x, u, from_core, from_side),
         [((tx, ty + 4, tz, LANES), F32), ((hx, hy + 2, tz, LANES), F32)],
-        name="second",
         vmem=4,
     )
     near = [(i, i ^ 1) for i in range(n_gx)]
     far = [(i, i + 1) for i in range(1, n_gx - 1, 2)]
     far += [(j, i) for i, j in far]
+    from_near = lax.ppermute(to_near, "gx", near)
     from_far = lax.ppermute(to_far, "gx", far)
-    from_near = lax.ppermute(to_near, "gx", near)
+    inner = tx - 2
+    *results, = call(
+        functools.partial(inner_kernel, dims),
+        [((inner * ey * tz, LANES), BF16)] * 2
+        + [((inner * ty * tz, LANES), F32), ((9 * LANES, 3 * LANES), F32)],
+        (x, u, from_core, from_side, conv_lanes, down_rows, bias),
+        [
+            ((tx, ty + 4, tz, LANES), F32),
+            ((hx, hy + 2, tz, LANES), F32),
+            ((inner, ey, tz, LANES), F32),
+            ((hx - 1, 2, hy + 1, 2, tz, LANES), F32),
+            ((inner, ey, tz, LANES), F32),
+        ],
+        cost=pl.CostEstimate(flops=5_000_000_000, bytes_accessed=4_000_000, transcendentals=0),
+        vmem=12,
+    )
+    from_far, from_near, *results = lax.optimization_barrier((from_far, from_near, *results))
+    gp_inner, s_inner, gs_inner, acc = results
 
     block_rows = ch * ch // LANES
     half_rows = -(-(27 * block_rows + 8) // 64) * 64
-    keep, send, gp, gs, s = call(
+    keep, send, gp_edge, s_edge, gs_edge = call(
         functools.partial(main_kernel, dims),
         [((half_rows, LANES), F32), ((half_rows, LANES), BF16)]
-        + [((ex * ey * tz, LANES), BF16), ((fine, LANES), F32), ((ex * ey * tz, LANES), BF16)],
+        + [((4 * ey * tz, LANES), BF16)] * 2
+        + [((2 * ty * tz, LANES), F32)],
         (
             x, u, from_core, from_side, from_near, from_far, conv_lanes, down_rows, bias,
+            gp_inner, s_inner, acc,
         ),
         [
             ((tx + 4, ty + 4, tz, LANES), F32),
             ((hx + 2, hy + 2, tz, LANES), F32),
             ((hx + 1, 2, hy + 1, 2, tz, LANES), F32),
-            ((ex, ey, tz, LANES), F32),
-            ((hx + 1, 2, hy + 1, 2, tz, LANES), F32),
-            ((ex, ey, tz, LANES), F32),
+            ((4, ey, tz, LANES), F32),
+            ((2, 2, hy + 1, 2, tz, LANES), F32),
+            ((2, ty, tz, LANES), F32),
             ((2, half_rows, LANES), F32),
         ],
-        name="main",
         vmem=16,
     )
 
@@ -456,21 +551,19 @@
         functools.partial(other_weights_kernel, ch),
         [in_rows, in_lanes],
         (raw_conv, raw_down),
-        name="weights2",
         vmem=4,
     )
     conv_rows, down_lanes = rest
     down, grad_voxels = call(
         functools.partial(second_outputs, dims),
         [((hx * hy * hz, ch), BF16), ((fine, ch), BF16)],
-        (x, u, gp, gs, s, conv_rows, down_lanes),
+        (x, u, gp_inner, gp_edge, gs_inner, gs_edge, s_inner, s_edge, conv_rows, down_lanes),
         [
             ((ex, ey, tz, LANES), F32),
             ((hx + 1, 2, hy + 1, 2, tz, LANES), F32),
             ((coarse, LANES), F32),
         ],
         cost=pl.CostEstimate(flops=5_000_000_000, bytes_accessed=4_000_000, transcendentals=0),
-        name="outputs",
         vmem=12,
     )
 
@@ -483,7 +576,6 @@
         split_kernel,
         [((quarter, LANES), F32)] + [((quarter, LANES), BF16)] * 3,
         (keep, got),
-        name="split",
         vmem=2,
     )
 
@@ -496,20 +588,16 @@
 
     arrived = [across(piece, k) for k, piece in zip((1, 2, 3), pieces)]
     *arrived, down, grad_voxels = lax.optimization_barrier((*arrived, down, grad_voxels))
-    (total,) = call(
-        sum_kernel,
-        [((quarter, LANES), BF16)],
-        (mine, *arrived),
-        name="sum",
-        vmem=2,
-    )
+    (total,) = call(sum_kernel, [((quarter, LANES), BF16)], (mine, *arrived), vmem=2)
     for axis, peers in (("gx", n_gx), ("gyc", n_gyc)):
         step = 2
         while step < peers:
             total = plus(total, lax.ppermute(total, axis, [(i, i ^ step) for i in range(peers)]))
             step *= 2
     own = [total] + [across(total, k) for k in (1, 2, 3)]
-    other = [lax.ppermute(piece, "core", swap) for piece in own]
+    other = []
+    for piece in own:
+        other.append(lax.ppermute(piece, "core", swap))
     factor = 1.0 / math.sqrt(tx * n_gx * ty * n_gy * tz)
     grad_conv, grad_down, grad_bias = call(
         functools.partial(last_kernel, ch, factor),
@@ -521,7 +609,6 @@
             ((27, ch, ch), F32),
             ((1, ch), F32),
         ],
-        name="last",
         vmem=10,
         far_outs=True,
         sems=7,
@@ -547,6 +634,7 @@
         P(),
         P("gx", gy, None, None),
     )
+
     return jax.shard_map(
         on_device,
         mesh=split,

time: 55.7 us -> 54.6 us (0.980)
  starting transfers between devices: 24.2 us -> 22.3 us
  waiting for transfers between devices: 19.2 us -> 20 us
    ppermute x6, starting transfers between devices: 11.2 us -> 7.49 us  [across(): return lax.ppermute(value, ('gx', 'gyc'), route)]
    ppermute x1, starting transfers between devices: 2.56 us -> 5.36 us  [on_device(): from_near = lax.ppermute(to_near, 'gx', near)]
    ppermute x6, waiting for transfers between devices: 7.93 us -> 9.98 us  [across(): return lax.ppermute(value, ('gx', 'gyc'), route)]
    ppermute x1, waiting for transfers between devices: 1.54 us -> 0.01 us  [on_device(): from_near = lax.ppermute(to_near, 'gx', near)]
    ppermute x2, starting transfers between devices: 5.95 us -> 4.64 us  [on_device(): lax.ppermute(total, axis, [(i, i ^ step) for i in range(peers)])]
    pallas_call x9 -> x10, Pallas kernels: 11.2 us -> 11.3 us  [call(): pl.pallas_call(body, out_shape=tuple((jax.ShapeDtypeStruct(s, d) for s, d...]
  transfers between devices with their start and end apart: 17 -> 17, of which waited for: 11 -> 10; matrix products, arithmetic and copies ran while one was open for 0% -> 0% of each run, Pallas kernels for 7% -> 11%
where the time goes in v4:
time: 54.6 us; the launch traced here: 54.4 us
  starting transfers between devices  22.3 us (41%)
  waiting for transfers between devices  20 us (37%)
  Pallas kernels  11.3 us (21%)
  between operations  0.75 us (1%)
    pallas_call x10, Pallas kernels, call(): pl.pallas_call(body, out_shape=tuple((jax.ShapeDtypeStruct(s, d) for s, d...  11.3 us
    ppermute x6, waiting for transfers between devices, across(): return lax.ppermute(value, ('gx', 'gyc'), route)  9.98 us
    ppermute x2, waiting for transfers between devices, on_device(): lax.ppermute(total, axis, [(i, i ^ step) for i in range(peers)])  7.6 us
    ppermute x6, starting transfers between devices, across(): return lax.ppermute(value, ('gx', 'gyc'), route)  7.49 us
    ppermute x1, starting transfers between devices, on_device(): from_near = lax.ppermute(to_near, 'gx', near)  5.36 us
    ppermute x2, starting transfers between devices, on_device(): lax.ppermute(total, axis, [(i, i ^ step) for i in range(peers)])  4.64 us
    ppermute x1, starting transfers between devices, on_device(): got = lax.ppermute(send, 'core', swap)  2.88 us
    ppermute x4, waiting for transfers between devices, on_device(): other.append(lax.ppermute(piece, 'core', swap))  1.33 us
  transfers between devices with their start and end apart: 17, of which 10 were waited for; matrix products, arithmetic and copies ran while one was open for 0% of the time, Pallas kernels for 11%

profile of v4, /device:TPU:0, one launch (start us, length us, event | category | flops | bytes accessed | tf_op | source)
XLA Modules:
  0.0 54.4 jit_solution(1903853764846998081)
XLA Ops:
  0.6 1.1 %shard_map.101 = (bf16[512,128]{1,0:T(8,128)(2,1)S(1)}, bf16[128,128]{1,0:T(8,128)(2,1)S(1)}, bf16[160,128]{1,0:T(8,128)(2,1)S(1)}, bf16[160,128]{1,0:T(8,128)(2,1)S(1)}) custom-call(bf16[512,96]{1,0:T(8,128)(2,1)} %bitcast.7, s32[64,8]{1,0:T(8,128)} %bitcast.8, bf16[64,96]{1,0:T(8,128)(2,1)} %bitcast.9), custom_call_target="tpu_custom_call" | custom-call | tf_op jit(solution)/shard_map/pallas_call | solution.py:28
  1.7 0.6 %collective-permute-start = (bf16[160,128]{1,0:T(8,128)(2,1)S(1)}, bf16[160,128]{1,0:T(8,128)(2,1)S(1)}, u32[]{:S(2)}, u32[]{:S(2)}) collective-permute-start(bf16[160,128]{1,0:T(8,128)(2,1)S(1)} %get-tuple-element.56), channel_id=1, source_target_pairs={{0,1},{1,0},{2,3},{3,2},{4,5},{5,4},{6,7},{7,6},{8,9},{9,8},{10,11... | collective-permute-start | bytes 122888 | tf_op jit(solution)/shard_map/ppermute | solution.py:482
  2.3 0.7 %collective-permute-start.1 = (bf16[160,128]{1,0:T(8,128)(2,1)S(1)}, bf16[160,128]{1,0:T(8,128)(2,1)S(1)}, u32[]{:S(2)}, u32[]{:S(2)}) collective-permute-start(bf16[160,128]{1,0:T(8,128)(2,1)S(1)} %get-tuple-element.57), channel_id=1, source_target_pairs={{1,2},{2,1},{5,6},{6,5},{9,10},{10,9},{13,14},{14,13},{17,18},{18,... | collective-permute-start | bytes 122888 | tf_op jit(solution)/shard_map/ppermute | solution.py:483
  2.9 1.7 %shard_map.102 = (bf16[1152,384]{1,0:T(8,128)(2,1)S(1)}, bf16[9,384,128]{2,1,0:T(8,128)(2,1)S(1)}, f32[1,128]{1,0:T(1,128)S(1)}, bf16[27,96,96]{2,1,0:T(8,128)(2,1)S(1)}, bf16[27,96,96]{2,1,0:T(8,128)(2,1)S(1)}) custom-call(bf16[27,96,96]{2,1,0:T(8,128)(2,1)} %cw_far.1, bf16[27,96,96]{2,1,0:T(8,128)(2,1)} %dw_far.1, f32[1,96]{1,0:T(1,128)} %bitcast.10), custom_call_target="tpu_custom_call" | custom-call | tf_op jit(solution)/shard_map/pallas_call | solution.py:28
  4.7 0.0 collective-permute-done.core_ref
  4.7 0.0 collective-permute-done.1.side_ref
  4.7 0.1 shard_map.103
  4.8 0.7 %collective-permute-start.2 = (bf16[240,128]{1,0:T(8,128)(2,1)S(1)}, bf16[240,128]{1,0:T(8,128)(2,1)S(1)}, u32[]{:S(2)}, u32[]{:S(2)}) collective-permute-start(bf16[240,128]{1,0:T(8,128)(2,1)S(1)} %get-tuple-element.65), channel_id=1, source_target_pairs={{4,8},{12,16},{20,24},{8,4},{16,12},{24,20},{5,9},{13,17},{21,25},... | collective-permute-start | bytes 184328 | tf_op jit(solution)/shard_map/ppermute | solution.py:507
  5.4 5.4 %collective-permute-start.3 = (bf16[240,128]{1,0:T(8,128)(2,1)S(1)}, bf16[240,128]{1,0:T(8,128)(2,1)S(1)}, u32[]{:S(2)}, u32[]{:S(2)}) collective-permute-start(bf16[240,128]{1,0:T(8,128)(2,1)S(1)} %get-tuple-element.66), channel_id=1, source_target_pairs={{0,4},{4,0},{8,12},{12,8},{16,20},{20,16},{24,28},{28,24},{1,5},{5... | collective-permute-start | bytes 184328 | tf_op jit(solution)/shard_map/ppermute | solution.py:506
  10.8 2.3 %shard_map.104 = (bf16[480,128]{1,0:T(8,128)(2,1)S(1)}, bf16[480,128]{1,0:T(8,128)(2,1)S(1)}, f32[384,128]{1,0:T(8,128)S(1)}, f32[1152,384]{1,0:T(8,128)S(1)}) custom-call(bf16[512,128]{1,0:T(8,128)(2,1)S(1)} %get-tuple-element.54.x_ref, bf16[128,128]{1,0:T(8,128)(2,1)S(1)} %get-tuple-element.55.u_ref, bf16[160,128]{1,0:T(8,128)(2,1)S(1)} %collective-permute-done.core_ref, ...), custom_call_target="tpu_custom_call" | custom-call | flops 5000000000 | bytes 4000000 | tf_op jit(solution)/shard_map/pallas_call | solution.py:28
  13.1 0.0 collective-permute-done.2.far_ref
  13.1 0.0 collective-permute-done.3.near_ref
  13.1 2.0 %shard_map.105 = (f32[1984,128]{1,0:T(8,128)S(1)}, bf16[1984,128]{1,0:T(8,128)(2,1)S(1)}, bf16[320,128]{1,0:T(8,128)(2,1)S(1)}, bf16[320,128]{1,0:T(8,128)(2,1)S(1)}, f32[128,128]{1,0:T(8,128)S(1)}) custom-call(bf16[512,128]{1,0:T(8,128)(2,1)S(1)} %get-tuple-element.54.x_ref, bf16[128,128]{1,0:T(8,128)(2,1)S(1)} %get-tuple-element.55.u_ref, ...), custom_call_target="tpu_custom_call" | custom-call | tf_op jit(solution)/shard_map/pallas_call | solution.py:28
  15.1 2.9 %collective-permute-start.4 = (bf16[1984,128]{1,0:T(8,128)(2,1)S(1)}, bf16[1984,128]{1,0:T(8,128)(2,1)S(1)}, u32[]{:S(2)}, u32[]{:S(2)}) collective-permute-start(bf16[1984,128]{1,0:T(8,128)(2,1)S(1)} %get-tuple-element.80), channel_id=1, source_target_pairs={{0,1},{1,0},{2,3},{3,2},{4,5},{5,4},{6,7},{7,6},{8,9},{9,8},{10,11... | collective-permute-start | bytes 1523720 | tf_op jit(solution)/shard_map/ppermute | solution.py:573
  18.0 0.4 shard_map.107
  18.4 1.1 %collective-permute-done.4.got_ref = bf16[1984,128]{1,0:T(8,128)(2,1)S(1)} collective-permute-done((bf16[1984,128]{1,0:T(8,128)(2,1)S(1)}, bf16[1984,128]{1,0:T(8,128)(2,1)S(1)}, u32[]{:S(2)}, u32[]{:S(2)}) %collective-permute-start.4) | collective-permute-done | bytes 507936 | tf_op jit(solution)/shard_map/ppermute | solution.py:573
  19.5 0.1 shard_map.106
  19.6 2.0 %collective-permute-start.5 = (bf16[496,128]{1,0:T(8,128)(2,1)S(1)}, bf16[496,128]{1,0:T(8,128)(2,1)S(1)}, u32[]{:S(2)}, u32[]{:S(2)}) collective-permute-start(bf16[496,128]{1,0:T(8,128)(2,1)S(1)} %get-tuple-element.81), channel_id=1, source_target_pairs={{0,2},{2,0},{4,6},{6,4},{8,10},{10,8},{12,14},{14,12},{16,18},{18,... | collective-permute-start | bytes 380936 | tf_op jit(solution)/shard_map/ppermute | solution.py:587
  21.7 1.9 %collective-permute-start.6 = (bf16[496,128]{1,0:T(8,128)(2,1)S(1)}, bf16[496,128]{1,0:T(8,128)(2,1)S(1)}, u32[]{:S(2)}, u32[]{:S(2)}) collective-permute-start(bf16[496,128]{1,0:T(8,128)(2,1)S(1)} %get-tuple-element.82), channel_id=1, source_target_pairs={{0,4},{2,6},{4,0},{6,2},{8,12},{10,14},{12,8},{14,10},{16,20},{18,... | collective-permute-start | bytes 380936 | tf_op jit(solution)/shard_map/ppermute | solution.py:587
  23.6 0.0 collective-permute-start.7
  23.6 1.7 %shard_map.108 = (bf16[64,96]{1,0:T(8,128)(2,1)}, bf16[512,96]{1,0:T(8,128)(2,1)}) custom-call(bf16[512,128]{1,0:T(8,128)(2,1)S(1)} %get-tuple-element.54.x_ref, bf16[128,128]{1,0:T(8,128)(2,1)S(1)} %get-tuple-element.55.u_ref, bf16[480,128]{1,0:T(8,128)(2,1)S(1)} %get-tuple-element.76.gpa_ref, bf16[320,128]{1,0:T(8,128)(2,1)S(1)} %get-tuple-element.84.gpb_ref, ...), custom_call_target="tpu_custom_call" | custom-call | flops 5000000000 | bytes 4000000 | tf_op jit(solution)/shard_map/pallas_call | solution.py:28
  25.3 0.1 collective-permute-done.5.a_ref
  25.4 2.5 %collective-permute-done.6.b_ref = bf16[496,128]{1,0:T(8,128)(2,1)S(1)} collective-permute-done((bf16[496,128]{1,0:T(8,128)(2,1)S(1)}, bf16[496,128]{1,0:T(8,128)(2,1)S(1)}, u32[]{:S(2)}, u32[]{:S(2)}) %collective-permute-start.6) | collective-permute-done | bytes 127008 | tf_op jit(solution)/shard_map/ppermute | solution.py:587
  27.9 1.6 %collective-permute-done.7.c_ref = bf16[496,128]{1,0:T(8,128)(2,1)S(1)} collective-permute-done((bf16[496,128]{1,0:T(8,128)(2,1)S(1)}, bf16[496,128]{1,0:T(8,128)(2,1)S(1)}, u32[]{:S(2)}, u32[]{:S(2)}) %collective-permute-start.7) | collective-permute-done | bytes 127008 | tf_op jit(solution)/shard_map/ppermute | solution.py:587
  29.5 0.1 shard_map.109
  29.6 1.8 %collective-permute-start.8 = (bf16[496,128]{1,0:T(8,128)(2,1)S(1)}, bf16[496,128]{1,0:T(8,128)(2,1)S(1)}, u32[]{:S(2)}, u32[]{:S(2)}) collective-permute-start(bf16[496,128]{1,0:T(8,128)(2,1)S(1)} %shard_map.109), channel_id=1, source_target_pairs={{0,8},{4,12},{8,0},{12,4},{16,24},{20,28},{24,16},{28,20},{1,9},{5... | collective-permute-start | bytes 380936 | tf_op jit(solution)/shard_map/ppermute | solution.py:595
  31.4 3.2 %collective-permute-done.8 = bf16[496,128]{1,0:T(8,128)(2,1)S(1)} collective-permute-done((bf16[496,128]{1,0:T(8,128)(2,1)S(1)}, bf16[496,128]{1,0:T(8,128)(2,1)S(1)}, u32[]{:S(2)}, u32[]{:S(2)}) %collective-permute-start.8) | collective-permute-done | bytes 127008 | tf_op jit(solution)/shard_map/ppermute | solution.py:595
  34.6 2.8 %collective-permute-start.9 = (bf16[496,128]{1,0:T(8,128)(2,1)S(1)}, bf16[496,128]{1,0:T(8,128)(2,1)S(1)}, u32[]{:S(2)}, u32[]{:S(2)}) collective-permute-start(bf16[496,128]{1,0:T(8,128)(2,1)S(1)} %add_convert_fusion.1), channel_id=1, source_target_pairs={{0,16},{4,20},{8,24},{12,28},{16,0},{20,4},{24,8},{28,12},{1,17},{... | collective-permute-start | bytes 380936 | tf_op jit(solution)/shard_map/ppermute | solution.py:595
  37.5 4.4 %collective-permute-done.9 = bf16[496,128]{1,0:T(8,128)(2,1)S(1)} collective-permute-done((bf16[496,128]{1,0:T(8,128)(2,1)S(1)}, bf16[496,128]{1,0:T(8,128)(2,1)S(1)}, u32[]{:S(2)}, u32[]{:S(2)}) %collective-permute-start.9) | collective-permute-done | bytes 127008 | tf_op jit(solution)/shard_map/ppermute | solution.py:595
  41.9 1.7 %collective-permute-start.10 = (bf16[496,128]{1,0:T(8,128)(2,1)S(1)}, bf16[496,128]{1,0:T(8,128)(2,1)S(1)}, u32[]{:S(2)}, u32[]{:S(2)}) collective-permute-start(bf16[496,128]{1,0:T(8,128)(2,1)S(1)} %add_convert_fusion.refs_0_), channel_id=1, source_target_pairs={{0,2},{2,0},{4,6},{6,4},{8,10},{10,8},{12,14},{14,12},{16,18},{18,... | collective-permute-start | bytes 380936 | tf_op jit(solution)/shard_map/ppermute | solution.py:587
  43.6 1.7 %collective-permute-start.11 = (bf16[496,128]{1,0:T(8,128)(2,1)S(1)}, bf16[496,128]{1,0:T(8,128)(2,1)S(1)}, u32[]{:S(2)}, u32[]{:S(2)}) collective-permute-start(bf16[496,128]{1,0:T(8,128)(2,1)S(1)} %add_convert_fusion.refs_0_), channel_id=1, source_target_pairs={{0,4},{2,6},{4,0},{6,2},{8,12},{10,14},{12,8},{14,10},{16,20},{18,... | collective-permute-start | bytes 380936 | tf_op jit(solution)/shard_map/ppermute | solution.py:587
  45.4 0.1 collective-permute-start.12
  45.5 0.0 collective-permute-start.13
  45.5 2.3 %collective-permute-done.10.refs_1_ = bf16[496,128]{1,0:T(8,128)(2,1)S(1)} collective-permute-done((bf16[496,128]{1,0:T(8,128)(2,1)S(1)}, bf16[496,128]{1,0:T(8,128)(2,1)S(1)}, u32[]{:S(2)}, u32[]{:S(2)}) %collective-permute-start.10) | collective-permute-done | bytes 127008 | tf_op jit(solution)/shard_map/ppermute | solution.py:587
  47.7 0.0 collective-permute-start.14
  47.7 0.8 %collective-permute-done.11.refs_2_ = bf16[496,128]{1,0:T(8,128)(2,1)S(1)} collective-permute-done((bf16[496,128]{1,0:T(8,128)(2,1)S(1)}, bf16[496,128]{1,0:T(8,128)(2,1)S(1)}, u32[]{:S(2)}, u32[]{:S(2)}) %collective-permute-start.11) | collective-permute-done | bytes 127008 | tf_op jit(solution)/shard_map/ppermute | solution.py:587
  48.6 0.0 collective-permute-start.15
  48.6 2.6 %collective-permute-done.12.refs_3_ = bf16[496,128]{1,0:T(8,128)(2,1)S(1)} collective-permute-done((bf16[496,128]{1,0:T(8,128)(2,1)S(1)}, bf16[496,128]{1,0:T(8,128)(2,1)S(1)}, u32[]{:S(2)}, u32[]{:S(2)}) %collective-permute-start.12) | collective-permute-done | bytes 127008 | tf_op jit(solution)/shard_map/ppermute | solution.py:587
  51.2 0.0 collective-permute-start.16
  51.2 0.0 collective-permute-done.13.refs_4_
  51.2 0.0 collective-permute-done.14.refs_5_
  51.2 0.0 collective-permute-done.15.refs_6_
  51.2 1.3 %collective-permute-done.16.refs_7_ = bf16[496,128]{1,0:T(8,128)(2,1)S(1)} collective-permute-done((bf16[496,128]{1,0:T(8,128)(2,1)S(1)}, bf16[496,128]{1,0:T(8,128)(2,1)S(1)}, u32[]{:S(2)}, u32[]{:S(2)}) %collective-permute-start.16) | collective-permute-done | bytes 127008 | tf_op jit(solution)/shard_map/ppermute | solution.py:600
  52.6 1.9 %shard_map.110 = (f32[27,96,96]{2,1,0:T(8,128)}, f32[27,96,96]{2,1,0:T(8,128)}, f32[1,96]{1,0:T(1,128)}) custom-call(bf16[496,128]{1,0:T(8,128)(2,1)S(1)} %add_convert_fusion.refs_0_, bf16[496,128]{1,0:T(8,128)(2,1)S(1)} %collective-permute-done.10.refs_1_, bf16[496,128]{1,0:T(8,128)(2,1)S(1)} %collective-permute-done.11.refs_2_, ...), custom_call_target="tpu_custom_call" | custom-call | tf_op jit(solution)/shard_map/pallas_call | solution.py:28
  (2 shorter events, 0.1 us)
Async XLA Ops:
  1.7 3.0 %collective-permute-start = (bf16[160,128]{1,0:T(8,128)(2,1)S(1)}, bf16[160,128]{1,0:T(8,128)(2,1)S(1)}, u32[]{:S(2)}, u32[]{:S(2)}) collective-permute-start(bf16[160,128]{1,0:T(8,128)(2,1)S(1)} %get-tuple-element.56), channel_id=1, source_target_pairs={{0,1},{1,0},{2,3},{3,2},{4,5},{5,4},{6,7},{7,6},{8,9},{9,8},{10,11... | collective-permute-start | bytes 122888 | tf_op jit(solution)/shard_map/ppermute | solution.py:482
  2.3 2.4 %collective-permute-start.1 = (bf16[160,128]{1,0:T(8,128)(2,1)S(1)}, bf16[160,128]{1,0:T(8,128)(2,1)S(1)}, u32[]{:S(2)}, u32[]{:S(2)}) collective-permute-start(bf16[160,128]{1,0:T(8,128)(2,1)S(1)} %get-tuple-element.57), channel_id=1, source_target_pairs={{1,2},{2,1},{5,6},{6,5},{9,10},{10,9},{13,14},{14,13},{17,18},{18,... | collective-permute-start | bytes 122888 | tf_op jit(solution)/shard_map/ppermute | solution.py:483
  4.8 8.3 %collective-permute-start.2 = (bf16[240,128]{1,0:T(8,128)(2,1)S(1)}, bf16[240,128]{1,0:T(8,128)(2,1)S(1)}, u32[]{:S(2)}, u32[]{:S(2)}) collective-permute-start(bf16[240,128]{1,0:T(8,128)(2,1)S(1)} %get-tuple-element.65), channel_id=1, source_target_pairs={{4,8},{12,16},{20,24},{8,4},{16,12},{24,20},{5,9},{13,17},{21,25},... | collective-permute-start | bytes 184328 | tf_op jit(solution)/shard_map/ppermute | solution.py:507
  5.4 7.7 %collective-permute-start.3 = (bf16[240,128]{1,0:T(8,128)(2,1)S(1)}, bf16[240,128]{1,0:T(8,128)(2,1)S(1)}, u32[]{:S(2)}, u32[]{:S(2)}) collective-permute-start(bf16[240,128]{1,0:T(8,128)(2,1)S(1)} %get-tuple-element.66), channel_id=1, source_target_pairs={{0,4},{4,0},{8,12},{12,8},{16,20},{20,16},{24,28},{28,24},{1,5},{5... | collective-permute-start | bytes 184328 | tf_op jit(solution)/shard_map/ppermute | solution.py:506
  15.1 4.4 %collective-permute-start.4 = (bf16[1984,128]{1,0:T(8,128)(2,1)S(1)}, bf16[1984,128]{1,0:T(8,128)(2,1)S(1)}, u32[]{:S(2)}, u32[]{:S(2)}) collective-permute-start(bf16[1984,128]{1,0:T(8,128)(2,1)S(1)} %get-tuple-element.80), channel_id=1, source_target_pairs={{0,1},{1,0},{2,3},{3,2},{4,5},{5,4},{6,7},{7,6},{8,9},{9,8},{10,11... | collective-permute-start | bytes 1523720 | tf_op jit(solution)/shard_map/ppermute | solution.py:573
  19.6 5.8 %collective-permute-start.5 = (bf16[496,128]{1,0:T(8,128)(2,1)S(1)}, bf16[496,128]{1,0:T(8,128)(2,1)S(1)}, u32[]{:S(2)}, u32[]{:S(2)}) collective-permute-start(bf16[496,128]{1,0:T(8,128)(2,1)S(1)} %get-tuple-element.81), channel_id=1, source_target_pairs={{0,2},{2,0},{4,6},{6,4},{8,10},{10,8},{12,14},{14,12},{16,18},{18,... | collective-permute-start | bytes 380936 | tf_op jit(solution)/shard_map/ppermute | solution.py:587
  21.7 6.3 %collective-permute-start.6 = (bf16[496,128]{1,0:T(8,128)(2,1)S(1)}, bf16[496,128]{1,0:T(8,128)(2,1)S(1)}, u32[]{:S(2)}, u32[]{:S(2)}) collective-permute-start(bf16[496,128]{1,0:T(8,128)(2,1)S(1)} %get-tuple-element.82), channel_id=1, source_target_pairs={{0,4},{2,6},{4,0},{6,2},{8,12},{10,14},{12,8},{14,10},{16,20},{18,... | collective-permute-start | bytes 380936 | tf_op jit(solution)/shard_map/ppermute | solution.py:587
  23.6 5.9 %collective-permute-start.7 = (bf16[496,128]{1,0:T(8,128)(2,1)S(1)}, bf16[496,128]{1,0:T(8,128)(2,1)S(1)}, u32[]{:S(2)}, u32[]{:S(2)}) collective-permute-start(bf16[496,128]{1,0:T(8,128)(2,1)S(1)} %get-tuple-element.83), channel_id=1, source_target_pairs={{0,6},{2,4},{4,2},{6,0},{8,14},{10,12},{12,10},{14,8},{16,22},{18,... | collective-permute-start | bytes 380936 | tf_op jit(solution)/shard_map/ppermute | solution.py:587
  29.6 5.0 %collective-permute-start.8 = (bf16[496,128]{1,0:T(8,128)(2,1)S(1)}, bf16[496,128]{1,0:T(8,128)(2,1)S(1)}, u32[]{:S(2)}, u32[]{:S(2)}) collective-permute-start(bf16[496,128]{1,0:T(8,128)(2,1)S(1)} %shard_map.109), channel_id=1, source_target_pairs={{0,8},{4,12},{8,0},{12,4},{16,24},{20,28},{24,16},{28,20},{1,9},{5... | collective-permute-start | bytes 380936 | tf_op jit(solution)/shard_map/ppermute | solution.py:595
  34.6 7.2 %collective-permute-start.9 = (bf16[496,128]{1,0:T(8,128)(2,1)S(1)}, bf16[496,128]{1,0:T(8,128)(2,1)S(1)}, u32[]{:S(2)}, u32[]{:S(2)}) collective-permute-start(bf16[496,128]{1,0:T(8,128)(2,1)S(1)} %add_convert_fusion.1), channel_id=1, source_target_pairs={{0,16},{4,20},{8,24},{12,28},{16,0},{20,4},{24,8},{28,12},{1,17},{... | collective-permute-start | bytes 380936 | tf_op jit(solution)/shard_map/ppermute | solution.py:595
  41.9 5.8 %collective-permute-start.10 = (bf16[496,128]{1,0:T(8,128)(2,1)S(1)}, bf16[496,128]{1,0:T(8,128)(2,1)S(1)}, u32[]{:S(2)}, u32[]{:S(2)}) collective-permute-start(bf16[496,128]{1,0:T(8,128)(2,1)S(1)} %add_convert_fusion.refs_0_), channel_id=1, source_target_pairs={{0,2},{2,0},{4,6},{6,4},{8,10},{10,8},{12,14},{14,12},{16,18},{18,... | collective-permute-start | bytes 380936 | tf_op jit(solution)/shard_map/ppermute | solution.py:587
  43.6 4.9 %collective-permute-start.11 = (bf16[496,128]{1,0:T(8,128)(2,1)S(1)}, bf16[496,128]{1,0:T(8,128)(2,1)S(1)}, u32[]{:S(2)}, u32[]{:S(2)}) collective-permute-start(bf16[496,128]{1,0:T(8,128)(2,1)S(1)} %add_convert_fusion.refs_0_), channel_id=1, source_target_pairs={{0,4},{2,6},{4,0},{6,2},{8,12},{10,14},{12,8},{14,10},{16,20},{18,... | collective-permute-start | bytes 380936 | tf_op jit(solution)/shard_map/ppermute | solution.py:587
  45.4 5.8 %collective-permute-start.12 = (bf16[496,128]{1,0:T(8,128)(2,1)S(1)}, bf16[496,128]{1,0:T(8,128)(2,1)S(1)}, u32[]{:S(2)}, u32[]{:S(2)}) collective-permute-start(bf16[496,128]{1,0:T(8,128)(2,1)S(1)} %add_convert_fusion.refs_0_), channel_id=1, source_target_pairs={{0,6},{2,4},{4,2},{6,0},{8,14},{10,12},{12,10},{14,8},{16,22},{18,... | collective-permute-start | bytes 380936 | tf_op jit(solution)/shard_map/ppermute | solution.py:587
  45.5 5.7 %collective-permute-start.13 = (bf16[496,128]{1,0:T(8,128)(2,1)S(1)}, bf16[496,128]{1,0:T(8,128)(2,1)S(1)}, u32[]{:S(2)}, u32[]{:S(2)}) collective-permute-start(bf16[496,128]{1,0:T(8,128)(2,1)S(1)} %add_convert_fusion.refs_0_), channel_id=1, source_target_pairs={{0,1},{1,0},{2,3},{3,2},{4,5},{5,4},{6,7},{7,6},{8,9},{9,8},{10,11... | collective-permute-start | bytes 380936 | tf_op jit(solution)/shard_map/ppermute | solution.py:600
  47.7 3.5 %collective-permute-start.14 = (bf16[496,128]{1,0:T(8,128)(2,1)S(1)}, bf16[496,128]{1,0:T(8,128)(2,1)S(1)}, u32[]{:S(2)}, u32[]{:S(2)}) collective-permute-start(bf16[496,128]{1,0:T(8,128)(2,1)S(1)} %collective-permute-done.10.refs_1_), channel_id=1, source_target_pairs={{0,1},{1,0},{2,3},{3,2},{4,5},{5,4},{6,7},{7,6},{8,9},{9,8},{10,11... | collective-permute-start | bytes 380936 | tf_op jit(solution)/shard_map/ppermute | solution.py:600
  48.6 2.7 %collective-permute-start.15 = (bf16[496,128]{1,0:T(8,128)(2,1)S(1)}, bf16[496,128]{1,0:T(8,128)(2,1)S(1)}, u32[]{:S(2)}, u32[]{:S(2)}) collective-permute-start(bf16[496,128]{1,0:T(8,128)(2,1)S(1)} %collective-permute-done.11.refs_2_), channel_id=1, source_target_pairs={{0,1},{1,0},{2,3},{3,2},{4,5},{5,4},{6,7},{7,6},{8,9},{9,8},{10,11... | collective-permute-start | bytes 380936 | tf_op jit(solution)/shard_map/ppermute | solution.py:600
  51.2 1.3 %collective-permute-start.16 = (bf16[496,128]{1,0:T(8,128)(2,1)S(1)}, bf16[496,128]{1,0:T(8,128)(2,1)S(1)}, u32[]{:S(2)}, u32[]{:S(2)}) collective-permute-start(bf16[496,128]{1,0:T(8,128)(2,1)S(1)} %collective-permute-done.12.refs_3_), channel_id=1, source_target_pairs={{0,1},{1,0},{2,3},{3,2},{4,5},{5,4},{6,7},{7,6},{8,9},{9,8},{10,11... | collective-permute-start | bytes 380936 | tf_op jit(solution)/shard_map/ppermute | solution.py:600
